TPU v7x, 32 devices: a whole 2x2x4 slice. The times are simulated.
32 devices in a mesh: seq: 8 (over z, x), tp: 4 (over y, core).
Axes of the slice: x: 2, y: 2, z: 4, core: 2. Of those that a mesh axis runs over, the one named last changes fastest.
Arguments:
- tokens_in: bfloat16 [4, 16, 1024], replicated, may hold values from -6 to 6
- key_cache: bfloat16 [16, 2048, 1024], P(None, 'seq', 'tp'), may hold values from -6 to 6
- value_cache: bfloat16 [16, 2048, 1024], P(None, 'seq', 'tp'), may hold values from -6 to 6
- cache_len: int32 [16], replicated, may hold values from 1 to 2048, as said below
- bucket_table: int32 [2052], replicated, may hold values from 0 to 31, as said below
- rel_bias: float32 [32, 16], P(None, 'tp'), may hold values from -4 to 283
- attn_gain: float32 [1024], replicated, may hold values from 0.1 to 1.9
- moe_gain: float32 [1024], replicated, may hold values from 0.1 to 1.9
- w_qkv: bfloat16 [3, 1024, 1024], P(None, None, 'tp'), may hold values from -0.1875 to 0.1875
- w_out: bfloat16 [1024, 1024], P('tp'), may hold values from -0.1875 to 0.1875
- router: bfloat16 [1024, 16], replicated, may hold values from -0.1875 to 0.1875
- expert_choice: int32 [4, 16, 2], replicated, may hold values from 0 to 15, all different within a row
- w_gate_up: bfloat16 [2, 45056, 1024], P(None, ('seq', 'tp')), may hold values from -0.1875 to 0.1875
- w_down: bfloat16 [45056, 1024], P(('seq', 'tp')), may hold values from -0.109375 to 0.109375
Outputs:
- layer_out: bfloat16 [4, 16, 1024], replicated
Inputs may be any that keep to these rules, and one draw needn't show every extreme that they name: Request r's cache holds its positions 0 to cache_len[r] - 1; some request holds exactly 2048. `bucket_table`: non-decreasing in the distance, 0 at distance 0. `expert_choice`: the 2 experts of a token differ.
All inputs are finite; a program needn't handle non-finite values.
Results may differ from a plain program's by a relative error of at most 0.012.
Values sent between devices are 32-bit elements; how exact they have to be, the bound alone decides.
No kernel may reach another device: no remote copies, remote signals or barrier semaphores. Data moves between devices by JAX's collectives and lax.ppermute only.
A program may use at most 64 MiB of HBM per device.

v0:
```python
import jax
import jax.numpy as jnp
from jax import lax
from jax.sharding import PartitionSpec as P

HEAD_DIM = 64
FF = 2816


NEG = -1e30
EPS = 1e-06


def rms_scale(values, gain_vec):
    return values * lax.rsqrt(jnp.mean(values * values, axis=-1, keepdims=True) + EPS) * gain_vec


def on_device(
    tokens_in,
    key_cache,
    value_cache,
    cache_len,
    bucket_table,
    rel_bias,
    attn_gain,
    moe_gain,
    w_qkv,
    w_out,
    router,
    expert_choice,
    w_gate_up,
    w_down,
):
    steps_all, requests, model_width = tokens_in.shape
    cache_rows = key_cache.shape[1]
    heads_local = key_cache.shape[2] // HEAD_DIM
    table_len = bucket_table.shape[0]
    num_buckets = rel_bias.shape[0]
    num_experts = router.shape[1]
    hidden_local = w_down.shape[0]
    bucket_ids = jnp.arange(num_buckets, dtype=jnp.int32)

    def bias_lookup(buckets, pattern):
        onehot = (buckets[..., None] == bucket_ids).astype(jnp.float32)
        return jnp.einsum(pattern, onehot, rel_bias, precision=lax.Precision.HIGHEST)

    normed = rms_scale(tokens_in.astype(jnp.float32), attn_gain).astype(jnp.bfloat16)
    projected = jnp.einsum(
        "srd,kdf->ksrf", normed, w_qkv, preferred_element_type=jnp.float32
    ).astype(jnp.bfloat16)
    head_shape = (steps_all, requests, heads_local, HEAD_DIM)
    queries = projected[0].reshape(head_shape)
    fresh_keys = projected[1].reshape(head_shape)
    fresh_values = projected[2].reshape(head_shape)
    keys_heads = key_cache.reshape(requests, cache_rows, heads_local, HEAD_DIM)
    values_heads = value_cache.reshape(requests, cache_rows, heads_local, HEAD_DIM)
    positions = lax.axis_index("seq") * cache_rows + jnp.arange(cache_rows, dtype=jnp.int32)
    live_rows = positions[None, :] < cache_len[:, None]

    def cache_part(query_blk, step_ids, keys_blk, vals_blk, lens_blk, live_blk):
        scores = jnp.einsum(
            "srhd,rchd->srhc", query_blk, keys_blk, preferred_element_type=jnp.float32
        )
        distance = lens_blk[None, :, None] + step_ids[:, None, None] - positions[None, None, :]
        buckets = jnp.take(bucket_table, jnp.clip(distance, 0, table_len - 1))
        scores = scores + bias_lookup(buckets, "srcb,bh->srhc")
        usable = live_blk[None, :, None, :]
        scores = jnp.where(usable, scores, NEG)
        maxima = jnp.max(scores, axis=-1)
        weights = jnp.where(usable, jnp.exp(scores - maxima[..., None]), 0.0)
        summed = jnp.einsum(
            "srhc,rchd->srhd", weights, vals_blk, preferred_element_type=jnp.float32
        )
        return (maxima, jnp.sum(weights, axis=-1), summed)

    def attend_cache(query_blk, step_ids):
        return cache_part(query_blk, step_ids, keys_heads, values_heads, cache_len, live_rows)

    def merge_cache(maxima, totals, summed):
        overall = lax.pmax(maxima, "seq")
        factor = jnp.exp(maxima - overall)
        totals, summed = lax.psum((totals * factor, summed * factor[..., None]), "seq")
        return (overall, totals, summed)

    def attend_recent(query_blk, step_ids):
        scores = jnp.einsum(
            "srhd,jrhd->srhj", query_blk, fresh_keys, preferred_element_type=jnp.float32
        )
        distance = step_ids[:, None] - jnp.arange(steps_all, dtype=jnp.int32)[None, :]
        buckets = jnp.take(bucket_table, jnp.clip(distance, 0, table_len - 1))
        scores = scores + bias_lookup(buckets, "sjb,bh->shj")[:, None]
        usable = (distance >= 0)[:, None, None, :]
        scores = jnp.where(usable, scores, NEG)
        maxima = jnp.max(scores, axis=-1)
        weights = jnp.where(usable, jnp.exp(scores - maxima[..., None]), 0.0)
        summed = jnp.einsum(
            "srhj,jrhd->srhd", weights, fresh_values, preferred_element_type=jnp.float32
        )
        return (maxima, jnp.sum(weights, axis=-1), summed)

    first_col = (lax.axis_index("seq") * lax.axis_size("tp") + lax.axis_index("tp")) * hidden_local
    col_expert = (first_col + jnp.arange(hidden_local, dtype=jnp.int32)) // FF
    owner = (col_expert[None, :] == jnp.arange(num_experts, dtype=jnp.int32)[:, None]).astype(
        jnp.float32
    )

    def layer(start, step_count):
        step_ids = jnp.arange(start, start + step_count, dtype=jnp.int32)
        query_blk = queries[start : start + step_count]
        cache_max, cache_tot, cache_sum = merge_cache(*attend_cache(query_blk, step_ids))
        new_max, new_tot, new_sum = attend_recent(query_blk, step_ids)
        joint = jnp.maximum(cache_max, new_max)
        scale_cache = jnp.exp(cache_max - joint)
        scale_new = jnp.exp(new_max - joint)
        totals = cache_tot * scale_cache + new_tot * scale_new
        summed = cache_sum * scale_cache[..., None] + new_sum * scale_new[..., None]
        attended = (
            (summed / totals[..., None])
            .reshape(step_count, requests, heads_local * HEAD_DIM)
            .astype(jnp.bfloat16)
        )
        partial_value = jnp.einsum(
            "srf,fd->srd", attended, w_out, preferred_element_type=jnp.float32
        )
        mid = tokens_in[start : start + step_count].astype(jnp.float32) + lax.psum(
            partial_value, "tp"
        )
        moe_in = rms_scale(mid, moe_gain).astype(jnp.bfloat16)
        logits = jnp.einsum("srd,de->sre", moe_in, router, preferred_element_type=jnp.float32)
        picked = expert_choice[start : start + step_count][..., None] == jnp.arange(
            num_experts, dtype=jnp.int32
        )
        chosen = jnp.sum(jnp.where(picked, logits[:, :, None, :], 0.0), axis=-1)
        leading = jax.nn.sigmoid(chosen[..., 0] - chosen[..., 1])
        gate_pair = jnp.stack([leading, 1.0 - leading], axis=-1)
        per_expert = jnp.sum(jnp.where(picked, gate_pair[..., None], 0.0), axis=2)
        coef = jnp.einsum("sre,ef->srf", per_expert, owner, precision=lax.Precision.HIGHEST)
        gate_up = jnp.einsum("srd,kfd->ksrf", moe_in, w_gate_up, preferred_element_type=jnp.float32)
        hidden = (jax.nn.gelu(gate_up[0], approximate=True) * gate_up[1] * coef).astype(
            jnp.bfloat16
        )
        expert_part = jnp.einsum("srf,fd->srd", hidden, w_down, preferred_element_type=jnp.float32)
        mixture = lax.psum(expert_part, ("seq", "tp"))
        return (mid + mixture).astype(jnp.bfloat16)

    outputs = [layer(start, 1) for start in range(steps_all)]
    return jnp.concatenate(outputs, axis=0)


def solution(mesh):
    return jax.shard_map(
        on_device,
        mesh=mesh,
        in_specs=(
            P(),
            P(None, "seq", "tp"),
            P(None, "seq", "tp"),
            P(),
            P(),
            P(None, "tp"),
            P(),
            P(),
            P(None, None, "tp"),
            P("tp", None),
            P(),
            P(),
            P(None, ("seq", "tp"), None),
            P(("seq", "tp"), None),
        ),
        out_specs=P(),
        check_vma=False,
    )
```

profile of v0, /device:TPU:0, one launch (start us, length us, event | category | flops | bytes accessed | tf_op | source)
XLA Modules:
  0.0 458.9 jit_solution(6743066980730547285)
XLA Ops:
  9.3 23.0 %gather_fusion.4 = s32[4096]{0:T(1024)S(1)} fusion(s32[2052]{0:T(1024)S(1)} %copy-done.1, s32[4096]{0:T(1024)S(1)} %broadcast_clamp_fusion.1), kind=kCustom, calls=%fused_computation.3.clone | custom fusion | bytes 49152 | tf_op jit(solution)/shard_map/jit(_take)/gather | solution.py:65
  32.4 23.0 %gather_fusion.6 = s32[4096]{0:T(1024)S(1)} fusion(s32[2052]{0:T(1024)S(1)} %copy-done.1, s32[4096]{0:T(1024)S(1)} %broadcast_clamp_fusion), kind=kCustom, calls=%fused_computation.4.clone | custom fusion | bytes 49152 | tf_op jit(solution)/shard_map/jit(_take)/gather | solution.py:65
  55.5 23.0 %gather_fusion.2 = s32[4096]{0:T(1024)S(1)} fusion(s32[2052]{0:T(1024)S(1)} %copy-done.1, s32[4096]{0:T(1024)S(1)} %broadcast_clamp_fusion.2), kind=kCustom, calls=%fused_computation.2.clone | custom fusion | bytes 49152 | tf_op jit(solution)/shard_map/jit(_take)/gather | solution.py:65
  79.3 23.0 %gather_fusion = s32[4096]{0:T(1024)S(1)} fusion(s32[2052]{0:T(1024)S(1)} %copy-done.1, s32[4096]{0:T(1024)S(1)} %broadcast_clamp_fusion.3), kind=kCustom, calls=%fused_computation.clone | custom fusion | bytes 49152 | tf_op jit(solution)/shard_map/jit(_take)/gather | solution.py:65
  103.0 1.8 fusion.9
  105.2 3.9 copy.134
  109.2 2.0 fusion.206
  112.2 2.0 fusion.205
  115.2 2.8 fusion.204
  126.0 23.4 %all-reduce.2 = (f32[1,16,4]{1,2,0:T(4,128)S(1)}, f32[1,16,4]{1,2,0:T(4,128)S(1)}, f32[1,16,4]{1,2,0:T(4,128)S(1)}, f32[1,16,4]{1,2,0:T(4,128)S(1)}) all-reduce(f32[1,16,4]{1,2,0:T(4,128)} %bitcast.599, f32[1,16,4]{1,2,0:T(4,128)} %bitcast.601, f32[1,16,4]{1,2,0:T(4,128)} %bitcast.598, ...), channel_id=1, replica_groups=mesh['seq'=8,'tp'=4] {'seq'}, use_global_device_ids=true, to_apply=%region_2.4 | all-reduce | flops 256 | bytes 2048 | tf_op jit(solution)/shard_map/pmax | solution.py:80
  152.4 3.9 copy.135
  156.4 2.4 fusion.63
  176.6 1.5 convolution_bitcast_fusion.15
  199.5 1.5 reshape_squeeze.8
  206.7 1.7 fusion.108
  208.4 1.7 fusion.106
  215.6 1.7 fusion.110
  218.7 1.7 fusion.104
  221.7 10.9 %all-reduce.10.cloned.1.call-done = (f32[1,16,4,64]{3,2,1,0:T(4,128)}, f32[1,16,4]{1,2,0:T(4,128)}, f32[1,16,4,64]{3,2,1,0:T(4,128)}, f32[1,16,4]{1,2,0:T(4,128)...) async-done(((f32[1,16,4,64]{3,2,1,0:T(4,128)}, f32[1,16,4]{1,2,0:T(4,128)}, f32[1,16,4,64]{3,2,1,0:T(4,128)}, ...) | async-done | bytes 66576 | tf_op jit(solution)/shard_map/psum | solution.py:82
  244.6 1.5 fusion.102
  249.6 1.5 fusion.103
  255.2 1.5 fusion.101
  259.4 1.5 fusion.100
  262.4 1.5 convolution_bitcast_fusion.14
  263.9 1.5 convolution_bitcast_fusion.13
  265.4 1.5 convolution_bitcast_fusion.11
  268.7 30.7 %all-reduce.12.cloned.1.call-done = (f32[1,16,1024]{2,1,0:T(8,128)}, f32[1,16,1024]{2,1,0:T(8,128)}, f32[1,16,1024]{2,1,0:T(8,128)}, f32[1,16,1024]{2,1,0:T(8,128)}) async-done(((f32[1,16,1024]{2,1,0:T(8,128)}, f32[1,16,1024]{2,1,0:T(8,128)}, f32[1,16,1024]{2,1,0:T(8,128)}, f32[1,16,1024]{2,1,0:T(8,128)}), (f32[1,16,1024]{2,1,0:T(8,128)}, f32[1,16,1024]{2,1,0:T(8,128)}, f32[1,16,1024]{2,1,0:T(8,128)}, ...) | async-done | bytes 262160 | tf_op jit(solution)/shard_map/psum | solution.py:125
  303.4 4.4 fusion.95
  307.8 4.4 convolution_bitcast_fusion
  312.3 4.2 convolution_bitcast_fusion.1
  316.7 1.6 convolution_bitcast_fusion.2
  324.6 126.1 %all-reduce.8.cloned.1.call-done = (f32[1,16,1024]{2,1,0:T(8,128)}, f32[1,16,1024]{2,1,0:T(8,128)}, f32[1,16,1024]{2,1,0:T(8,128)}, f32[1,16,1024]{2,1,0:T(8,128)}) async-done(((f32[1,16,1024]{2,1,0:T(8,128)}, f32[1,16,1024]{2,1,0:T(8,128)}, f32[1,16,1024]{2,1,0:T(8,128)}, f32[1,16,1024]{2,1,0:T(8,128)}), (f32[1,16,1024]{2,1,0:T(8,128)}, f32[1,16,1024]{2,1,0:T(8,128)}, f32[1,16,1024]{2,1,0:T(8,128)}, ...) | async-done | bytes 262160 | tf_op jit(solution)/shard_map/psum | solution.py:143
  (228 shorter events, 108.4 us)
Async XLA Ops:
  6.5 313.0 %copy-start = (bf16[1408,1024]{1,0:T(8,128)(2,1)S(1)}, bf16[1408,1024]{1,0:T(8,128)(2,1)}, u32[]{:S(2)}) copy-start(bf16[1408,1024]{1,0:T(8,128)(2,1)} %param.31) | copy-start | bytes 8650756
  6.5 2.8 copy-start.1
  6.5 226.1 %all-reduce.10.cloned.1.call-start = ((), (), s32[]{:S(2)}) async-start(), calls=%async_computation.1 | async-start | bytes 278528 | tf_op jit(solution)/shard_map/psum | solution.py:82
  55.5 23.1 %copy-start.20 = (s32[16]{0:T(128)S(1)}, s32[16]{0:T(128)}, u32[]{:S(2)}) copy-start(s32[16]{0:T(128)} %param.21) | copy-start | bytes 196
  79.3 23.8 %copy-start.4 = (bf16[4,16,1024]{2,1,0:T(8,128)(2,1)S(1)}, bf16[4,16,1024]{2,1,0:T(8,128)(2,1)}, u32[]{:S(2)}) copy-start(bf16[4,16,1024]{2,1,0:T(8,128)(2,1)} %param.18) | copy-start | bytes 393220
  79.3 23.8 %copy-start.18 = (f32[1024]{0:T(1024)S(1)}, f32[1024]{0:T(1024)}, u32[]{:S(2)}) copy-start(f32[1024]{0:T(1024)} %param.24) | copy-start | bytes 12292
  109.2 2.0 copy-start.25
  115.2 2.8 copy-start.2
  115.2 3.1 copy-start.19
  149.5 1.4 copy-start.23
  149.5 1.4 copy-start.24
  149.5 2.8 copy-start.21
  149.5 2.8 copy-start.22
  152.4 3.9 copy-start.17
  156.4 2.4 copy-start.5
  156.4 2.4 copy-start.16
  156.4 3.1 copy-start.15
  158.8 1.3 copy-start.14
  160.1 11.9 %copy-start.26 = (f32[32,4]{0,1:T(4,128)S(1)}, f32[32,4]{0,1:T(4,128)}, u32[]{:S(2)}) copy-start(f32[32,4]{0,1:T(4,128)} %param.23) | copy-start | bytes 1540
  163.5 135.9 %all-reduce.12.cloned.1.call-start = ((), (), s32[]{:S(2)}) async-start(), calls=%async_computation.2 | async-start | bytes 524288 | tf_op jit(solution)/shard_map/psum | solution.py:125
  172.0 90.3 %copy-start.3 = (bf16[256,1024]{1,0:T(8,128)(2,1)S(1)}, bf16[256,1024]{1,0:T(8,128)(2,1)}, u32[]{:S(2)}) copy-start(bf16[256,1024]{1,0:T(8,128)(2,1)} %param.27) | copy-start | bytes 1572868
  173.5 10.0 %copy-start.13 = (f32[4,4]{1,0:T(4,128)}, f32[4,4]{1,0:T(4,128)S(1)}, u32[]{:S(2)}) copy-start(f32[4,4]{1,0:T(4,128)S(1)} %copy.153) | copy-start | bytes 196
  181.6 0.6 copy-start.11
  212.3 0.6 copy-start.12
  267.7 183.0 %all-reduce.8.cloned.1.call-start = ((), (), s32[]{:S(2)}) async-start(), calls=%async_computation | async-start | bytes 524288 | tf_op jit(solution)/shard_map/psum | solution.py:143
  303.4 13.3 %slice-start = ((s8[5767168]{0:T(1024)(128)(4,1)}), s8[4194304]{0:T(1024)(128)(4,1)S(1)}, s32[]{:S(2)}) async-start(s8[5767168]{0:T(1024)(128)(4,1)} %bitcast.574), calls=%async_computation.3 | async-start | bytes 8388608
  307.8 4.4 copy-start.10
  307.8 8.9 %slice-start.1 = ((s8[5767168]{0:T(1024)(128)(4,1)}), s8[1572864]{0:T(1024)(128)(4,1)S(1)}, s32[]{:S(2)}) async-start(s8[5767168]{0:T(1024)(128)(4,1)} %bitcast.574), calls=%async_computation.4 | async-start | bytes 3145728
  323.3 127.4 %copy-start.6 = (f32[1,16,1024]{2,1,0:T(8,128)S(1)}, f32[1,16,1024]{2,1,0:T(8,128)}, u32[]{:S(2)}) copy-start(f32[1,16,1024]{2,1,0:T(8,128)} %get-tuple-element.31) | copy-start | bytes 196612
  323.3 127.4 %copy-start.7 = (f32[1,16,1024]{2,1,0:T(8,128)S(1)}, f32[1,16,1024]{2,1,0:T(8,128)}, u32[]{:S(2)}) copy-start(f32[1,16,1024]{2,1,0:T(8,128)} %get-tuple-element.32) | copy-start | bytes 196612
  323.3 127.4 %copy-start.8 = (f32[1,16,1024]{2,1,0:T(8,128)S(1)}, f32[1,16,1024]{2,1,0:T(8,128)}, u32[]{:S(2)}) copy-start(f32[1,16,1024]{2,1,0:T(8,128)} %get-tuple-element.33) | copy-start | bytes 196612
  323.3 127.4 %copy-start.9 = (f32[1,16,1024]{2,1,0:T(8,128)S(1)}, f32[1,16,1024]{2,1,0:T(8,128)}, u32[]{:S(2)}) copy-start(f32[1,16,1024]{2,1,0:T(8,128)} %get-tuple-element.34) | copy-start | bytes 196612
Sparse Core Ops, SparseCore 0:
  163.6 68.9 all-reduce.9
  267.8 31.5 all-reduce.11
  324.7 125.9 all-reduce.7
where the time goes:
time: 462 us; the launch traced here: 459 us
  waiting for transfers between devices  168 us (36%)
  local copies, waits for them, and re-layouts  149 us (32%)
  matrix products  57.1 us (12%)
  other arithmetic  48.1 us (10%)
  blocking collectives  23.4 us (5%)
  between operations  13.6 us (3%)
    psum x1, waiting for transfers between devices, layer(): mixture = lax.psum(expert_part, ('seq', 'tp'))  126 us
    gather x8, local copies, waits for them, and re-layouts, cache_part(): buckets = jnp.take(bucket_table, jnp.clip(distance, 0, table_len - 1))  92.2 us
    psum x1, waiting for transfers between devices, layer(): lax.psum(partial_value, 'tp')  30.7 us
    pmax x1, blocking collectives, merge_cache(): overall = lax.pmax(maxima, 'seq')  23.4 us
    dot_general x4, matrix products, layer(): jnp.einsum('srd,kfd->ksrf', moe_in, w_gate_up, preferred_element_type=jnp...  14.6 us
    psum x1, waiting for transfers between devices, merge_cache(): lax.psum((totals * factor, summed * factor[..., None]), 'seq')  10.9 us
  transfers between devices with their start and end apart: 3, of which 3 were waited for; matrix products, arithmetic and copies ran while one was open for 13% of the time, Pallas kernels for 0%

commit v1 on v0

--- a/solution.py
+++ b/solution.py
@@ -143,8 +143,7 @@
         mixture = lax.psum(expert_part, ("seq", "tp"))
         return (mid + mixture).astype(jnp.bfloat16)
 
-    outputs = [layer(start, 1) for start in range(steps_all)]
-    return jnp.concatenate(outputs, axis=0)
+    return layer(0, steps_all)
 
 
 def solution(mesh):

time: 462 us -> 402 us (0.87)
  blocking collectives: 23.4 us -> 72.5 us
  local copies, waits for them, and re-layouts: 149 us -> 105 us
  other arithmetic: 48.1 us -> 7.9 us
  matrix products: 57.1 us -> 18.5 us
  waiting for transfers between devices: 168 us -> 183 us
    psum x0 -> x1, blocking collectives: none -> 33.7 us  [merge_cache(): lax.psum((totals * factor, summed * factor[..., None]), 'seq')]
    psum x1, waiting for transfers between devices: 10.9 us -> 26.5 us  [merge_cache(): lax.psum((totals * factor, summed * factor[..., None]), 'seq')]
    pmax x1, blocking collectives: 23.4 us -> 38.8 us  [merge_cache(): overall = lax.pmax(maxima, 'seq')]
    dot_general x4 -> x1, matrix products: 14.6 us -> 4.5 us  [layer(): jnp.einsum('srd,kfd->ksrf', moe_in, w_gate_up, preferred_element_type=jnp...]
    dot_general x8 -> x0, local copies, waits for them, and re-layouts: 9.3 us -> none  [the longest x4 5.19 us: attend_recent(): jnp.einsum('srhd,jrhd->srhj', query_blk, fresh_keys, preferred_element_ty...]
    mul x12 -> x0, local copies, waits for them, and re-layouts: 9.1 us -> none  [the longest x8 8.77 us: layer(): summed = cache_sum * scale_cache[..., None] + new_sum * scale_new[..., None]]
    mul x8 -> x0, other arithmetic: 7.89 us -> none  [the longest x4 5.14 us: layer(): summed = cache_sum * scale_cache[..., None] + new_sum * scale_new[..., None]]
    convert_element_type x4 -> x0, other arithmetic: 6.07 us -> none  [layer(): attended = (summed / totals[..., None]).reshape(step_count, requests, hea...]
  transfers between devices with their start and end apart: 3 -> 3, of which waited for: 3 -> 3; matrix products, arithmetic and copies ran while one was open for 13% -> 2% of each run, Pallas kernels for 0% -> 0%
where the time goes in v1:
time: 402 us; the launch traced here: 401 us
  waiting for transfers between devices  183 us (46%)
  local copies, waits for them, and re-layouts  105 us (26%)
  blocking collectives  72.5 us (18%)
  matrix products  18.5 us (5%)
  between operations  13.4 us (3%)
  other arithmetic  7.9 us (2%)
    psum x1, waiting for transfers between devices, layer(): mixture = lax.psum(expert_part, ('seq', 'tp'))  125 us
    gather x2, local copies, waits for them, and re-layouts, cache_part(): buckets = jnp.take(bucket_table, jnp.clip(distance, 0, table_len - 1))  90.6 us
    pmax x1, blocking collectives, merge_cache(): overall = lax.pmax(maxima, 'seq')  38.8 us
    psum x1, blocking collectives, merge_cache(): lax.psum((totals * factor, summed * factor[..., None]), 'seq')  33.7 us
    psum x1, waiting for transfers between devices, layer(): lax.psum(partial_value, 'tp')  31.3 us
    psum x1, waiting for transfers between devices, merge_cache(): lax.psum((totals * factor, summed * factor[..., None]), 'seq')  26.5 us
    unnamed x31, local copies, waits for them, and re-layouts  8.62 us
  transfers between devices with their start and end apart: 3, of which 3 were waited for; matrix products, arithmetic and copies ran while one was open for 2% of the time, Pallas kernels for 0%

profile of v1, /device:TPU:0, one launch (start us, length us, event | category | flops | bytes accessed | tf_op | source)
XLA Modules:
  0.0 400.7 jit_solution(13281460656458387013)
XLA Ops:
  6.5 0.8 iota_add_fusion.1
  7.4 0.8 broadcast_compare_fusion
  8.3 90.5 %gather_fusion = s32[16384]{0:T(1024)S(1)} fusion(s32[2052]{0:T(1024)S(1)} %copy-done.1, s32[16384]{0:T(1024)S(1)} %broadcast_clamp_fusion), kind=kCustom, calls=%fused_computation | custom fusion | bytes 196608 | tf_op jit(solution)/shard_map/jit(_take)/gather | solution.py:65
  99.2 1.8 fusion.23
  101.0 0.6 fusion.78
  101.7 4.0 copy.81
  105.7 0.7 fusion.8
  106.4 2.1 fusion.80
  108.6 38.8 %pmax.7 = f32[4,16,4]{0,2,1:T(4,128)S(1)} all-reduce(f32[4,16,4]{0,2,1:T(4,128)S(1)} %get-tuple-element.17), channel_id=1, replica_groups=mesh['seq'=8,'tp'=4] {'seq'}, use_global_device_ids=true, to_apply=%region_2.3 | all-reduce | flops 256 | bytes 2048 | tf_op jit(solution)/shard_map/pmax | solution.py:80
  147.4 0.3 fusion.40
  147.7 3.9 copy.84
  151.7 3.0 fusion.16
  154.7 33.7 %psum.29 = f32[4,16,4]{0,2,1:T(4,128)} all-reduce(f32[4,16,4]{0,2,1:T(4,128)S(1)} %bitcast.133), channel_id=1, replica_groups=mesh['seq'=8,'tp'=4] {'seq'}, use_global_device_ids=true, to_apply=%region_6.7 | all-reduce | flops 256 | bytes 2048 | tf_op jit(solution)/shard_map/psum | solution.py:82
  188.4 0.7 reshape_squeeze.10
  189.3 0.7 gather_fusion.1
  190.4 1.2 fusion.81
  191.6 0.6 copy-done.7
  192.4 1.4 multiply_add_fusion
  193.9 1.5 reshape_squeeze.11
  195.3 26.5 %all-reduce.4.cloned.1.call-done = f32[4,16,4,64]{3,0,2,1:T(4,128)} async-done(((f32[4,16,4,64]{3,0,2,1:T(4,128)}), f32[4,16,4,64]{3,0,2,1:T(4,128)}) %all-reduce.4.cloned.1.call-update) | async-done | bytes 65552 | tf_op jit(solution)/shard_map/psum | solution.py:82
  221.9 1.4 fusion.22
  223.2 0.7 copy.91
  223.9 1.6 convert_element_type.36
  225.5 1.7 fusion.27
  227.2 31.3 %all-reduce.6.cloned.1.call-done = f32[4,16,1024]{2,1,0:T(8,128)} async-done(((f32[4,16,1024]{2,1,0:T(8,128)}), f32[4,16,1024]{2,1,0:T(8,128)}) %all-reduce.6.cloned.1.call-update) | async-done | bytes 262160 | tf_op jit(solution)/shard_map/psum | solution.py:125
  258.5 1.1 multiply_reduce_fusion
  259.6 1.1 multiply_convert_fusion
  260.7 4.5 %fusion.4 = f32[2,4,16,1408]{3,2,0,1:T(8,128)S(1)} fusion(bf16[2,1408,1024]{2,1,0:T(8,128)(2,1)} %param.26, bf16[4,16,1024]{2,1,0:T(8,128)(2,1)S(1)} %multiply_convert_fusion), kind=kOutput, calls=%fused_computation.6 | convolution fusion | flops 369098752 | bytes 6619136 | tf_op jit(solution)/shard_map/srd,kfd->ksrf/dot_general | solution.py:138
  265.7 0.3 fusion.7
  266.1 1.3 fusion.2
  267.5 125.1 %all-reduce.8.cloned.1.call-done = f32[4,16,1024]{2,1,0:T(8,128)} async-done(((f32[4,16,1024]{2,1,0:T(8,128)}), f32[4,16,1024]{2,1,0:T(8,128)}) %all-reduce.8.cloned.1.call-update) | async-done | bytes 262160 | tf_op jit(solution)/shard_map/psum | solution.py:143
  392.5 1.6 add_convert_fusion
  (62 shorter events, 1.9 us)
Async XLA Ops:
  6.5 259.5 %copy-start = (bf16[1408,1024]{1,0:T(8,128)(2,1)S(1)}, bf16[1408,1024]{1,0:T(8,128)(2,1)}, u32[]{:S(2)}) copy-start(bf16[1408,1024]{1,0:T(8,128)(2,1)} %param.27) | copy-start | bytes 8650756
  6.5 1.8 copy-start.1
  6.5 215.3 %all-reduce.4.cloned.1.call-start = ((), (), s32[]{:S(2)}) async-start(), calls=%async_computation | async-start | bytes 262144 | tf_op jit(solution)/shard_map/psum | solution.py:82
  8.3 90.7 %copy-start.2 = (bf16[4,16,1024]{2,1,0:T(8,128)(2,1)S(1)}, bf16[4,16,1024]{2,1,0:T(8,128)(2,1)}, u32[]{:S(2)}) copy-start(bf16[4,16,1024]{2,1,0:T(8,128)(2,1)} %param.14) | copy-start | bytes 393220
  8.3 90.8 %copy-start.10 = (f32[1024]{0:T(1024)S(1)}, f32[1024]{0:T(1024)}, u32[]{:S(2)}) copy-start(f32[1024]{0:T(1024)} %param.20) | copy-start | bytes 12292
  101.7 4.7 %copy-start.6 = (bf16[4,16,4,64]{3,2,1,0:T(4,128)(2,1)}, bf16[4,16,4,64]{3,2,1,0:T(4,128)(2,1)S(1)}, u32[]{:S(2)}) copy-start(bf16[4,16,4,64]{3,2,1,0:T(4,128)(2,1)S(1)} %reshape_squeeze.9) | copy-start | bytes 98308
  101.7 4.0 copy-start.13
  147.4 4.2 %copy-start.5 = (f32[4,16,4]{0,2,1:T(4,128)}, f32[4,16,4]{0,2,1:T(4,128)S(1)}, u32[]{:S(2)}) copy-start(f32[4,16,4]{0,2,1:T(4,128)S(1)} %pmax.7) | copy-start | bytes 3076
  154.7 103.9 %all-reduce.6.cloned.1.call-start = ((), (), s32[]{:S(2)}) async-start(), calls=%async_computation.1 | async-start | bytes 524288 | tf_op jit(solution)/shard_map/psum | solution.py:125
  190.4 35.0 %copy-start.4 = (bf16[256,1024]{1,0:T(8,128)(2,1)S(1)}, bf16[256,1024]{1,0:T(8,128)(2,1)}, u32[]{:S(2)}) copy-start(bf16[256,1024]{1,0:T(8,128)(2,1)} %param.23) | copy-start | bytes 1572868
  191.6 0.7 copy-start.7
  191.6 0.8 copy-start.8
  221.9 37.8 %copy-start.12 = (f32[1024]{0:T(1024)S(1)}, f32[1024]{0:T(1024)}, u32[]{:S(2)}) copy-start(f32[1024]{0:T(1024)} %param.21) | copy-start | bytes 12292
  227.1 165.4 %all-reduce.8.cloned.1.call-start = ((), (), s32[]{:S(2)}) async-start(), calls=%async_computation.2 | async-start | bytes 524288 | tf_op jit(solution)/shard_map/psum | solution.py:143
  260.7 4.5 %copy-start.9 = (bf16[1024,16]{0,1:T(8,128)(2,1)S(1)}, bf16[1024,16]{0,1:T(8,128)(2,1)}, u32[]{:S(2)}) copy-start(bf16[1024,16]{0,1:T(8,128)(2,1)} %param.24) | copy-start | bytes 98308
  260.7 4.7 %copy-start.11 = (s32[4,16,2]{1,2,0:T(2,128)S(1)}, s32[4,16,2]{1,2,0:T(2,128)}, u32[]{:S(2)}) copy-start(s32[4,16,2]{1,2,0:T(2,128)} %param.25) | copy-start | bytes 1540
  266.1 126.5 %copy-start.3 = (f32[4,16,1024]{2,1,0:T(8,128)S(1)}, f32[4,16,1024]{2,1,0:T(8,128)}, u32[]{:S(2)}) copy-start(f32[4,16,1024]{2,1,0:T(8,128)} %all-reduce.6.cloned.1.call-done) | copy-start | bytes 786436
Sparse Core Ops, SparseCore 0:
  154.8 67.0 all-reduce.3
  227.3 31.2 all-reduce.5
  267.6 124.9 all-reduce.7

commit v2 on v1

v2 whole, which is shorter than its diff:
```python
import jax
import jax.numpy as jnp
from jax import lax
from jax.sharding import PartitionSpec as P

HEAD_DIM = 64
FF = 2816


NEG = -1e30
EPS = 1e-06


def rms_scale(values, gain_vec):
    return values * lax.rsqrt(jnp.mean(values * values, axis=-1, keepdims=True) + EPS) * gain_vec


def swap(value, axis, bit):
    size = lax.axis_size(axis)
    return lax.ppermute(value, axis, [(i, i ^ bit) for i in range(size)])


def bits_of(axis):
    size = lax.axis_size(axis)
    assert size & (size - 1) == 0
    return [1 << k for k in range(size.bit_length() - 1)]


def sum_over(make_half, rows, swaps):
    (axis, bit), others = swaps[0], swaps[1:]
    side = (lax.axis_index(axis) // bit) % 2
    given = swap(make_half(1 - side), axis, bit)
    half = make_half(side) + given
    for other_axis, other_bit in others:
        half = half + swap(half, other_axis, other_bit)
    back = swap(half, axis, bit)
    return jnp.where(side == 0, jnp.concatenate([half, back]), jnp.concatenate([back, half]))


def on_device(
    tokens_in,
    key_cache,
    value_cache,
    cache_len,
    bucket_table,
    rel_bias,
    attn_gain,
    moe_gain,
    w_qkv,
    w_out,
    router,
    expert_choice,
    w_gate_up,
    w_down,
):
    steps, requests, width = tokens_in.shape
    tokens = steps * requests
    cache_rows = key_cache.shape[1]
    features = key_cache.shape[2]
    heads = features // HEAD_DIM
    num_buckets = rel_bias.shape[0]
    num_experts = router.shape[1]
    hidden_local = w_down.shape[0]

    starts = jnp.sum(
        (bucket_table[None, :] < jnp.arange(num_buckets, dtype=jnp.int32)[:, None]).astype(jnp.int32), axis=1
    )

    def bias_of(distance):
        bias = jnp.broadcast_to(rel_bias[0], distance.shape + (heads,))
        for b in range(1, num_buckets):
            bias = jnp.where((distance >= starts[b])[..., None], rel_bias[b], bias)
        return bias

    flat_in = tokens_in.reshape(tokens, width).astype(jnp.float32)
    normed = rms_scale(flat_in, attn_gain).astype(jnp.bfloat16)
    projected = jnp.einsum("td,kdf->ktf", normed, w_qkv, preferred_element_type=jnp.float32).astype(jnp.bfloat16)
    head_shape = (steps, requests, heads, HEAD_DIM)
    queries = projected[0].reshape(head_shape)
    fresh_keys = projected[1].reshape(head_shape)
    fresh_values = projected[2].reshape(head_shape)
    keys_heads = key_cache.reshape(requests, cache_rows, heads, HEAD_DIM)
    values_heads = value_cache.reshape(requests, cache_rows, heads, HEAD_DIM)
    positions = lax.axis_index("seq") * cache_rows + jnp.arange(cache_rows, dtype=jnp.int32)
    step_ids = jnp.arange(steps, dtype=jnp.int32)

    scores = jnp.einsum("srhd,rchd->rshc", queries, keys_heads, preferred_element_type=jnp.float32)
    distance = cache_len[:, None, None] + step_ids[None, :, None] - positions[None, None, :]
    bias = jnp.broadcast_to(rel_bias[0][None, None, :, None], scores.shape)
    for b in range(1, num_buckets):
        bias = jnp.where((distance >= starts[b])[:, :, None, :], rel_bias[b][None, None, :, None], bias)
    usable = (positions[None, :] < cache_len[:, None])[:, None, None, :]
    scores = jnp.where(usable, scores + bias, NEG)
    maxima = jnp.max(scores, axis=-1)
    weights = jnp.where(usable, jnp.exp(scores - maxima[..., None]), 0.0)
    totals = jnp.sum(weights, axis=-1)
    summed = jnp.einsum(
        "rshc,rchd->rshd", weights.astype(jnp.bfloat16), values_heads, preferred_element_type=jnp.float32
    )

    def spread(stat):
        return jnp.broadcast_to(stat[..., None], stat.shape + (HEAD_DIM,))

    stats = jnp.concatenate([maxima.reshape(tokens, heads), totals.reshape(tokens, heads)], axis=1)
    stats = jnp.pad(stats, ((0, 0), (0, 128 - 2 * heads)))
    packed = jnp.concatenate([summed.reshape(tokens, features), stats], axis=1)

    def unpack(packed):
        sums = packed[:, :features].reshape(tokens, heads, HEAD_DIM)
        return packed[:, features : features + heads], packed[:, features + heads : features + 2 * heads], sums

    def merge(one, two):
        (max_one, tot_one, sum_one), (max_two, tot_two, sum_two) = one, two
        top = jnp.maximum(max_one, max_two)
        scale_one, scale_two = jnp.exp(max_one - top), jnp.exp(max_two - top)
        return (
            top,
            tot_one * scale_one + tot_two * scale_two,
            sum_one * spread(scale_one) + sum_two * spread(scale_two),
        )

    for bit in bits_of("seq"):
        top, tot, sums = merge(unpack(packed), unpack(swap(packed, "seq", bit)))
        packed = jnp.concatenate(
            [sums.reshape(tokens, features), jnp.pad(jnp.concatenate([top, tot], 1), ((0, 0), (0, 128 - 2 * heads)))], 1
        )

    new_scores = jnp.einsum("srhd,jrhd->rshj", queries, fresh_keys, preferred_element_type=jnp.float32)
    new_distance = step_ids[:, None] - step_ids[None, :]
    new_scores = new_scores + bias_of(new_distance).transpose(0, 2, 1)[None]
    new_usable = (new_distance >= 0)[None, :, None, :]
    new_scores = jnp.where(new_usable, new_scores, NEG)
    new_max = jnp.max(new_scores, axis=-1)
    new_weights = jnp.where(new_usable, jnp.exp(new_scores - new_max[..., None]), 0.0)
    new_sum = jnp.einsum("rshj,jrhd->rshd", new_weights, fresh_values, preferred_element_type=jnp.float32)
    new_part = (
        new_max.reshape(tokens, heads),
        jnp.sum(new_weights, axis=-1).reshape(tokens, heads),
        new_sum.reshape(tokens, heads, HEAD_DIM),
    )
    _, totals, summed = merge(unpack(packed), new_part)
    attended = (summed / spread(totals)).reshape(requests, steps, features).astype(jnp.bfloat16)
    attended = attended.transpose(1, 0, 2).reshape(tokens, features)

    half_rows = tokens // 2
    tp_swaps = [("tp", bit) for bit in bits_of("tp")]
    all_swaps = tp_swaps + [("seq", bit) for bit in bits_of("seq")]

    def rows_of(value, side):
        return lax.dynamic_slice_in_dim(value, side * half_rows, half_rows, 0)

    mid = flat_in + sum_over(
        lambda side: jnp.dot(rows_of(attended, side), w_out, preferred_element_type=jnp.float32), tokens, tp_swaps
    )
    moe_in = rms_scale(mid, moe_gain).astype(jnp.bfloat16)
    logits = jnp.dot(moe_in, router, preferred_element_type=jnp.float32)
    choice = expert_choice.reshape(tokens, -1)
    picked = choice[..., None] == jnp.arange(num_experts, dtype=jnp.int32)
    chosen = jnp.sum(jnp.where(picked, logits[:, None, :], 0.0), axis=-1)
    leading = jax.nn.sigmoid(chosen[:, 0] - chosen[:, 1])
    gate_pair = jnp.stack([leading, 1.0 - leading], axis=-1)
    device = lax.axis_index("seq") * lax.axis_size("tp") + lax.axis_index("tp")
    col_expert = (device * hidden_local + jnp.arange(hidden_local, dtype=jnp.int32)) // FF
    coef = jnp.where(choice[:, 0:1] == col_expert[None, :], gate_pair[:, 0:1], 0.0)
    coef = jnp.where(choice[:, 1:2] == col_expert[None, :], gate_pair[:, 1:2], coef)
    gate_up = jnp.einsum("td,kfd->ktf", moe_in, w_gate_up, preferred_element_type=jnp.float32)
    hidden = (jax.nn.gelu(gate_up[0], approximate=True) * gate_up[1] * coef).astype(jnp.bfloat16)
    mixture = sum_over(
        lambda side: jnp.dot(rows_of(hidden, side), w_down, preferred_element_type=jnp.float32), tokens, all_swaps
    )
    return (mid + mixture).astype(jnp.bfloat16).reshape(steps, requests, width)


def solution(mesh):
    return jax.shard_map(
        on_device,
        mesh=mesh,
        in_specs=(
            P(),
            P(None, "seq", "tp"),
            P(None, "seq", "tp"),
            P(),
            P(),
            P(None, "tp"),
            P(),
            P(),
            P(None, None, "tp"),
            P("tp", None),
            P(),
            P(),
            P(None, ("seq", "tp"), None),
            P(("seq", "tp"), None),
        ),
        out_specs=P(),
        check_vma=False,
    )
```

time: 402 us -> 175 us (0.44)
  waiting for transfers between devices: 183 us -> 29 us
  blocking collectives: 72.5 us -> 0 us
  local copies, waits for them, and re-layouts: 105 us -> 49.9 us
  other arithmetic: 7.9 us -> 60.4 us
  between operations: 13.4 us -> 0.52 us
  starting transfers between devices: 0.09 us -> 12.1 us
    psum x3 -> x0, waiting for transfers between devices: 183 us -> none  [the longest x1 125 us: layer(): mixture = lax.psum(expert_part, ('seq', 'tp'))]
    gather x4 -> x0, local copies, waits for them, and re-layouts: 91.3 us -> none  [the longest x2 90.6 us: cache_part(): buckets = jnp.take(bucket_table, jnp.clip(distance, 0, table_len - 1))]
    ge x1 -> x19, other arithmetic: 0.01 us -> 44.4 us  [the longest x16 23.9 us: bias_of(): bias = jnp.where((distance >= starts[b])[..., None], rel_bias[b], bias)]
    pmax x1 -> x0, blocking collectives: 38.8 us -> none  [merge_cache(): overall = lax.pmax(maxima, 'seq')]
    psum x1 -> x0, blocking collectives: 33.7 us -> none  [merge_cache(): lax.psum((totals * factor, summed * factor[..., None]), 'seq')]
    ppermute x0 -> x12, waiting for transfers between devices: none -> 29 us  [swap(): return lax.ppermute(value, axis, [(i, i ^ bit) for i in range(size)])]
    broadcast_in_dim x0 -> x18, local copies, waits for them, and re-layouts: none -> 16.3 us  [spread(): return jnp.broadcast_to(stat[..., None], stat.shape + (HEAD_DIM,))]
    ppermute x0 -> x12, starting transfers between devices: none -> 12.1 us  [swap(): return lax.ppermute(value, axis, [(i, i ^ bit) for i in range(size)])]
  transfers between devices with their start and end apart: 3 -> 12, of which waited for: 3 -> 9; matrix products, arithmetic and copies ran while one was open for 2% -> 27% of each run, Pallas kernels for 0% -> 0%
where the time goes in v2:
time: 175 us; the launch traced here: 173 us
  other arithmetic  60.4 us (35%)
  local copies, waits for them, and re-layouts  49.9 us (29%)
  waiting for transfers between devices  29 us (17%)
  matrix products  21.2 us (12%)
  starting transfers between devices  12.1 us (7%)
    ppermute x12, waiting for transfers between devices, swap(): return lax.ppermute(value, axis, [(i, i ^ bit) for i in range(size)])  29 us
    ge x16, other arithmetic, bias_of(): bias = jnp.where((distance >= starts[b])[..., None], rel_bias[b], bias)  23.9 us
    ge x2, other arithmetic, on_device(): distance >= starts[b]  20 us
    broadcast_in_dim x18, local copies, waits for them, and re-layouts, spread(): return jnp.broadcast_to(stat[..., None], stat.shape + (HEAD_DIM,))  16.3 us
    ppermute x12, starting transfers between devices, swap(): return lax.ppermute(value, axis, [(i, i ^ bit) for i in range(size)])  12.1 us
    unnamed x39, local copies, waits for them, and re-layouts  9.66 us
    slice x2, local copies, waits for them, and re-layouts, on_device(): rel_bias[b][None, None, :, None]  4.62 us
    dot_general x1, matrix products, on_device(): jnp.einsum('td,kfd->ktf', moe_in, w_gate_up, preferred_element_type=jnp.f...  4.5 us
  transfers between devices with their start and end apart: 12, of which 9 were waited for; matrix products, arithmetic and copies ran while one was open for 27% of the time, Pallas kernels for 0%

profile of v2, /device:TPU:0, one launch (start us, length us, event | category | flops | bytes accessed | tf_op | source)
XLA Modules:
  0.0 173.1 jit_solution(12474836321743567056)
XLA Ops:
  2.4 2.1 %slice_reduce_fusion.30 = (f32[4]{0:T(128)S(1)}, f32[4]{0:T(128)S(1)}, f32[4]{0:T(128)S(1)}, f32[4]{0:T(128)}, f32[4]{0:T(128)}, /*index=5*/f32[4]{0:T(128)}, f3...) fusion(f32[32,4]{0,1:T(4,128)} %param.19), kind=kLoop, calls=%fused_computation.215 | loop fusion | bytes 416 | tf_op jit(solution)/shard_map/slice | solution.py:91
  4.6 2.5 %slice_reduce_fusion.31 = (f32[4]{0:T(128)}, f32[4]{0:T(128)}, f32[4]{0:T(128)}, f32[4]{0:T(128)}, f32[4]{0:T(128)}, /*index=5*/f32[4]{0:T(128)}, f32[4]{0:T(128...) fusion(f32[32,4]{0,1:T(4,128)} %param.19), kind=kLoop, calls=%fused_computation.216 | loop fusion | bytes 608 | tf_op jit(solution)/shard_map/slice | solution.py:91
  10.6 1.8 %fusion.4 = bf16[3,64,256]{2,1,0:T(8,128)(2,1)S(1)} fusion(bf16[3,1024,256]{2,1,0:T(8,128)(2,1)} %param.22, bf16[64,1024]{1,0:T(8,128)(2,1)S(1)} %fusion.17), kind=kOutput, calls=%fused_computation.12 | convolution fusion | flops 100712448 | bytes 1802240 | tf_op jit(solution)/shard_map/td,kdf->ktf/dot_general | solution.py:77
  12.6 4.0 %copy.139 = bf16[16,256,256]{1,2,0:T(8,128)(2,1)} copy(bf16[16,256,256]{2,1,0:T(8,128)(2,1)} %param.15) | data formatting | bytes 4194304 | tf_op args[1]
  16.5 9.0 %subtract_compare_fusion.29 = (pred[16,4,256]{2,1,0:T(4,128)(4,1)S(1)}, pred[16,4,256]{2,1,0:T(4,128)(4,1)S(1)}, pred[16,4,256]{2,1,0:T(4,128)(4,1)S(1)}, pred[1...) fusion(s32[]{:T(128)} %bitcast.6, ...), kind=kLoop, calls=%fused_computation.42 | loop fusion | flops 245760 | bytes 230712 | tf_op jit(solution)/shard_map/ge | solution.py:91
  25.5 11.0 %subtract_compare_fusion.30 = (pred[16,4,256]{2,1,0:T(4,128)(4,1)S(1)}, pred[16,4,256]{2,1,0:T(4,128)(4,1)S(1)}, pred[16,4,256]{2,1,0:T(4,128)(4,1)S(1)}, pred[1...) fusion(s32[]{:T(128)} %bitcast.5, ...), kind=kLoop, calls=%fused_computation.43 | loop fusion | flops 294912 | bytes 279876 | tf_op jit(solution)/shard_map/ge | solution.py:91
  36.6 3.6 %fusion.103 = (f32[16,4,4]{1,2,0:T(4,128)S(1)}, f32[16,4,4,256]{3,1,2,0:T(4,128)S(1)}) fusion(f32[4]{0:T(128)} %get-tuple-element.35, f32[4]{0:T(128)} %get-tuple-element.36, pred[16,4,256]{2,1,0:T(4,128)(4,1)S(1)} %get-tuple-element.60, f32[4]{0:T(128)} %get-tuple-element.6, pred[16,4,256]{2,1,0:T(4,128)(4,1)S(1)} %get-tuple-element.61, ...), kind=kOutput, calls=%fused_computation.237 | convolution fusion | flops 10616576 | bytes 2905600 | tf_op jit(solution)/shard_map/srhd,rchd->rshc/dot_general | solution.py:87
  40.8 3.9 %copy.141 = bf16[16,256,256]{1,2,0:T(8,128)(2,1)} copy(bf16[16,256,256]{2,1,0:T(8,128)(2,1)} %param.16) | data formatting | bytes 4194304 | tf_op args[2]
  44.7 2.3 %convolution_bitcast_fusion.4 = f32[16,4,4,64]{3,1,2,0:T(4,128)S(1)} fusion(bf16[16,256,4,64]{1,3,2,0:T(8,128)(2,1)} %bitcast.135, f32[16,4,4,256]{3,1,2,0:T(4,128)S(1)} %get-tuple-element.124, f32[16,4,4]{1,2,0:T(4,128)S(1)} %get-tuple-element.123, pred[16,256]{1,0:T(8,128)(4,1)S(1)} %broadcast_compare_fusion), kind=kOutput, calls=%fused_computation.10 | convolution fusion | flops 8585216 | bytes 2429952 | tf_op jit(solution)/shard_map/rshc,rchd->rshd/dot_general | solution.py:97
  47.3 3.0 %collective-permute-start = (f32[64,384]{0,1:T(8,128)S(1)}, f32[64,384]{0,1:T(8,128)}, u32[]{:S(2)}, u32[]{:S(2)}) collective-permute-start(f32[64,384]{0,1:T(8,128)S(1)} %pad_maximum_fusion), channel_id=1, source_target_pairs={{0,4},{4,0},{8,12},{12,8},{16,20},{20,16},{24,28},{28,24},{1,5},{5... | collective-permute-start | bytes 294920 | tf_op jit(solution)/shard_map/ppermute | solution.py:20
  62.0 1.7 fusion.62
  63.7 1.7 %fusion.64 = (pred[4,4]{0,1:T(4,128)(4,1)}, pred[4,4]{0,1:T(4,128)(4,1)}) fusion(s32[]{:T(128)} %bitcast.29, s32[]{:T(128)} %bitcast.28), kind=kLoop, calls=%fused_computation.153 | loop fusion | flops 48 | bytes 40 | tf_op jit(solution)/shard_map/ge | solution.py:72
  65.5 1.8 %fusion.66 = (pred[4,4]{0,1:T(4,128)(4,1)}, pred[4,4]{0,1:T(4,128)(4,1)}) fusion(s32[]{:T(128)} %bitcast.27, s32[]{:T(128)} %bitcast.26), kind=kLoop, calls=%fused_computation.155 | loop fusion | flops 48 | bytes 40 | tf_op jit(solution)/shard_map/ge | solution.py:72
  67.3 1.8 %fusion.68 = (pred[4,4]{0,1:T(4,128)(4,1)}, pred[4,4]{0,1:T(4,128)(4,1)}) fusion(s32[]{:T(128)} %bitcast.25, s32[]{:T(128)} %bitcast.24), kind=kLoop, calls=%fused_computation.157 | loop fusion | flops 48 | bytes 40 | tf_op jit(solution)/shard_map/ge | solution.py:72
  69.2 1.9 %fusion.70 = (pred[4,4]{0,1:T(4,128)(4,1)}, pred[4,4]{0,1:T(4,128)(4,1)}) fusion(s32[]{:T(128)} %bitcast.23, s32[]{:T(128)} %bitcast.22), kind=kLoop, calls=%fused_computation.159 | loop fusion | flops 48 | bytes 40 | tf_op jit(solution)/shard_map/ge | solution.py:72
  71.1 1.9 %fusion.72 = (pred[4,4]{0,1:T(4,128)(4,1)}, pred[4,4]{0,1:T(4,128)(4,1)}) fusion(s32[]{:T(128)} %bitcast.21, s32[]{:T(128)} %bitcast.20), kind=kLoop, calls=%fused_computation.161 | loop fusion | flops 48 | bytes 40 | tf_op jit(solution)/shard_map/ge | solution.py:72
  73.0 1.8 %fusion.74 = (pred[4,4]{0,1:T(4,128)(4,1)}, pred[4,4]{0,1:T(4,128)(4,1)}) fusion(s32[]{:T(128)} %bitcast.19, s32[]{:T(128)} %bitcast.18), kind=kLoop, calls=%fused_computation.163 | loop fusion | flops 48 | bytes 40 | tf_op jit(solution)/shard_map/ge | solution.py:72
  76.1 2.3 %fusion.104 = (f32[16,4,4]{1,2,0:T(4,128)}, f32[16,4,4,4]{1,3,2,0:T(4,128)}) fusion(f32[4,4,4]{0,2,1:T(4,128)S(1)} %select_select_fusion, bf16[4,16,4,64]{3,2,1,0:T(4,128)(2,1)} %copy-done.5, bf16[4,16,4,64]{3,2,1,0:T(4,128)(2,1)S(1)} %reshape_squeeze.10, pred[4,4]{0,1:T(4,128)(4,1)} %fusion.89), kind=kOutput, calls=%fused_computation.238 | convolution fusion | flops 133888 | bytes 70928 | tf_op jit(solution)/shard_map/srhd,jrhd->rshj/dot_general | solution.py:128
  82.2 1.6 collective-permute-start.1
  83.7 1.8 %convolution_bitcast_fusion.2 = f32[16,4,4,64]{3,1,2,0:T(4,128)} fusion(f32[16,4,4,4]{1,3,2,0:T(4,128)} %get-tuple-element.126, bf16[4,16,4,64]{3,2,1,0:T(4,128)(2,1)} %reshape_squeeze.11, f32[16,4,4]{1,2,0:T(4,128)} %get-tuple-element.125, pred[4,4]{0,1:T(4,128)(4,1)} %fusion.89), kind=kOutput, calls=%fused_computation.7 | convolution fusion | flops 133120 | bytes 103440 | tf_op jit(solution)/shard_map/rshj,jrhd->rshd/dot_general | solution.py:135
  93.1 2.6 %collective-permute-start.2 = (f32[64,384]{0,1:T(8,128)}, f32[64,384]{0,1:T(8,128)}, u32[]{:S(2)}, u32[]{:S(2)}) collective-permute-start(f32[64,384]{0,1:T(8,128)} %pad_maximum_fusion.2), channel_id=1, source_target_pairs={{0,16},{4,20},{8,24},{12,28},{16,0},{20,4},{24,8},{28,12},{1,17},{... | collective-permute-start | bytes 294920 | tf_op jit(solution)/shard_map/ppermute | solution.py:20
  118.4 1.6 broadcast_in_dim.988
  120.0 1.6 broadcast_in_dim.989
  123.2 1.6 broadcast_in_dim.1063
  127.6 1.7 collective-permute-done.3
  129.3 1.8 %convolution_add_fusion.1 = f32[32,1024]{1,0:T(8,128)} fusion(f32[32,1024]{1,0:T(8,128)} %collective-permute-done.3, bf16[256,1024]{1,0:T(8,128)(2,1)S(1)} %copy-done.2, bf16[64,256]{1,0:T(8,128)(2,1)} %bitcast.138, s32[]{:T(128)S(6)} %select_n.487), kind=kOutput, calls=%fused_computation.6 | convolution fusion | flops 16809984 | bytes 802820 | tf_op jit(solution)/shard_map/dot_general | solution.py:153
  132.7 4.1 %collective-permute-done.4 = f32[32,1024]{1,0:T(8,128)S(1)} collective-permute-done((f32[32,1024]{1,0:T(8,128)}, f32[32,1024]{1,0:T(8,128)S(1)}, u32[]{:S(2)}, u32[]{:S(2)}) %collective-permute-start.4) | collective-permute-done | bytes 131104 | tf_op jit(solution)/shard_map/ppermute | solution.py:20
  140.5 4.5 %convolution_bitcast_fusion = f32[2,64,1408]{2,1,0:T(8,128)S(1)} fusion(bf16[2,1408,1024]{2,1,0:T(8,128)(2,1)} %param.26, bf16[64,1024]{1,0:T(8,128)(2,1)S(1)} %fusion.20), kind=kOutput, calls=%fused_computation | convolution fusion | flops 369098752 | bytes 6619136 | tf_op jit(solution)/shard_map/td,kfd->ktf/dot_general | solution.py:166
  149.4 4.0 %collective-permute-done.7 = f32[32,1024]{1,0:T(8,128)S(1)} collective-permute-done((f32[32,1024]{1,0:T(8,128)S(1)}, f32[32,1024]{1,0:T(8,128)S(1)}, u32[]{:S(2)}, u32[]{:S(2)}) %collective-permute-start.7) | collective-permute-done | bytes 131104 | tf_op jit(solution)/shard_map/ppermute | solution.py:20
  154.1 4.4 %collective-permute-done.8 = f32[32,1024]{1,0:T(8,128)S(1)} collective-permute-done((f32[32,1024]{1,0:T(8,128)S(1)}, f32[32,1024]{1,0:T(8,128)S(1)}, u32[]{:S(2)}, u32[]{:S(2)}) %collective-permute-start.8) | collective-permute-done | bytes 131104 | tf_op jit(solution)/shard_map/ppermute | solution.py:20
  159.0 4.5 %collective-permute-done.9 = f32[32,1024]{1,0:T(8,128)S(1)} collective-permute-done((f32[32,1024]{1,0:T(8,128)S(1)}, f32[32,1024]{1,0:T(8,128)S(1)}, u32[]{:S(2)}, u32[]{:S(2)}) %collective-permute-start.9) | collective-permute-done | bytes 131104 | tf_op jit(solution)/shard_map/ppermute | solution.py:20
  164.0 6.9 %collective-permute-done.10 = f32[32,1024]{1,0:T(8,128)S(1)} collective-permute-done((f32[32,1024]{1,0:T(8,128)S(1)}, f32[32,1024]{1,0:T(8,128)S(1)}, u32[]{:S(2)}, u32[]{:S(2)}) %collective-permute-start.10) | collective-permute-done | bytes 131104 | tf_op jit(solution)/shard_map/ppermute | solution.py:20
  (159 shorter events, 71.3 us)
Async XLA Ops:
  0.0 145.3 %copy-start = (bf16[1408,1024]{1,0:T(8,128)(2,1)S(1)}, bf16[1408,1024]{1,0:T(8,128)(2,1)}, u32[]{:S(2)}) copy-start(bf16[1408,1024]{1,0:T(8,128)(2,1)} %param.27) | copy-start | bytes 8650756
  4.6 32.0 %copy-start.16 = (f32[4]{0:T(128)}, f32[4]{0:T(128)S(1)}, u32[]{:S(2)}) copy-start(f32[4]{0:T(128)S(1)} %get-tuple-element.25) | copy-start | bytes 52
  4.6 32.0 %copy-start.17 = (f32[4]{0:T(128)}, f32[4]{0:T(128)S(1)}, u32[]{:S(2)}) copy-start(f32[4]{0:T(128)S(1)} %get-tuple-element.26) | copy-start | bytes 52
  12.6 24.0 %copy-start.5 = (bf16[4,16,4,64]{3,2,1,0:T(4,128)(2,1)}, bf16[4,16,4,64]{3,2,1,0:T(4,128)(2,1)S(1)}, u32[]{:S(2)}) copy-start(bf16[4,16,4,64]{3,2,1,0:T(4,128)(2,1)S(1)} %reshape_squeeze.9) | copy-start | bytes 98308
  47.3 31.9 %collective-permute-start = (f32[64,384]{0,1:T(8,128)S(1)}, f32[64,384]{0,1:T(8,128)}, u32[]{:S(2)}, u32[]{:S(2)}) collective-permute-start(f32[64,384]{0,1:T(8,128)S(1)} %pad_maximum_fusion), channel_id=1, source_target_pairs={{0,4},{4,0},{8,12},{12,8},{16,20},{20,16},{24,28},{28,24},{1,5},{5... | collective-permute-start | bytes 294920 | tf_op jit(solution)/shard_map/ppermute | solution.py:20
  79.2 16.5 %copy-start.3 = (f32[16,4,4,4]{1,3,2,0:T(4,128)S(1)}, f32[16,4,4,4]{1,3,2,0:T(4,128)}, u32[]{:S(2)}) copy-start(f32[16,4,4,4]{1,3,2,0:T(4,128)} %get-tuple-element.126) | copy-start | bytes 12292
  79.9 0.6 copy-start.10
  79.9 0.6 copy-start.11
  82.2 8.0 %collective-permute-start.1 = (f32[64,384]{0,1:T(8,128)}, f32[64,384]{0,1:T(8,128)}, u32[]{:S(2)}, u32[]{:S(2)}) collective-permute-start(f32[64,384]{0,1:T(8,128)} %pad_maximum_fusion.1), channel_id=1, source_target_pairs={{0,8},{4,12},{8,0},{12,4},{16,24},{20,28},{24,16},{28,20},{1,9},{5... | collective-permute-start | bytes 294920 | tf_op jit(solution)/shard_map/ppermute | solution.py:20
  90.9 0.6 copy-start.6
  90.9 0.6 copy-start.8
  93.1 13.0 %collective-permute-start.2 = (f32[64,384]{0,1:T(8,128)}, f32[64,384]{0,1:T(8,128)}, u32[]{:S(2)}, u32[]{:S(2)}) collective-permute-start(f32[64,384]{0,1:T(8,128)} %pad_maximum_fusion.2), channel_id=1, source_target_pairs={{0,16},{4,20},{8,24},{12,28},{16,0},{20,4},{24,8},{28,12},{1,17},{... | collective-permute-start | bytes 294920 | tf_op jit(solution)/shard_map/ppermute | solution.py:20
  98.1 11.1 %copy-start.7 = (f32[64,4]{0,1:T(4,128)S(1)}, f32[64,4]{0,1:T(4,128)}, u32[]{:S(2)}) copy-start(f32[64,4]{0,1:T(4,128)} %copy-done.6) | copy-start | bytes 3076
  98.2 11.0 %copy-start.9 = (f32[64,4]{0,1:T(4,128)S(1)}, f32[64,4]{0,1:T(4,128)}, u32[]{:S(2)}) copy-start(f32[64,4]{0,1:T(4,128)} %copy-done.8) | copy-start | bytes 3076
  102.8 24.0 %copy-start.2 = (bf16[256,1024]{1,0:T(8,128)(2,1)S(1)}, bf16[256,1024]{1,0:T(8,128)(2,1)}, u32[]{:S(2)}) copy-start(bf16[256,1024]{1,0:T(8,128)(2,1)} %param.23) | copy-start | bytes 1572868
  113.5 19.1 %copy-start.13 = (s32[4,16,2]{1,2,0:T(2,128)S(1)}, s32[4,16,2]{1,2,0:T(2,128)}, u32[]{:S(2)}) copy-start(s32[4,16,2]{1,2,0:T(2,128)} %param.25) | copy-start | bytes 1540
  118.4 20.8 %copy-start.1 = (bf16[4,16,1024]{2,1,0:T(8,128)(2,1)S(1)}, bf16[4,16,1024]{2,1,0:T(8,128)(2,1)}, u32[]{:S(2)}) copy-start(bf16[4,16,1024]{2,1,0:T(8,128)(2,1)} %param.14) | copy-start | bytes 393220
  121.7 17.8 %copy-start.12 = (f32[1024]{0:T(1024)S(1)}, f32[1024]{0:T(1024)}, u32[]{:S(2)}) copy-start(f32[1024]{0:T(1024)} %param.21) | copy-start | bytes 12292
  126.2 0.6 copy-start.4
  127.6 1.7 collective-permute-start.3
  131.1 5.8 %collective-permute-start.4 = (f32[32,1024]{1,0:T(8,128)}, f32[32,1024]{1,0:T(8,128)S(1)}, u32[]{:S(2)}, u32[]{:S(2)}) collective-permute-start(f32[32,1024]{1,0:T(8,128)} %convolution_add_fusion.1), channel_id=1, source_target_pairs={{0,2},{1,3},{2,0},{3,1},{4,6},{5,7},{6,4},{7,5},{8,10},{9,11},{10,... | collective-permute-start | bytes 393224 | tf_op jit(solution)/shard_map/ppermute | solution.py:20
  137.8 1.4 collective-permute-start.5
  140.5 4.5 %copy-start.14 = (s32[64]{0:T(128)S(1)}, s32[64]{0:T(128)}, u32[]{:S(2)}) copy-start(s32[64]{0:T(128)} %get-tuple-element.90) | copy-start | bytes 772
  140.5 4.5 %copy-start.15 = (s32[64]{0:T(128)S(1)}, s32[64]{0:T(128)}, u32[]{:S(2)}) copy-start(s32[64]{0:T(128)} %get-tuple-element.91) | copy-start | bytes 772
  145.9 1.4 collective-permute-start.6
  147.9 5.6 %collective-permute-start.7 = (f32[32,1024]{1,0:T(8,128)S(1)}, f32[32,1024]{1,0:T(8,128)S(1)}, u32[]{:S(2)}, u32[]{:S(2)}) collective-permute-start(f32[32,1024]{1,0:T(8,128)S(1)} %convolution_add_fusion), channel_id=1, source_target_pairs={{0,2},{1,3},{2,0},{3,1},{4,6},{5,7},{6,4},{7,5},{8,10},{9,11},{10,... | collective-permute-start | bytes 393224 | tf_op jit(solution)/shard_map/ppermute | solution.py:20
  153.5 5.0 %collective-permute-start.8 = (f32[32,1024]{1,0:T(8,128)S(1)}, f32[32,1024]{1,0:T(8,128)S(1)}, u32[]{:S(2)}, u32[]{:S(2)}) collective-permute-start(f32[32,1024]{1,0:T(8,128)S(1)} %add.215), channel_id=1, source_target_pairs={{0,4},{4,0},{8,12},{12,8},{16,20},{20,16},{24,28},{28,24},{1,5},{5... | collective-permute-start | bytes 393224 | tf_op jit(solution)/shard_map/ppermute | solution.py:20
  158.5 5.0 %collective-permute-start.9 = (f32[32,1024]{1,0:T(8,128)S(1)}, f32[32,1024]{1,0:T(8,128)S(1)}, u32[]{:S(2)}, u32[]{:S(2)}) collective-permute-start(f32[32,1024]{1,0:T(8,128)S(1)} %add.216), channel_id=1, source_target_pairs={{0,8},{4,12},{8,0},{12,4},{16,24},{20,28},{24,16},{28,20},{1,9},{5... | collective-permute-start | bytes 393224 | tf_op jit(solution)/shard_map/ppermute | solution.py:20
  163.6 7.3 %collective-permute-start.10 = (f32[32,1024]{1,0:T(8,128)S(1)}, f32[32,1024]{1,0:T(8,128)S(1)}, u32[]{:S(2)}, u32[]{:S(2)}) collective-permute-start(f32[32,1024]{1,0:T(8,128)S(1)} %add.217), channel_id=1, source_target_pairs={{0,16},{4,20},{8,24},{12,28},{16,0},{20,4},{24,8},{28,12},{1,17},{... | collective-permute-start | bytes 393224 | tf_op jit(solution)/shard_map/ppermute | solution.py:20
  170.9 1.4 collective-permute-start.11

commit v3 on v1

v3 whole, which is shorter than its diff:
```python
import functools

import jax
import jax.numpy as jnp
from jax import lax
from jax.experimental import pallas as pl
from jax.experimental.pallas import tpu as pltpu
from jax.sharding import PartitionSpec as P

HEAD_DIM = 64
FF = 2816
LANES = 128
NEG = -1e30
EPS = 1e-06
F32 = jnp.float32
BF16 = jnp.bfloat16
VMEM = pl.BlockSpec(memory_space=pltpu.VMEM)
SMEM = pl.BlockSpec(memory_space=pltpu.SMEM)
ANY = pl.BlockSpec(memory_space=pl.ANY)
NT = (((1,), (1,)), ((), ()))


def dot(one, two):
    return jnp.dot(one, two, preferred_element_type=F32)


def dot_nt(one, two):
    return lax.dot_general(one, two, NT, preferred_element_type=F32)


def iota(shape, dim):
    return lax.broadcasted_iota(jnp.int32, shape, dim)


def rms_scale(values, gain_vec):
    return values * lax.rsqrt(jnp.mean(values * values, axis=-1, keepdims=True) + EPS) * gain_vec


def attend_kernel(
    steps, requests, heads, len_ref, tokens_ref, gain_ref, table_ref, rel_ref, w_hbm, k_hbm, v_hbm,
    out_ref, w_buf, k_buf, v_buf, bias_buf, score_buf, weight_buf, start_buf, step_buf, w_sem, k_sem, v_sem,
):
    tokens = steps * requests
    group = steps * heads
    rows = requests * group
    buckets = rel_ref.shape[1]
    cache_rows, features = k_buf.shape[1:]
    w_copies = [pltpu.make_async_copy(w_hbm.at[k], w_buf.at[k], w_sem.at[k]) for k in range(3)]
    k_copies = [pltpu.make_async_copy(k_hbm.at[r], k_buf.at[r], k_sem.at[r]) for r in range(requests)]
    v_copies = [pltpu.make_async_copy(v_hbm.at[r], v_buf.at[r], v_sem.at[r]) for r in range(requests)]
    for copy in w_copies + k_copies + v_copies:
        copy.start()

    seq = lax.axis_index("seq")
    base = seq * cache_rows

    table = table_ref[...]
    below = jnp.where(table < iota((buckets, table.shape[1]), 0), 1.0, 0.0)
    starts = jnp.sum(below, axis=1, keepdims=True).astype(jnp.int32)
    start_buf[...] = jnp.broadcast_to(starts, (buckets, LANES))

    group_head = iota((group, buckets), 0) // steps
    level = jnp.zeros((group, buckets), F32)
    for h in range(heads):
        level = jnp.where(group_head == h, rel_ref[h : h + 1, :], level)
    for b in range(buckets):
        step_buf[b] = jnp.broadcast_to(level[:, b : b + 1], (group, LANES))

    def bias_of(distance):
        parts = []
        for c in range(0, distance.shape[1], LANES):
            piece = distance[:, c : c + LANES]
            bias = step_buf[0][:, : piece.shape[1]]
            for b in range(1, buckets):
                bias = jnp.where(
                    piece >= start_buf[b : b + 1, : piece.shape[1]], step_buf[b][:, : piece.shape[1]], bias
                )
            parts.append(bias)
        return parts

    group_step = iota((group, cache_rows), 0) % steps
    offset = group_step - iota((group, cache_rows), 1) - base

    def fill_bias(r, carry):
        length = len_ref[r]
        distance = offset + length
        live = distance > group_step
        parts = bias_of(distance)
        for c, bias in enumerate(parts):
            cols = slice(c * LANES, c * LANES + bias.shape[1])
            bias_buf[pl.ds(pl.multiple_of(r * group, group), group), cols] = jnp.where(live[:, cols], bias, NEG)
        return carry

    lax.fori_loop(0, requests, fill_bias, 0)

    x = tokens_ref[...].astype(F32)
    normed = rms_scale(x, gain_ref[...]).astype(BF16)
    projected = []
    for k in range(3):
        w_copies[k].wait()
        projected.append(dot(normed, w_buf[k]).astype(BF16))
    queries, fresh_keys, fresh_values = projected

    row = iota((rows, tokens), 0)
    source = (row % steps) * requests + row // group
    pick = jnp.where(source == iota((rows, tokens), 1), 1.0, 0.0).astype(BF16)
    own_head = (iota((rows, features), 0) // steps) % heads == iota((rows, features), 1) // HEAD_DIM
    spread = jnp.where(own_head, dot(pick, queries), 0.0).astype(BF16)

    column = iota((rows, tokens), 1)
    key_step, key_request = column // requests, column % requests
    ahead = row % steps - key_step
    fresh_live = jnp.logical_and(jnp.logical_and(ahead >= 0, key_request == row // group), seq == 0)
    group_ahead = iota((group, tokens), 0) % steps - iota((group, tokens), 1) // requests
    fresh_bias = bias_of(group_ahead)[0]
    fresh_bias = jnp.concatenate([fresh_bias] * requests, axis=0)
    fresh_scores = jnp.where(fresh_live, dot_nt(spread, fresh_keys) + fresh_bias, NEG)

    for r in range(requests):
        at = slice(r * group, (r + 1) * group)
        k_copies[r].wait()
        score_buf[at, :] = dot_nt(spread[at], k_buf[r])
    scores = score_buf[...] + bias_buf[...]
    top = jnp.maximum(jnp.max(scores, axis=1, keepdims=True), jnp.max(fresh_scores, axis=1, keepdims=True))
    weights = jnp.where(scores > 0.5 * NEG, jnp.exp(scores - top), 0.0)
    fresh_weights = jnp.where(fresh_live, jnp.exp(fresh_scores - top), 0.0)
    total = jnp.sum(weights, axis=1, keepdims=True) + jnp.sum(fresh_weights, axis=1, keepdims=True)
    weight_buf[...] = weights.astype(BF16)
    score_buf[...] = dot(fresh_weights.astype(BF16), fresh_values)
    for r in range(requests):
        at = slice(r * group, (r + 1) * group)
        v_copies[r].wait()
        score_buf[at, :] += dot(weight_buf[at, :], v_buf[r])

    sums = jnp.where(own_head, score_buf[...], 0.0)
    lane = iota((rows, LANES), 1)
    head = (iota((rows, LANES), 0) // steps) % heads
    stats = jnp.where(lane == head, top, jnp.where(lane == heads + head, total, 0.0))
    first = iota((8, 1), 0) < steps
    for values, cols in ((sums, slice(0, features)), (stats, slice(features, features + LANES))):
        for pair in range(requests // 2):
            folded = []
            for r in (2 * pair, 2 * pair + 1):
                part = values[r * group : r * group + 8] + values[r * group + 8 : r * group + 16]
                folded.append(part + pltpu.roll(part, steps, 0))
            out_ref[8 * pair : 8 * pair + 8, cols] = jnp.where(first, folded[0], folded[1])


def widen(stats, first, features):
    heads = features // HEAD_DIM
    lane_head = iota((stats.shape[0], features), 1) // HEAD_DIM
    wide = jnp.broadcast_to(stats[:, first : first + 1], lane_head.shape)
    for h in range(1, heads):
        wide = jnp.where(lane_head == h, stats[:, first + h : first + h + 1], wide)
    return wide


def merged(features, one_ref, two_ref):
    heads = features // HEAD_DIM
    one, two = one_ref[:, features:], two_ref[:, features:]
    top = jnp.maximum(one, two)
    scale_one, scale_two = jnp.exp(one - top), jnp.exp(two - top)
    totals = one * pltpu.roll(scale_one, heads, 1) + two * pltpu.roll(scale_two, heads, 1)
    sums = one_ref[:, :features] * widen(scale_one, 0, features) + two_ref[:, :features] * widen(scale_two, 0, features)
    return sums, jnp.where(iota(top.shape, 1) < heads, top, totals)


def merge_kernel(features, one_ref, two_ref, out_ref):
    sums, stats = merged(features, one_ref, two_ref)
    out_ref[:, :features] = sums
    out_ref[:, features:] = stats


def store_halves(value, bit, keep_ref, give_ref):
    half = value.shape[0] // 2
    low = lax.axis_index("tp") // bit % 2 == 0
    keep_ref[...] = jnp.where(low, value[:half], value[half:])
    give_ref[...] = jnp.where(low, value[half:], value[:half])


def project_kernel(steps, requests, features, one_ref, two_ref, w_ref, keep_ref, give_ref):
    sums, stats = merged(features, one_ref, two_ref)
    attended = (sums / widen(stats, features // HEAD_DIM, features)).astype(BF16)
    tokens = steps * requests
    row = iota((tokens, tokens), 0)
    source = (row % requests) * steps + row // requests
    order = jnp.where(source == iota((tokens, tokens), 1), 1.0, 0.0).astype(BF16)
    attended = dot(order, attended).astype(BF16)
    store_halves(dot(attended, w_ref[...]), 1, keep_ref, give_ref)


def chunks_of(total, size):
    return [(at, min(size, total - at)) for at in range(0, total, size)]


def expert_kernel(
    half_ref, back_ref, tokens_ref, gain_ref, router_ref, choice_ref, up_hbm, down_hbm,
    mid_ref, keep_ref, give_ref, up_buf, down_buf, up_sem, down_sem,
):
    hidden_local = down_buf.shape[0]
    chunks = chunks_of(hidden_local, 256)
    copies = []
    for i, (at, size) in enumerate(chunks):
        at = pl.ds(at, size)
        copies.append(
            [pltpu.make_async_copy(up_hbm.at[k, at], up_buf.at[k, at], up_sem.at[k, i]) for k in range(2)]
            + [pltpu.make_async_copy(down_hbm.at[at], down_buf.at[at], down_sem.at[i])]
        )
        for copy in copies[-1]:
            copy.start()
    half = half_ref.shape[0]
    low = lax.axis_index("tp") % 2 == 0
    mine, other = half_ref[...], back_ref[...]
    mid_ref[:half] = tokens_ref[:half].astype(F32) + jnp.where(low, mine, other)
    mid_ref[half:] = tokens_ref[half:].astype(F32) + jnp.where(low, other, mine)
    moe_in = rms_scale(mid_ref[...], gain_ref[...]).astype(BF16)
    logits = dot_nt(moe_in, router_ref[...])
    expert = iota(logits.shape, 1)
    first_choice, second_choice = choice_ref[:, 0:1], choice_ref[:, 1:2]
    chosen = [
        jnp.sum(jnp.where(expert == pick, logits, 0.0), axis=1, keepdims=True) for pick in (first_choice, second_choice)
    ]
    first = 1.0 / (1.0 + jnp.exp(chosen[1] - chosen[0]))
    second = 1.0 - first
    device = lax.axis_index("seq") * lax.axis_size("tp") + lax.axis_index("tp")
    total = jnp.zeros(mid_ref.shape, F32)
    for (at, size), (gate_copy, up_copy, down_copy) in zip(chunks, copies):
        column_expert = (device * hidden_local + at + iota((mid_ref.shape[0], size), 1)) // FF
        coef = jnp.where(
            column_expert == first_choice, first, jnp.where(column_expert == second_choice, second, 0.0)
        )
        gate_copy.wait()
        gate = dot_nt(moe_in, up_buf[0, at : at + size, :])
        up_copy.wait()
        up = dot_nt(moe_in, up_buf[1, at : at + size, :])
        hidden = (jax.nn.gelu(gate, approximate=True) * up * coef).astype(BF16)
        down_copy.wait()
        total = total + dot(hidden, down_buf[at : at + size, :])
    store_halves(total, 1, keep_ref, give_ref)


def swap(value, axis, bit):
    return lax.ppermute(value, axis, [(i, i ^ bit) for i in range(lax.axis_size(axis))])


def bits_of(axis):
    size = lax.axis_size(axis)
    assert size & (size - 1) == 0
    return [1 << k for k in range(size.bit_length() - 1)]


def reduce_halves(keep, give, swaps):
    half = keep + swap(give, *swaps[0])
    for axis, bit in swaps[1:]:
        half = half + swap(half, axis, bit)
    return half, swap(half, *swaps[0])


def call(kernel, out_shape, in_specs, scratch=()):
    shapes = [jax.ShapeDtypeStruct(shape, dtype) for shape, dtype in out_shape]
    return pl.pallas_call(
        kernel,
        out_shape=shapes,
        in_specs=in_specs,
        out_specs=[VMEM] * len(shapes),
        scratch_shapes=list(scratch),
        compiler_params=pltpu.CompilerParams(vmem_limit_bytes=40 << 20),
    )


def on_device(
    tokens_in,
    key_cache,
    value_cache,
    cache_len,
    bucket_table,
    rel_bias,
    attn_gain,
    moe_gain,
    w_qkv,
    w_out,
    router,
    expert_choice,
    w_gate_up,
    w_down,
):
    steps, requests, width = tokens_in.shape
    tokens = steps * requests
    half = tokens // 2
    _, cache_rows, features = key_cache.shape
    heads = features // HEAD_DIM
    rows = tokens * heads
    buckets = rel_bias.shape[0]
    hidden_local = w_down.shape[0]
    packed_shape = (tokens, features + LANES)
    flat_in = tokens_in.reshape(tokens, width)
    dma = pltpu.SemaphoreType.DMA

    (packed,) = call(
        functools.partial(attend_kernel, steps, requests, heads),
        [(packed_shape, F32)],
        [SMEM, VMEM, VMEM, VMEM, VMEM, ANY, ANY, ANY],
        [
            pltpu.VMEM(w_qkv.shape, BF16),
            pltpu.VMEM(key_cache.shape, BF16),
            pltpu.VMEM(value_cache.shape, BF16),
            pltpu.VMEM((rows, cache_rows), F32),
            pltpu.VMEM((rows, cache_rows), F32),
            pltpu.VMEM((rows, cache_rows), BF16),
            pltpu.VMEM((buckets, LANES), jnp.int32),
            pltpu.VMEM((buckets, steps * heads, LANES), F32),
            dma((3,)),
            dma((requests,)),
            dma((requests,)),
        ],
    )(
        cache_len, flat_in, attn_gain[None], bucket_table[None], rel_bias.T, w_qkv, key_cache, value_cache
    )

    seq_bits = bits_of("seq")
    for bit in seq_bits[:-1]:
        (packed,) = call(functools.partial(merge_kernel, features), [(packed_shape, F32)], [VMEM, VMEM])(
            packed, swap(packed, "seq", bit)
        )
    half_shape = ((half, width), F32)
    keep, give = call(
        functools.partial(project_kernel, steps, requests, features), [half_shape, half_shape], [VMEM, VMEM, VMEM]
    )(packed, swap(packed, "seq", seq_bits[-1]), w_out)

    tp_swaps = [("tp", bit) for bit in bits_of("tp")]
    mine, other = reduce_halves(keep, give, tp_swaps)

    n_chunks = len(chunks_of(hidden_local, 256))
    mid, keep, give = call(
        expert_kernel,
        [((tokens, width), F32), half_shape, half_shape],
        [VMEM] * 6 + [ANY, ANY],
        [
            pltpu.VMEM(w_gate_up.shape, BF16),
            pltpu.VMEM(w_down.shape, BF16),
            dma((2, n_chunks)),
            dma((n_chunks,)),
        ],
    )(mine, other, flat_in, moe_gain[None], router.T, expert_choice.reshape(tokens, -1), w_gate_up, w_down)

    mine, other = reduce_halves(keep, give, tp_swaps + [("seq", bit) for bit in seq_bits])
    low = lax.axis_index("tp") % 2 == 0
    mixture = jnp.concatenate([jnp.where(low, mine, other), jnp.where(low, other, mine)])
    return (mid + mixture).astype(BF16).reshape(steps, requests, width)


def solution(mesh):
    return jax.shard_map(
        on_device,
        mesh=mesh,
        in_specs=(
            P(),
            P(None, "seq", "tp"),
            P(None, "seq", "tp"),
            P(),
            P(),
            P(None, "tp"),
            P(),
            P(),
            P(None, None, "tp"),
            P("tp", None),
            P(),
            P(),
            P(None, ("seq", "tp"), None),
            P(("seq", "tp"), None),
        ),
        out_specs=P(),
        check_vma=False,
    )
```

time: 402 us -> 85.5 us (0.21)
  waiting for transfers between devices: 183 us -> 29.4 us
  local copies, waits for them, and re-layouts: 105 us -> 13.1 us
  blocking collectives: 72.5 us -> 0 us
  Pallas kernels: 0 us -> 21.7 us
  starting transfers between devices: 0.09 us -> 19.2 us
  matrix products: 18.5 us -> 0 us
  between operations: 13.4 us -> 0.17 us
  other arithmetic: 7.9 us -> 0.82 us
    psum x3 -> x0, waiting for transfers between devices: 183 us -> none  [the longest x1 125 us: layer(): mixture = lax.psum(expert_part, ('seq', 'tp'))]
    gather x4 -> x0, local copies, waits for them, and re-layouts: 91.3 us -> none  [the longest x2 90.6 us: cache_part(): buckets = jnp.take(bucket_table, jnp.clip(distance, 0, table_len - 1))]
    pmax x1 -> x0, blocking collectives: 38.8 us -> none  [merge_cache(): overall = lax.pmax(maxima, 'seq')]
    psum x1 -> x0, blocking collectives: 33.7 us -> none  [merge_cache(): lax.psum((totals * factor, summed * factor[..., None]), 'seq')]
    ppermute x0 -> x12, waiting for transfers between devices: none -> 29.4 us  [swap(): lax.ppermute(value, axis, [(i, i ^ bit) for i in range(lax.axis_size(axis...]
    pallas_call x0 -> x5, Pallas kernels: none -> 21.7 us  [the longest x1 14.1 us: on_device(): call(functools.partial(attend_kernel, steps, requests, heads), [(packed_s...]
    ppermute x0 -> x12, starting transfers between devices: none -> 19.2 us  [swap(): lax.ppermute(value, axis, [(i, i ^ bit) for i in range(lax.axis_size(axis...]
    dot_general x12 -> x0, matrix products: 18.5 us -> none  [the longest x1 4.5 us: layer(): jnp.einsum('srd,kfd->ksrf', moe_in, w_gate_up, preferred_element_type=jnp...]
  transfers between devices with their start and end apart: 3 -> 12, of which waited for: 3 -> 12; matrix products, arithmetic and copies ran while one was open for 2% -> 1% of each run, Pallas kernels for 0% -> 0%
where the time goes in v3:
time: 85.5 us; the launch traced here: 84.5 us
  waiting for transfers between devices  29.4 us (34%)
  Pallas kernels  21.7 us (25%)
  starting transfers between devices  19.2 us (22%)
  local copies, waits for them, and re-layouts  13.1 us (15%)
    ppermute x12, waiting for transfers between devices, swap(): lax.ppermute(value, axis, [(i, i ^ bit) for i in range(lax.axis_size(axis...  29.4 us
    ppermute x12, starting transfers between devices, swap(): lax.ppermute(value, axis, [(i, i ^ bit) for i in range(lax.axis_size(axis...  19.2 us
    pallas_call x1, Pallas kernels, on_device(): call(functools.partial(attend_kernel, steps, requests, heads), [(packed_s...  14.1 us
    unnamed x30, local copies, waits for them, and re-layouts  11.7 us
    pallas_call x1, Pallas kernels, on_device(): call(expert_kernel, [((tokens, width), F32), half_shape, half_shape], [VM...  6.73 us
  transfers between devices with their start and end apart: 12, of which 12 were waited for; matrix products, arithmetic and copies ran while one was open for 1% of the time, Pallas kernels for 0%

profile of v3, /device:TPU:0, one launch (start us, length us, event | category | flops | bytes accessed | tf_op | source)
XLA Modules:
  0.0 84.5 jit_solution(8960846707662299075)
XLA Ops:
  0.0 0.7 broadcast_in_dim.10.table_ref
  0.7 1.6 %copy-done.2 = bf16[16,256,256]{2,1,0:T(8,128)(2,1)S(1)} copy-done((bf16[16,256,256]{2,1,0:T(8,128)(2,1)S(1)}, bf16[16,256,256]{2,1,0:T(8,128)(2,1)}, u32[]{:S(2)}) %copy-start.2) | copy-done | bytes 2097176
  2.3 1.6 %copy-done.3 = bf16[16,256,256]{2,1,0:T(8,128)(2,1)S(1)} copy-done((bf16[16,256,256]{2,1,0:T(8,128)(2,1)S(1)}, bf16[16,256,256]{2,1,0:T(8,128)(2,1)}, u32[]{:S(2)}) %copy-start.3) | copy-done | bytes 2097176
  3.9 1.4 %copy-done.4 = bf16[3,1024,256]{2,1,0:T(8,128)(2,1)S(1)} copy-done((bf16[3,1024,256]{2,1,0:T(8,128)(2,1)S(1)}, bf16[3,1024,256]{2,1,0:T(8,128)(2,1)}, u32[]{:S(2)}) %copy-start.4) | copy-done | bytes 1572888
  5.3 0.9 %copy-done.5 = bf16[4,16,1024]{2,1,0:T(8,128)(2,1)S(1)} copy-done((bf16[4,16,1024]{2,1,0:T(8,128)(2,1)S(1)}, bf16[4,16,1024]{2,1,0:T(8,128)(2,1)}, u32[]{:S(2)}) %copy-start.5) | copy-done | bytes 131096
  6.2 0.7 copy-done.11
  8.2 14.1 %shard_map.136.one_ref = f32[64,384]{1,0:T(8,128)S(1)} custom-call(s32[16]{0:T(128)S(1)} %copy-done.13, bf16[64,1024]{1,0:T(8,128)(2,1)S(1)} %bitcast.7, f32[1,1024]{1,0:T(1,128)S(1)} %bitcast.12, s32[1,2052]{1,0:T(1,128)S(1)} %broadcast_in_dim.10.table_ref, f32[4,32]{1,0:T(4,128)S(1)} %bitcast.13, bf16[3,1024,256]{2,1,0:T(8,128)(2,1)S(1)} %copy-done.4, ...), custom_call_target="tpu_custom_call" | custom-call | tf_op jit(solution)/shard_map/pallas_call | solution.py:299
  22.4 3.0 %collective-permute-start = (f32[64,384]{1,0:T(8,128)S(1)}, f32[64,384]{1,0:T(8,128)S(1)}, u32[]{:S(2)}, u32[]{:S(2)}) collective-permute-start(f32[64,384]{1,0:T(8,128)S(1)} %shard_map.136.one_ref), channel_id=1, source_target_pairs={{0,4},{4,0},{8,12},{12,8},{16,20},{20,16},{24,28},{28,24},{1,5},{5... | collective-permute-start | bytes 294920 | tf_op jit(solution)/shard_map/ppermute | solution.py:243
  25.4 2.8 %collective-permute-done.two_ref = f32[64,384]{1,0:T(8,128)S(1)} collective-permute-done((f32[64,384]{1,0:T(8,128)S(1)}, f32[64,384]{1,0:T(8,128)S(1)}, u32[]{:S(2)}, u32[]{:S(2)}) %collective-permute-start) | collective-permute-done | bytes 98336 | tf_op jit(solution)/shard_map/ppermute | solution.py:243
  28.4 2.0 %collective-permute-start.1 = (f32[64,384]{1,0:T(8,128)S(1)}, f32[64,384]{1,0:T(8,128)S(1)}, u32[]{:S(2)}, u32[]{:S(2)}) collective-permute-start(f32[64,384]{1,0:T(8,128)S(1)} %shard_map.137.one_ref), channel_id=1, source_target_pairs={{0,8},{4,12},{8,0},{12,4},{16,24},{20,28},{24,16},{28,20},{1,9},{5... | collective-permute-start | bytes 294920 | tf_op jit(solution)/shard_map/ppermute | solution.py:243
  30.3 2.7 %collective-permute-done.1.two_ref = f32[64,384]{1,0:T(8,128)S(1)} collective-permute-done((f32[64,384]{1,0:T(8,128)S(1)}, f32[64,384]{1,0:T(8,128)S(1)}, u32[]{:S(2)}, u32[]{:S(2)}) %collective-permute-start.1) | collective-permute-done | bytes 98336 | tf_op jit(solution)/shard_map/ppermute | solution.py:243
  33.2 3.0 %collective-permute-start.2 = (f32[64,384]{1,0:T(8,128)S(1)}, f32[64,384]{1,0:T(8,128)S(1)}, u32[]{:S(2)}, u32[]{:S(2)}) collective-permute-start(f32[64,384]{1,0:T(8,128)S(1)} %shard_map.138.one_ref), channel_id=1, source_target_pairs={{0,16},{4,20},{8,24},{12,28},{16,0},{20,4},{24,8},{28,12},{1,17},{... | collective-permute-start | bytes 294920 | tf_op jit(solution)/shard_map/ppermute | solution.py:243
  36.2 2.6 %collective-permute-done.2.two_ref = f32[64,384]{1,0:T(8,128)S(1)} collective-permute-done((f32[64,384]{1,0:T(8,128)S(1)}, f32[64,384]{1,0:T(8,128)S(1)}, u32[]{:S(2)}, u32[]{:S(2)}) %collective-permute-start.2) | collective-permute-done | bytes 98336 | tf_op jit(solution)/shard_map/ppermute | solution.py:243
  39.4 1.3 %collective-permute-done.3 = f32[32,1024]{1,0:T(8,128)S(1)} collective-permute-done((f32[32,1024]{1,0:T(8,128)S(1)}, f32[32,1024]{1,0:T(8,128)S(1)}, u32[]{:S(2)}, u32[]{:S(2)}) %collective-permute-start.3) | collective-permute-done | bytes 131104 | tf_op jit(solution)/shard_map/ppermute | solution.py:243
  40.8 1.9 %collective-permute-start.4 = (f32[32,1024]{1,0:T(8,128)S(1)}, f32[32,1024]{1,0:T(8,128)S(1)}, u32[]{:S(2)}, u32[]{:S(2)}) collective-permute-start(f32[32,1024]{1,0:T(8,128)S(1)} %add.28), channel_id=1, source_target_pairs={{0,2},{1,3},{2,0},{3,1},{4,6},{5,7},{6,4},{7,5},{8,10},{9,11},{10,... | collective-permute-start | bytes 393224 | tf_op jit(solution)/shard_map/ppermute | solution.py:243
  42.7 3.8 %collective-permute-done.4 = f32[32,1024]{1,0:T(8,128)S(1)} collective-permute-done((f32[32,1024]{1,0:T(8,128)S(1)}, f32[32,1024]{1,0:T(8,128)S(1)}, u32[]{:S(2)}, u32[]{:S(2)}) %collective-permute-start.4) | collective-permute-done | bytes 131104 | tf_op jit(solution)/shard_map/ppermute | solution.py:243
  46.6 0.7 copy.17
  48.0 2.6 %copy-done = bf16[2,1408,1024]{2,1,0:T(8,128)(2,1)S(1)} copy-done((bf16[2,1408,1024]{2,1,0:T(8,128)(2,1)S(1)}, bf16[2,1408,1024]{2,1,0:T(8,128)(2,1)}, u32[]{:S(2)}) %copy-start) | copy-done | bytes 5767192
  50.6 0.8 copy-done.8
  51.4 0.8 copy-done.9
  52.1 6.7 %shard_map.140 = (f32[64,1024]{1,0:T(8,128)S(1)}, f32[32,1024]{1,0:T(8,128)S(1)}, f32[32,1024]{1,0:T(8,128)S(1)}) custom-call(f32[32,1024]{1,0:T(8,128)S(1)} %add.29.half_ref, f32[32,1024]{1,0:T(8,128)S(1)} %collective-permute-done.5.back_ref, bf16[64,1024]{1,0:T(8,128)(2,1)S(1)} %bitcast.8, f32[1,1024]{1,0:T(1,128)S(1)} %bitcast.11, ...), custom_call_target="tpu_custom_call" | custom-call | tf_op jit(solution)/shard_map/pallas_call | solution.py:334
  59.1 1.2 %collective-permute-done.6 = f32[32,1024]{1,0:T(8,128)S(1)} collective-permute-done((f32[32,1024]{1,0:T(8,128)S(1)}, f32[32,1024]{1,0:T(8,128)S(1)}, u32[]{:S(2)}, u32[]{:S(2)}) %collective-permute-start.6) | collective-permute-done | bytes 131104 | tf_op jit(solution)/shard_map/ppermute | solution.py:243
  60.3 1.8 %collective-permute-start.7 = (f32[32,1024]{1,0:T(8,128)S(1)}, f32[32,1024]{1,0:T(8,128)S(1)}, u32[]{:S(2)}, u32[]{:S(2)}) collective-permute-start(f32[32,1024]{1,0:T(8,128)S(1)} %add.31), channel_id=1, source_target_pairs={{0,2},{1,3},{2,0},{3,1},{4,6},{5,7},{6,4},{7,5},{8,10},{9,11},{10,... | collective-permute-start | bytes 393224 | tf_op jit(solution)/shard_map/ppermute | solution.py:243
  62.1 3.8 %collective-permute-done.7 = f32[32,1024]{1,0:T(8,128)S(1)} collective-permute-done((f32[32,1024]{1,0:T(8,128)S(1)}, f32[32,1024]{1,0:T(8,128)S(1)}, u32[]{:S(2)}, u32[]{:S(2)}) %collective-permute-start.7) | collective-permute-done | bytes 131104 | tf_op jit(solution)/shard_map/ppermute | solution.py:243
  65.9 1.8 %collective-permute-start.8 = (f32[32,1024]{1,0:T(8,128)S(1)}, f32[32,1024]{1,0:T(8,128)S(1)}, u32[]{:S(2)}, u32[]{:S(2)}) collective-permute-start(f32[32,1024]{1,0:T(8,128)S(1)} %add.32), channel_id=1, source_target_pairs={{0,4},{4,0},{8,12},{12,8},{16,20},{20,16},{24,28},{28,24},{1,5},{5... | collective-permute-start | bytes 393224 | tf_op jit(solution)/shard_map/ppermute | solution.py:243
  67.7 3.3 %collective-permute-done.8 = f32[32,1024]{1,0:T(8,128)S(1)} collective-permute-done((f32[32,1024]{1,0:T(8,128)S(1)}, f32[32,1024]{1,0:T(8,128)S(1)}, u32[]{:S(2)}, u32[]{:S(2)}) %collective-permute-start.8) | collective-permute-done | bytes 131104 | tf_op jit(solution)/shard_map/ppermute | solution.py:243
  71.0 2.0 %collective-permute-start.9 = (f32[32,1024]{1,0:T(8,128)S(1)}, f32[32,1024]{1,0:T(8,128)S(1)}, u32[]{:S(2)}, u32[]{:S(2)}) collective-permute-start(f32[32,1024]{1,0:T(8,128)S(1)} %add.33), channel_id=1, source_target_pairs={{0,8},{4,12},{8,0},{12,4},{16,24},{20,28},{24,16},{28,20},{1,9},{5... | collective-permute-start | bytes 393224 | tf_op jit(solution)/shard_map/ppermute | solution.py:243
  73.0 3.0 %collective-permute-done.9 = f32[32,1024]{1,0:T(8,128)S(1)} collective-permute-done((f32[32,1024]{1,0:T(8,128)S(1)}, f32[32,1024]{1,0:T(8,128)S(1)}, u32[]{:S(2)}, u32[]{:S(2)}) %collective-permute-start.9) | collective-permute-done | bytes 131104 | tf_op jit(solution)/shard_map/ppermute | solution.py:243
  76.1 3.4 %collective-permute-start.10 = (f32[32,1024]{1,0:T(8,128)S(1)}, f32[32,1024]{1,0:T(8,128)S(1)}, u32[]{:S(2)}, u32[]{:S(2)}) collective-permute-start(f32[32,1024]{1,0:T(8,128)S(1)} %add.34), channel_id=1, source_target_pairs={{0,16},{4,20},{8,24},{12,28},{16,0},{20,4},{24,8},{28,12},{1,17},{... | collective-permute-start | bytes 393224 | tf_op jit(solution)/shard_map/ppermute | solution.py:243
  79.4 2.9 %collective-permute-done.10 = f32[32,1024]{1,0:T(8,128)S(1)} collective-permute-done((f32[32,1024]{1,0:T(8,128)S(1)}, f32[32,1024]{1,0:T(8,128)S(1)}, u32[]{:S(2)}, u32[]{:S(2)}) %collective-permute-start.10) | collective-permute-done | bytes 131104 | tf_op jit(solution)/shard_map/ppermute | solution.py:243
  82.5 1.3 %collective-permute-done.11 = f32[32,1024]{1,0:T(8,128)S(1)} collective-permute-done((f32[32,1024]{1,0:T(8,128)S(1)}, f32[32,1024]{1,0:T(8,128)S(1)}, u32[]{:S(2)}, u32[]{:S(2)}) %collective-permute-start.11) | collective-permute-done | bytes 131104 | tf_op jit(solution)/shard_map/ppermute | solution.py:243
  83.8 0.7 fusion
  (38 shorter events, 3.4 us)
Async XLA Ops:
  0.7 1.6 %copy-start.2 = (bf16[16,256,256]{2,1,0:T(8,128)(2,1)S(1)}, bf16[16,256,256]{2,1,0:T(8,128)(2,1)}, u32[]{:S(2)}) copy-start(bf16[16,256,256]{2,1,0:T(8,128)(2,1)} %k_hbm.1) | copy-start | bytes 6291460
  2.3 1.6 %copy-start.3 = (bf16[16,256,256]{2,1,0:T(8,128)(2,1)S(1)}, bf16[16,256,256]{2,1,0:T(8,128)(2,1)}, u32[]{:S(2)}) copy-start(bf16[16,256,256]{2,1,0:T(8,128)(2,1)} %v_hbm.1) | copy-start | bytes 6291460
  3.9 1.4 %copy-start.4 = (bf16[3,1024,256]{2,1,0:T(8,128)(2,1)S(1)}, bf16[3,1024,256]{2,1,0:T(8,128)(2,1)}, u32[]{:S(2)}) copy-start(bf16[3,1024,256]{2,1,0:T(8,128)(2,1)} %w_hbm.1) | copy-start | bytes 4718596
  5.3 0.9 %copy-start.5 = (bf16[4,16,1024]{2,1,0:T(8,128)(2,1)S(1)}, bf16[4,16,1024]{2,1,0:T(8,128)(2,1)}, u32[]{:S(2)}) copy-start(bf16[4,16,1024]{2,1,0:T(8,128)(2,1)} %param.14) | copy-start | bytes 393220
  6.2 0.7 copy-start.11
  6.9 0.7 copy-start.12
  7.6 0.7 copy-start.13
  8.2 30.6 %copy-start.7 = (bf16[256,1024]{1,0:T(8,128)(2,1)S(1)}, bf16[256,1024]{1,0:T(8,128)(2,1)}, u32[]{:S(2)}) copy-start(bf16[256,1024]{1,0:T(8,128)(2,1)} %w_ref.1) | copy-start | bytes 1572868
  8.2 39.7 %copy-start.1 = (bf16[1408,1024]{1,0:T(8,128)(2,1)S(1)}, bf16[1408,1024]{1,0:T(8,128)(2,1)}, u32[]{:S(2)}) copy-start(bf16[1408,1024]{1,0:T(8,128)(2,1)} %down_hbm.1) | copy-start | bytes 8650756
  22.3 24.3 %copy-start.14 = (s32[4,16,2]{1,2,0:T(2,128)S(1)}, s32[4,16,2]{1,2,0:T(2,128)}, u32[]{:S(2)}) copy-start(s32[4,16,2]{1,2,0:T(2,128)} %param.25) | copy-start | bytes 1540
  22.4 25.6 %copy-start.6 = (bf16[4,16,1024]{2,1,0:T(8,128)(2,1)S(1)}, bf16[4,16,1024]{2,1,0:T(8,128)(2,1)}, u32[]{:S(2)}) copy-start(bf16[4,16,1024]{2,1,0:T(8,128)(2,1)} %param.14) | copy-start | bytes 393220
  22.4 25.6 %copy-start.10 = (f32[1024]{0:T(1024)S(1)}, f32[1024]{0:T(1024)}, u32[]{:S(2)}) copy-start(f32[1024]{0:T(1024)} %param.21) | copy-start | bytes 12292
  22.4 5.8 %collective-permute-start = (f32[64,384]{1,0:T(8,128)S(1)}, f32[64,384]{1,0:T(8,128)S(1)}, u32[]{:S(2)}, u32[]{:S(2)}) collective-permute-start(f32[64,384]{1,0:T(8,128)S(1)} %shard_map.136.one_ref), channel_id=1, source_target_pairs={{0,4},{4,0},{8,12},{12,8},{16,20},{20,16},{24,28},{28,24},{1,5},{5... | collective-permute-start | bytes 294920 | tf_op jit(solution)/shard_map/ppermute | solution.py:243
  28.4 4.7 %collective-permute-start.1 = (f32[64,384]{1,0:T(8,128)S(1)}, f32[64,384]{1,0:T(8,128)S(1)}, u32[]{:S(2)}, u32[]{:S(2)}) collective-permute-start(f32[64,384]{1,0:T(8,128)S(1)} %shard_map.137.one_ref), channel_id=1, source_target_pairs={{0,8},{4,12},{8,0},{12,4},{16,24},{20,28},{24,16},{28,20},{1,9},{5... | collective-permute-start | bytes 294920 | tf_op jit(solution)/shard_map/ppermute | solution.py:243
  33.2 5.6 %collective-permute-start.2 = (f32[64,384]{1,0:T(8,128)S(1)}, f32[64,384]{1,0:T(8,128)S(1)}, u32[]{:S(2)}, u32[]{:S(2)}) collective-permute-start(f32[64,384]{1,0:T(8,128)S(1)} %shard_map.138.one_ref), channel_id=1, source_target_pairs={{0,16},{4,20},{8,24},{12,28},{16,0},{20,4},{24,8},{28,12},{1,17},{... | collective-permute-start | bytes 294920 | tf_op jit(solution)/shard_map/ppermute | solution.py:243
  39.4 1.4 %collective-permute-start.3 = (f32[32,1024]{1,0:T(8,128)S(1)}, f32[32,1024]{1,0:T(8,128)S(1)}, u32[]{:S(2)}, u32[]{:S(2)}) collective-permute-start(f32[32,1024]{1,0:T(8,128)S(1)} %get-tuple-element.11), channel_id=1, source_target_pairs={{0,1},{1,0},{2,3},{3,2},{4,5},{5,4},{6,7},{7,6},{8,9},{9,8},{10,11... | collective-permute-start | bytes 393224 | tf_op jit(solution)/shard_map/ppermute | solution.py:243
  40.8 5.7 %collective-permute-start.4 = (f32[32,1024]{1,0:T(8,128)S(1)}, f32[32,1024]{1,0:T(8,128)S(1)}, u32[]{:S(2)}, u32[]{:S(2)}) collective-permute-start(f32[32,1024]{1,0:T(8,128)S(1)} %add.28), channel_id=1, source_target_pairs={{0,2},{1,3},{2,0},{3,1},{4,6},{5,7},{6,4},{7,5},{8,10},{9,11},{10,... | collective-permute-start | bytes 393224 | tf_op jit(solution)/shard_map/ppermute | solution.py:243
  46.6 1.4 %collective-permute-start.5 = (f32[32,1024]{1,0:T(8,128)S(1)}, f32[32,1024]{1,0:T(8,128)S(1)}, u32[]{:S(2)}, u32[]{:S(2)}) collective-permute-start(f32[32,1024]{1,0:T(8,128)S(1)} %add.29.half_ref), channel_id=1, source_target_pairs={{0,1},{1,0},{2,3},{3,2},{4,5},{5,4},{6,7},{7,6},{8,9},{9,8},{10,11... | collective-permute-start | bytes 393224 | tf_op jit(solution)/shard_map/ppermute | solution.py:243
  48.0 2.6 %copy-start = (bf16[2,1408,1024]{2,1,0:T(8,128)(2,1)S(1)}, bf16[2,1408,1024]{2,1,0:T(8,128)(2,1)}, u32[]{:S(2)}) copy-start(bf16[2,1408,1024]{2,1,0:T(8,128)(2,1)} %up_hbm.1) | copy-start | bytes 17301508
  50.6 0.8 copy-start.8
  51.4 0.8 copy-start.9
  58.9 1.4 %collective-permute-start.6 = (f32[32,1024]{1,0:T(8,128)S(1)}, f32[32,1024]{1,0:T(8,128)S(1)}, u32[]{:S(2)}, u32[]{:S(2)}) collective-permute-start(f32[32,1024]{1,0:T(8,128)S(1)} %get-tuple-element.14), channel_id=1, source_target_pairs={{0,1},{1,0},{2,3},{3,2},{4,5},{5,4},{6,7},{7,6},{8,9},{9,8},{10,11... | collective-permute-start | bytes 393224 | tf_op jit(solution)/shard_map/ppermute | solution.py:243
  60.3 5.6 %collective-permute-start.7 = (f32[32,1024]{1,0:T(8,128)S(1)}, f32[32,1024]{1,0:T(8,128)S(1)}, u32[]{:S(2)}, u32[]{:S(2)}) collective-permute-start(f32[32,1024]{1,0:T(8,128)S(1)} %add.31), channel_id=1, source_target_pairs={{0,2},{1,3},{2,0},{3,1},{4,6},{5,7},{6,4},{7,5},{8,10},{9,11},{10,... | collective-permute-start | bytes 393224 | tf_op jit(solution)/shard_map/ppermute | solution.py:243
  65.9 5.0 %collective-permute-start.8 = (f32[32,1024]{1,0:T(8,128)S(1)}, f32[32,1024]{1,0:T(8,128)S(1)}, u32[]{:S(2)}, u32[]{:S(2)}) collective-permute-start(f32[32,1024]{1,0:T(8,128)S(1)} %add.32), channel_id=1, source_target_pairs={{0,4},{4,0},{8,12},{12,8},{16,20},{20,16},{24,28},{28,24},{1,5},{5... | collective-permute-start | bytes 393224 | tf_op jit(solution)/shard_map/ppermute | solution.py:243
  71.0 5.0 %collective-permute-start.9 = (f32[32,1024]{1,0:T(8,128)S(1)}, f32[32,1024]{1,0:T(8,128)S(1)}, u32[]{:S(2)}, u32[]{:S(2)}) collective-permute-start(f32[32,1024]{1,0:T(8,128)S(1)} %add.33), channel_id=1, source_target_pairs={{0,8},{4,12},{8,0},{12,4},{16,24},{20,28},{24,16},{28,20},{1,9},{5... | collective-permute-start | bytes 393224 | tf_op jit(solution)/shard_map/ppermute | solution.py:243
  76.1 6.3 %collective-permute-start.10 = (f32[32,1024]{1,0:T(8,128)S(1)}, f32[32,1024]{1,0:T(8,128)S(1)}, u32[]{:S(2)}, u32[]{:S(2)}) collective-permute-start(f32[32,1024]{1,0:T(8,128)S(1)} %add.34), channel_id=1, source_target_pairs={{0,16},{4,20},{8,24},{12,28},{16,0},{20,4},{24,8},{28,12},{1,17},{... | collective-permute-start | bytes 393224 | tf_op jit(solution)/shard_map/ppermute | solution.py:243
  82.4 1.4 %collective-permute-start.11 = (f32[32,1024]{1,0:T(8,128)S(1)}, f32[32,1024]{1,0:T(8,128)S(1)}, u32[]{:S(2)}, u32[]{:S(2)}) collective-permute-start(f32[32,1024]{1,0:T(8,128)S(1)} %add.35), channel_id=1, source_target_pairs={{0,1},{1,0},{2,3},{3,2},{4,5},{5,4},{6,7},{7,6},{8,9},{9,8},{10,11... | collective-permute-start | bytes 393224 | tf_op jit(solution)/shard_map/ppermute | solution.py:243

commit v4 on v3

v4 whole, which is shorter than its diff:
```python
import functools

import jax
import jax.numpy as jnp
from jax import lax
from jax.experimental import pallas as pl
from jax.experimental.pallas import tpu as pltpu
from jax.sharding import PartitionSpec as P

HEAD_DIM = 64
FF = 2816
LANES = 128
NEG = -1e30
EPS = 1e-06
F32 = jnp.float32
BF16 = jnp.bfloat16
VMEM = pl.BlockSpec(memory_space=pltpu.VMEM)
HBM = pl.BlockSpec(memory_space=pltpu.HBM)
NT = (((1,), (1,)), ((), ()))


def dot(one, two):
    return jnp.dot(one, two, preferred_element_type=F32)


def dot_nt(one, two):
    return lax.dot_general(one, two, NT, preferred_element_type=F32)


def iota(shape, dim):
    return lax.broadcasted_iota(jnp.int32, shape, dim)


def rms_scale(values, gain_vec):
    return values * lax.rsqrt(jnp.mean(values * values, axis=-1, keepdims=True) + EPS) * gain_vec


def shift_of(size):
    assert size & (size - 1) == 0
    return size.bit_length() - 1


def over(value, size):
    return lax.shift_right_logical(value, jnp.int32(shift_of(size)))


def modulo(value, size):
    assert size & (size - 1) == 0
    return value & (size - 1)


def attend_kernel(
    steps, requests, heads, len_hbm, tokens_hbm, gain_hbm, table_hbm, rel_hbm, w_hbm, k_hbm, v_hbm,
    out_ref, len_ref, tokens_ref, gain_ref, table_ref, rel_ref, w_buf, k_buf, v_buf,
    bias_buf, score_buf, weight_buf, start_buf, step_buf, small_sem, w_sem, k_sem, v_sem,
):
    tokens = steps * requests
    group = steps * heads
    rows = requests * group
    buckets = rel_ref.shape[1]
    cache_rows, features = k_buf.shape[1:]
    small = (
        (len_hbm, len_ref),
        (table_hbm, table_ref.at[0]),
        (rel_hbm, rel_ref),
        (tokens_hbm, tokens_ref),
        (gain_hbm, gain_ref.at[0]),
    )
    small_copies = [pltpu.make_async_copy(src, dst, small_sem.at[i]) for i, (src, dst) in enumerate(small)]
    w_copies = [pltpu.make_async_copy(w_hbm.at[k], w_buf.at[k], w_sem.at[k]) for k in range(3)]
    k_copies = [pltpu.make_async_copy(k_hbm.at[r], k_buf.at[r], k_sem.at[r]) for r in range(requests)]
    v_copies = [pltpu.make_async_copy(v_hbm.at[r], v_buf.at[r], v_sem.at[r]) for r in range(requests)]
    for copy in small_copies + w_copies + k_copies + v_copies:
        copy.start()

    seq = lax.axis_index("seq")
    base = seq * cache_rows

    for copy in small_copies[:3]:
        copy.wait()
    table = table_ref[...]
    below = jnp.where(table < iota((buckets, table.shape[1]), 0), 1.0, 0.0)
    starts = jnp.sum(below, axis=1, keepdims=True).astype(jnp.int32)
    start_buf[...] = jnp.broadcast_to(starts, (buckets, LANES))

    group_head = over(iota((group, 1), 0), steps)
    level = jnp.zeros((group, buckets), F32)
    for h in range(heads):
        level = jnp.where(group_head == h, rel_ref[h : h + 1, :], level)
    for b in range(buckets):
        step_buf[b] = jnp.broadcast_to(level[:, b : b + 1], (group, LANES))

    def bias_of(pieces):
        width = pieces[0].shape[1]
        biases = [step_buf[0][:, :width]] * len(pieces)
        for b in range(1, buckets):
            start, value = start_buf[b : b + 1, :width], step_buf[b][:, :width]
            biases = [jnp.where(piece >= start, value, bias) for piece, bias in zip(pieces, biases)]
        return biases

    group_step = modulo(iota((group, 1), 0), steps)
    col_slices = [slice(c, c + LANES) for c in range(0, cache_rows, LANES)]
    offsets = [group_step - iota((1, LANES), 1) - (base + c.start) for c in col_slices]
    per_trip = 2

    def fill_bias(trip, carry):
        places, distances = [], []
        for i in range(per_trip):
            r = trip * per_trip + i
            length = len_ref[r]
            for cols, offset in zip(col_slices, offsets):
                places.append((pl.ds(pl.multiple_of(r * group, group), group), cols))
                distances.append(offset + length)
        for place, distance, bias in zip(places, distances, bias_of(distances)):
            bias_buf[place] = jnp.where(distance > group_step, bias, NEG)
        return carry

    lax.fori_loop(0, requests // per_trip, fill_bias, 0)

    for copy in small_copies[3:]:
        copy.wait()
    x = tokens_ref[...].astype(F32)
    normed = rms_scale(x, gain_ref[...]).astype(BF16)
    projected = []
    for k in range(3):
        w_copies[k].wait()
        projected.append(dot(normed, w_buf[k]).astype(BF16))
    queries, fresh_keys, fresh_values = projected

    row = iota((rows, 1), 0)
    row_step, row_head, row_request = modulo(row, steps), modulo(over(row, steps), heads), over(row, group)
    column = iota((1, tokens), 1)
    pick = jnp.where(row_step * requests + row_request == column, 1.0, 0.0).astype(BF16)
    own_head = row_head == over(iota((1, features), 1), HEAD_DIM)
    spread = jnp.where(own_head, dot(pick, queries), 0.0).astype(BF16)

    key_step, key_request = over(column, requests), modulo(column, requests)
    newest = jnp.where(seq == 0, row_step, -1)
    fresh_live = jnp.logical_and(key_step <= newest, key_request == row_request)
    (fresh_bias,) = bias_of([group_step - key_step])
    fresh_bias = jnp.concatenate([fresh_bias] * requests, axis=0)
    fresh_scores = jnp.where(fresh_live, dot_nt(spread, fresh_keys) + fresh_bias, NEG)

    for r in range(requests):
        at = slice(r * group, (r + 1) * group)
        k_copies[r].wait()
        score_buf[at, :] = dot_nt(spread[at], k_buf[r])
    scores = score_buf[...] + bias_buf[...]
    top = jnp.maximum(jnp.max(scores, axis=1, keepdims=True), jnp.max(fresh_scores, axis=1, keepdims=True))
    weights = jnp.where(scores > 0.5 * NEG, jnp.exp(scores - top), 0.0)
    fresh_weights = jnp.where(fresh_live, jnp.exp(fresh_scores - top), 0.0)
    total = jnp.sum(weights, axis=1, keepdims=True) + jnp.sum(fresh_weights, axis=1, keepdims=True)
    weight_buf[...] = weights.astype(BF16)
    score_buf[...] = dot(fresh_weights.astype(BF16), fresh_values)
    for r in range(requests):
        at = slice(r * group, (r + 1) * group)
        v_copies[r].wait()
        score_buf[at, :] += dot(weight_buf[at, :], v_buf[r])

    sums = jnp.where(own_head, score_buf[...], 0.0)
    lane = iota((1, LANES), 1)
    stats = jnp.where(lane == row_head, top, jnp.where(lane == heads + row_head, total, 0.0))
    first = iota((8, 1), 0) < steps
    for values, cols in ((sums, slice(0, features)), (stats, slice(features, features + LANES))):
        for pair in range(requests // 2):
            folded = []
            for r in (2 * pair, 2 * pair + 1):
                part = values[r * group : r * group + 8] + values[r * group + 8 : r * group + 16]
                folded.append(part + pltpu.roll(part, steps, 0))
            out_ref[8 * pair : 8 * pair + 8, cols] = jnp.where(first, folded[0], folded[1])


def widen(stats, first, features):
    heads = features // HEAD_DIM
    lane_head = over(iota((1, features), 1), HEAD_DIM)
    wide = jnp.broadcast_to(stats[:, first : first + 1], (stats.shape[0], features))
    for h in range(1, heads):
        wide = jnp.where(lane_head == h, stats[:, first + h : first + h + 1], wide)
    return wide


def merged(features, one_ref, two_ref):
    heads = features // HEAD_DIM
    one, two = one_ref[:, features:], two_ref[:, features:]
    top = jnp.maximum(one, two)
    scale_one, scale_two = jnp.exp(one - top), jnp.exp(two - top)
    totals = one * pltpu.roll(scale_one, heads, 1) + two * pltpu.roll(scale_two, heads, 1)
    sums = one_ref[:, :features] * widen(scale_one, 0, features) + two_ref[:, :features] * widen(scale_two, 0, features)
    return sums, jnp.where(iota(top.shape, 1) < heads, top, totals)


def merge_kernel(features, one_ref, two_ref, out_ref):
    sums, stats = merged(features, one_ref, two_ref)
    out_ref[:, :features] = sums
    out_ref[:, features:] = stats


def store_halves(value, bit, keep_ref, give_ref):
    half = value.shape[0] // 2
    low = lax.axis_index("tp") // bit % 2 == 0
    keep_ref[...] = jnp.where(low, value[:half], value[half:])
    give_ref[...] = jnp.where(low, value[half:], value[:half])


def project_kernel(steps, requests, features, one_ref, two_ref, w_ref, keep_ref, give_ref):
    sums, stats = merged(features, one_ref, two_ref)
    attended = (sums / widen(stats, features // HEAD_DIM, features)).astype(BF16)
    tokens = steps * requests
    row = iota((tokens, 1), 0)
    source = modulo(row, requests) * steps + over(row, requests)
    order = jnp.where(source == iota((1, tokens), 1), 1.0, 0.0).astype(BF16)
    attended = dot(order, attended).astype(BF16)
    store_halves(dot(attended, w_ref[...]), 1, keep_ref, give_ref)


def chunks_of(total, size):
    return [(at, min(size, total - at)) for at in range(0, total, size)]


def expert_kernel(
    half_ref, back_ref, tokens_ref, gain_ref, router_ref, choice_ref, up_ref, down_ref, mid_ref, keep_ref, give_ref
):
    hidden_local = down_ref.shape[0]
    half = half_ref.shape[0]
    steps, _, requests = choice_ref.shape
    low = lax.axis_index("tp") % 2 == 0
    mine, other = half_ref[...], back_ref[...]
    mid_ref[:half] = tokens_ref[:half].astype(F32) + jnp.where(low, mine, other)
    mid_ref[half:] = tokens_ref[half:].astype(F32) + jnp.where(low, other, mine)
    moe_in = rms_scale(mid_ref[...], gain_ref[...]).astype(BF16)
    logits = dot_nt(moe_in, router_ref[...])
    expert = iota((1, logits.shape[1]), 1)
    own = iota((requests, 1), 0) == iota((1, requests), 1)
    choices, chosen = [], []
    for pick in range(2):
        column = [
            jnp.sum(jnp.where(own, choice_ref[t, pick : pick + 1, :].astype(F32), 0.0), axis=1, keepdims=True)
            for t in range(steps)
        ]
        choices.append(jnp.concatenate(column, axis=0).astype(jnp.int32))
        chosen.append(jnp.sum(jnp.where(expert == choices[pick], logits, 0.0), axis=1, keepdims=True))
    first = 1.0 / (1.0 + jnp.exp(chosen[1] - chosen[0]))
    second = 1.0 - first
    device = lax.axis_index("seq") * lax.axis_size("tp") + lax.axis_index("tp")
    total = jnp.zeros(mid_ref.shape, F32)
    for at, size in chunks_of(hidden_local, 256):
        column_expert = (device * hidden_local + at + iota((1, size), 1)) // FF
        coef = jnp.where(column_expert == choices[0], first, jnp.where(column_expert == choices[1], second, 0.0))
        gate = dot_nt(moe_in, up_ref[0, at : at + size, :])
        up = dot_nt(moe_in, up_ref[1, at : at + size, :])
        hidden = (jax.nn.gelu(gate, approximate=True) * up * coef).astype(BF16)
        total = total + dot(hidden, down_ref[at : at + size, :])
    store_halves(total, 1, keep_ref, give_ref)


def swap(value, axis, bit):
    return lax.ppermute(value, axis, [(i, i ^ bit) for i in range(lax.axis_size(axis))])


def bits_of(axis):
    size = lax.axis_size(axis)
    assert size & (size - 1) == 0
    return [1 << k for k in range(size.bit_length() - 1)]


def reduce_halves(keep, give, swaps):
    half = keep + swap(give, *swaps[0])
    for axis, bit in swaps[1:]:
        half = half + swap(half, axis, bit)
    return half, swap(half, *swaps[0])


def in_hbm(value):
    return pltpu.with_memory_space_constraint(value, pltpu.HBM)


def call(kernel, out_shape, in_specs, limit, scratch=()):
    shapes = [jax.ShapeDtypeStruct(shape, dtype) for shape, dtype in out_shape]
    return pl.pallas_call(
        kernel,
        out_shape=shapes,
        in_specs=in_specs,
        out_specs=[VMEM] * len(shapes),
        scratch_shapes=list(scratch),
        compiler_params=pltpu.CompilerParams(vmem_limit_bytes=limit << 20),
    )


def on_device(
    tokens_in,
    key_cache,
    value_cache,
    cache_len,
    bucket_table,
    rel_bias,
    attn_gain,
    moe_gain,
    w_qkv,
    w_out,
    router,
    expert_choice,
    w_gate_up,
    w_down,
):
    steps, requests, width = tokens_in.shape
    tokens = steps * requests
    half = tokens // 2
    _, cache_rows, features = key_cache.shape
    heads = features // HEAD_DIM
    rows = tokens * heads
    buckets = rel_bias.shape[0]
    hidden_local = w_down.shape[0]
    packed_shape = (tokens, features + LANES)
    flat_in = tokens_in.reshape(tokens, width)
    dma = pltpu.SemaphoreType.DMA

    (packed,) = call(
        functools.partial(attend_kernel, steps, requests, heads),
        [(packed_shape, F32)],
        [HBM] * 8,
        16,
        [
            pltpu.SMEM(cache_len.shape, jnp.int32),
            pltpu.VMEM(flat_in.shape, BF16),
            pltpu.VMEM((1, width), F32),
            pltpu.VMEM((1,) + bucket_table.shape, jnp.int32),
            pltpu.VMEM((heads, buckets), F32),
            pltpu.VMEM(w_qkv.shape, BF16),
            pltpu.VMEM(key_cache.shape, BF16),
            pltpu.VMEM(value_cache.shape, BF16),
            pltpu.VMEM((rows, cache_rows), F32),
            pltpu.VMEM((rows, cache_rows), F32),
            pltpu.VMEM((rows, cache_rows), BF16),
            pltpu.VMEM((buckets, LANES), jnp.int32),
            pltpu.VMEM((buckets, steps * heads, LANES), F32),
            dma((5,)),
            dma((3,)),
            dma((requests,)),
            dma((requests,)),
        ],
    )(*map(in_hbm, (cache_len, flat_in, attn_gain, bucket_table, rel_bias.T, w_qkv, key_cache, value_cache)))

    seq_bits = bits_of("seq")
    for bit in seq_bits[:-1]:
        (packed,) = call(functools.partial(merge_kernel, features), [(packed_shape, F32)], [VMEM, VMEM], 2)(
            packed, swap(packed, "seq", bit)
        )
    half_shape = ((half, width), F32)
    keep, give = call(
        functools.partial(project_kernel, steps, requests, features), [half_shape, half_shape], [VMEM] * 3, 4
    )(packed, swap(packed, "seq", seq_bits[-1]), w_out)

    tp_swaps = [("tp", bit) for bit in bits_of("tp")]
    mine, other = reduce_halves(keep, give, tp_swaps)

    mid, keep, give = call(expert_kernel, [((tokens, width), F32), half_shape, half_shape], [VMEM] * 8, 8)(
        mine, other, flat_in, moe_gain[None], router.T, expert_choice.transpose(0, 2, 1), w_gate_up, w_down
    )

    mine, other = reduce_halves(keep, give, tp_swaps + [("seq", bit) for bit in seq_bits])
    low = lax.axis_index("tp") % 2 == 0
    mixture = jnp.concatenate([jnp.where(low, mine, other), jnp.where(low, other, mine)])
    return (mid + mixture).astype(BF16).reshape(steps, requests, width)


def solution(mesh):
    return jax.shard_map(
        on_device,
        mesh=mesh,
        in_specs=(
            P(),
            P(None, "seq", "tp"),
            P(None, "seq", "tp"),
            P(),
            P(),
            P(None, "tp"),
            P(),
            P(),
            P(None, None, "tp"),
            P("tp", None),
            P(),
            P(),
            P(None, ("seq", "tp"), None),
            P(("seq", "tp"), None),
        ),
        out_specs=P(),
        check_vma=False,
    )
```

time: 85.5 us -> 66.9 us (0.78)
  local copies, waits for them, and re-layouts: 13.1 us -> 1.84 us
  Pallas kernels: 21.7 us -> 14 us
    unnamed x30 -> x14, local copies, waits for them, and re-layouts: 11.7 us -> 1.84 us
    pallas_call x1, Pallas kernels: 14.1 us -> 9.88 us  [on_device(): call(functools.partial(attend_kernel, steps, requests, heads), [(packed_s...]
    pallas_call x1, Pallas kernels: 6.73 us -> 3.22 us  [on_device(): call(expert_kernel, [((tokens, width), F32), half_shape, half_shape], [VM...]
  transfers between devices with their start and end apart: 12 -> 12, of which waited for: 12 -> 12; matrix products, arithmetic and copies ran while one was open for 1% -> 0% of each run, Pallas kernels for 0% -> 0%
where the time goes in v4:
time: 66.9 us; the launch traced here: 66.2 us
  waiting for transfers between devices  30.2 us (45%)
  starting transfers between devices  19.2 us (29%)
  Pallas kernels  14 us (21%)
  local copies, waits for them, and re-layouts  1.84 us (3%)
  other arithmetic  0.84 us (1%)
    ppermute x12, waiting for transfers between devices, swap(): lax.ppermute(value, axis, [(i, i ^ bit) for i in range(lax.axis_size(axis...  30.2 us
    ppermute x12, starting transfers between devices, swap(): lax.ppermute(value, axis, [(i, i ^ bit) for i in range(lax.axis_size(axis...  19.2 us
    pallas_call x1, Pallas kernels, on_device(): call(functools.partial(attend_kernel, steps, requests, heads), [(packed_s...  9.88 us
    pallas_call x1, Pallas kernels, on_device(): call(expert_kernel, [((tokens, width), F32), half_shape, half_shape], [VM...  3.22 us
    unnamed x14, local copies, waits for them, and re-layouts  1.84 us
  transfers between devices with their start and end apart: 12, of which 12 were waited for; matrix products, arithmetic and copies ran while one was open for 0% of the time, Pallas kernels for 0%

profile of v4, /device:TPU:0, one launch (start us, length us, event | category | flops | bytes accessed | tf_op | source)
XLA Modules:
  0.0 66.2 jit_solution(8891473858680422287)
XLA Ops:
  0.0 9.9 %shard_map.136.one_ref = f32[64,384]{1,0:T(8,128)S(1)} custom-call(s32[16]{0:T(128)} %len_hbm.1, bf16[64,1024]{1,0:T(8,128)(2,1)} %bitcast.6, f32[1024]{0:T(1024)} %gain_hbm.1, s32[2052]{0:T(1024)} %table_hbm.1, f32[4,32]{1,0:T(4,128)} %bitcast.11, bf16[3,1024,256]{2,1,0:T(8,128)(2,1)} %w_hbm.1, bf16[16,256,256]{2,1,0:T(8,128)(2,1)} %k_hbm.1, ...), custom_call_target="tpu_custom_call" | custom-call | tf_op jit(solution)/shard_map/pallas_call | solution.py:317
  9.9 0.0 copy-start.3
  9.9 3.0 %collective-permute-start = (f32[64,384]{1,0:T(8,128)S(1)}, f32[64,384]{1,0:T(8,128)S(1)}, u32[]{:S(2)}, u32[]{:S(2)}) collective-permute-start(f32[64,384]{1,0:T(8,128)S(1)} %shard_map.136.one_ref), channel_id=1, source_target_pairs={{0,4},{4,0},{8,12},{12,8},{16,20},{20,16},{24,28},{28,24},{1,5},{5... | collective-permute-start | bytes 294920 | tf_op jit(solution)/shard_map/ppermute | solution.py:257
  12.9 2.8 %collective-permute-done.two_ref = f32[64,384]{1,0:T(8,128)S(1)} collective-permute-done((f32[64,384]{1,0:T(8,128)S(1)}, f32[64,384]{1,0:T(8,128)S(1)}, u32[]{:S(2)}, u32[]{:S(2)}) %collective-permute-start) | collective-permute-done | bytes 98336 | tf_op jit(solution)/shard_map/ppermute | solution.py:257
  15.7 0.2 shard_map.137.one_ref
  15.9 2.0 %collective-permute-start.1 = (f32[64,384]{1,0:T(8,128)S(1)}, f32[64,384]{1,0:T(8,128)S(1)}, u32[]{:S(2)}, u32[]{:S(2)}) collective-permute-start(f32[64,384]{1,0:T(8,128)S(1)} %shard_map.137.one_ref), channel_id=1, source_target_pairs={{0,8},{4,12},{8,0},{12,4},{16,24},{20,28},{24,16},{28,20},{1,9},{5... | collective-permute-start | bytes 294920 | tf_op jit(solution)/shard_map/ppermute | solution.py:257
  17.9 2.7 %collective-permute-done.1.two_ref = f32[64,384]{1,0:T(8,128)S(1)} collective-permute-done((f32[64,384]{1,0:T(8,128)S(1)}, f32[64,384]{1,0:T(8,128)S(1)}, u32[]{:S(2)}, u32[]{:S(2)}) %collective-permute-start.1) | collective-permute-done | bytes 98336 | tf_op jit(solution)/shard_map/ppermute | solution.py:257
  20.6 0.2 shard_map.138.one_ref
  20.8 3.0 %collective-permute-start.2 = (f32[64,384]{1,0:T(8,128)S(1)}, f32[64,384]{1,0:T(8,128)S(1)}, u32[]{:S(2)}, u32[]{:S(2)}) collective-permute-start(f32[64,384]{1,0:T(8,128)S(1)} %shard_map.138.one_ref), channel_id=1, source_target_pairs={{0,16},{4,20},{8,24},{12,28},{16,0},{20,4},{24,8},{28,12},{1,17},{... | collective-permute-start | bytes 294920 | tf_op jit(solution)/shard_map/ppermute | solution.py:257
  23.8 2.6 %collective-permute-done.2.two_ref = f32[64,384]{1,0:T(8,128)S(1)} collective-permute-done((f32[64,384]{1,0:T(8,128)S(1)}, f32[64,384]{1,0:T(8,128)S(1)}, u32[]{:S(2)}, u32[]{:S(2)}) %collective-permute-start.2) | collective-permute-done | bytes 98336 | tf_op jit(solution)/shard_map/ppermute | solution.py:257
  26.4 0.6 shard_map.139
  26.9 0.1 collective-permute-start.3
  27.0 1.3 %collective-permute-done.3 = f32[32,1024]{1,0:T(8,128)S(1)} collective-permute-done((f32[32,1024]{1,0:T(8,128)S(1)}, f32[32,1024]{1,0:T(8,128)S(1)}, u32[]{:S(2)}, u32[]{:S(2)}) %collective-permute-start.3) | collective-permute-done | bytes 131104 | tf_op jit(solution)/shard_map/ppermute | solution.py:257
  28.4 1.9 %collective-permute-start.4 = (f32[32,1024]{1,0:T(8,128)S(1)}, f32[32,1024]{1,0:T(8,128)S(1)}, u32[]{:S(2)}, u32[]{:S(2)}) collective-permute-start(f32[32,1024]{1,0:T(8,128)S(1)} %add.28), channel_id=1, source_target_pairs={{0,2},{1,3},{2,0},{3,1},{4,6},{5,7},{6,4},{7,5},{8,10},{9,11},{10,... | collective-permute-start | bytes 393224 | tf_op jit(solution)/shard_map/ppermute | solution.py:257
  30.3 3.8 %collective-permute-done.4 = f32[32,1024]{1,0:T(8,128)S(1)} collective-permute-done((f32[32,1024]{1,0:T(8,128)S(1)}, f32[32,1024]{1,0:T(8,128)S(1)}, u32[]{:S(2)}, u32[]{:S(2)}) %collective-permute-start.4) | collective-permute-done | bytes 131104 | tf_op jit(solution)/shard_map/ppermute | solution.py:257
  34.1 0.1 collective-permute-start.5
  34.2 1.3 %collective-permute-done.5.back_ref = f32[32,1024]{1,0:T(8,128)S(1)} collective-permute-done((f32[32,1024]{1,0:T(8,128)S(1)}, f32[32,1024]{1,0:T(8,128)S(1)}, u32[]{:S(2)}, u32[]{:S(2)}) %collective-permute-start.5) | collective-permute-done | bytes 131104 | tf_op jit(solution)/shard_map/ppermute | solution.py:257
  35.6 1.8 %copy-done.1 = bf16[1408,1024]{1,0:T(8,128)(2,1)S(1)} copy-done((bf16[1408,1024]{1,0:T(8,128)(2,1)S(1)}, bf16[1408,1024]{1,0:T(8,128)(2,1)}, u32[]{:S(2)}) %copy-start.1) | copy-done | bytes 2883608
  37.4 3.2 %shard_map.140 = (f32[64,1024]{1,0:T(8,128)S(1)}, f32[32,1024]{1,0:T(8,128)S(1)}, f32[32,1024]{1,0:T(8,128)S(1)}) custom-call(f32[32,1024]{1,0:T(8,128)S(1)} %add.29.half_ref, f32[32,1024]{1,0:T(8,128)S(1)} %collective-permute-done.5.back_ref, bf16[64,1024]{1,0:T(8,128)(2,1)S(1)} %bitcast.7, f32[1,1024]{1,0:T(1,128)S(1)} %bitcast.9, ...), custom_call_target="tpu_custom_call" | custom-call | tf_op jit(solution)/shard_map/pallas_call | solution.py:356
  40.6 0.2 collective-permute-start.6
  40.8 1.2 %collective-permute-done.6 = f32[32,1024]{1,0:T(8,128)S(1)} collective-permute-done((f32[32,1024]{1,0:T(8,128)S(1)}, f32[32,1024]{1,0:T(8,128)S(1)}, u32[]{:S(2)}, u32[]{:S(2)}) %collective-permute-start.6) | collective-permute-done | bytes 131104 | tf_op jit(solution)/shard_map/ppermute | solution.py:257
  42.0 1.8 %collective-permute-start.7 = (f32[32,1024]{1,0:T(8,128)S(1)}, f32[32,1024]{1,0:T(8,128)S(1)}, u32[]{:S(2)}, u32[]{:S(2)}) collective-permute-start(f32[32,1024]{1,0:T(8,128)S(1)} %add.31), channel_id=1, source_target_pairs={{0,2},{1,3},{2,0},{3,1},{4,6},{5,7},{6,4},{7,5},{8,10},{9,11},{10,... | collective-permute-start | bytes 393224 | tf_op jit(solution)/shard_map/ppermute | solution.py:257
  43.8 3.8 %collective-permute-done.7 = f32[32,1024]{1,0:T(8,128)S(1)} collective-permute-done((f32[32,1024]{1,0:T(8,128)S(1)}, f32[32,1024]{1,0:T(8,128)S(1)}, u32[]{:S(2)}, u32[]{:S(2)}) %collective-permute-start.7) | collective-permute-done | bytes 131104 | tf_op jit(solution)/shard_map/ppermute | solution.py:257
  47.7 1.8 %collective-permute-start.8 = (f32[32,1024]{1,0:T(8,128)S(1)}, f32[32,1024]{1,0:T(8,128)S(1)}, u32[]{:S(2)}, u32[]{:S(2)}) collective-permute-start(f32[32,1024]{1,0:T(8,128)S(1)} %add.32), channel_id=1, source_target_pairs={{0,4},{4,0},{8,12},{12,8},{16,20},{20,16},{24,28},{28,24},{1,5},{5... | collective-permute-start | bytes 393224 | tf_op jit(solution)/shard_map/ppermute | solution.py:257
  49.4 3.3 %collective-permute-done.8 = f32[32,1024]{1,0:T(8,128)S(1)} collective-permute-done((f32[32,1024]{1,0:T(8,128)S(1)}, f32[32,1024]{1,0:T(8,128)S(1)}, u32[]{:S(2)}, u32[]{:S(2)}) %collective-permute-start.8) | collective-permute-done | bytes 131104 | tf_op jit(solution)/shard_map/ppermute | solution.py:257
  52.7 2.0 %collective-permute-start.9 = (f32[32,1024]{1,0:T(8,128)S(1)}, f32[32,1024]{1,0:T(8,128)S(1)}, u32[]{:S(2)}, u32[]{:S(2)}) collective-permute-start(f32[32,1024]{1,0:T(8,128)S(1)} %add.33), channel_id=1, source_target_pairs={{0,8},{4,12},{8,0},{12,4},{16,24},{20,28},{24,16},{28,20},{1,9},{5... | collective-permute-start | bytes 393224 | tf_op jit(solution)/shard_map/ppermute | solution.py:257
  54.7 3.0 %collective-permute-done.9 = f32[32,1024]{1,0:T(8,128)S(1)} collective-permute-done((f32[32,1024]{1,0:T(8,128)S(1)}, f32[32,1024]{1,0:T(8,128)S(1)}, u32[]{:S(2)}, u32[]{:S(2)}) %collective-permute-start.9) | collective-permute-done | bytes 131104 | tf_op jit(solution)/shard_map/ppermute | solution.py:257
  57.8 3.4 %collective-permute-start.10 = (f32[32,1024]{1,0:T(8,128)S(1)}, f32[32,1024]{1,0:T(8,128)S(1)}, u32[]{:S(2)}, u32[]{:S(2)}) collective-permute-start(f32[32,1024]{1,0:T(8,128)S(1)} %add.34), channel_id=1, source_target_pairs={{0,16},{4,20},{8,24},{12,28},{16,0},{20,4},{24,8},{28,12},{1,17},{... | collective-permute-start | bytes 393224 | tf_op jit(solution)/shard_map/ppermute | solution.py:257
  61.1 2.9 %collective-permute-done.10 = f32[32,1024]{1,0:T(8,128)S(1)} collective-permute-done((f32[32,1024]{1,0:T(8,128)S(1)}, f32[32,1024]{1,0:T(8,128)S(1)}, u32[]{:S(2)}, u32[]{:S(2)}) %collective-permute-start.10) | collective-permute-done | bytes 131104 | tf_op jit(solution)/shard_map/ppermute | solution.py:257
  64.1 0.1 collective-permute-start.11
  64.2 1.3 %collective-permute-done.11 = f32[32,1024]{1,0:T(8,128)S(1)} collective-permute-done((f32[32,1024]{1,0:T(8,128)S(1)}, f32[32,1024]{1,0:T(8,128)S(1)}, u32[]{:S(2)}, u32[]{:S(2)}) %collective-permute-start.11) | collective-permute-done | bytes 131104 | tf_op jit(solution)/shard_map/ppermute | solution.py:257
  65.5 0.7 %fusion = bf16[64,1024]{1,0:T(8,128)(2,1)} fusion(f32[64,1024]{1,0:T(8,128)S(1)} %get-tuple-element.12, f32[32,1024]{1,0:T(8,128)S(1)} %get-tuple-element.16, f32[32,1024]{1,0:T(8,128)S(1)} %get-tuple-element.15), kind=kLoop, calls=%fused_computation.1 | loop fusion | flops 196608 | bytes 655360 | tf_op jit(solution)/shard_map/convert_element_type | solution.py:363
  (20 shorter events, 0.2 us)
Async XLA Ops:
  0.0 26.4 %copy-start.2 = (bf16[256,1024]{1,0:T(8,128)(2,1)S(1)}, bf16[256,1024]{1,0:T(8,128)(2,1)}, u32[]{:S(2)}) copy-start(bf16[256,1024]{1,0:T(8,128)(2,1)} %w_ref.1) | copy-start | bytes 1572868
  0.0 35.5 %copy-start = (bf16[2,1408,1024]{2,1,0:T(8,128)(2,1)S(1)}, bf16[2,1408,1024]{2,1,0:T(8,128)(2,1)}, u32[]{:S(2)}) copy-start(bf16[2,1408,1024]{2,1,0:T(8,128)(2,1)} %up_ref.1) | copy-start | bytes 17301508
  9.9 25.6 %copy-start.3 = (bf16[4,16,1024]{2,1,0:T(8,128)(2,1)S(1)}, bf16[4,16,1024]{2,1,0:T(8,128)(2,1)}, u32[]{:S(2)}) copy-start(bf16[4,16,1024]{2,1,0:T(8,128)(2,1)} %param.14) | copy-start | bytes 393220
  9.9 25.6 %copy-start.4 = (bf16[1024,16]{0,1:T(8,128)(2,1)S(1)}, bf16[1024,16]{0,1:T(8,128)(2,1)}, u32[]{:S(2)}) copy-start(bf16[1024,16]{0,1:T(8,128)(2,1)} %param.24) | copy-start | bytes 98308
  9.9 25.6 %copy-start.5 = (f32[1024]{0:T(1024)S(1)}, f32[1024]{0:T(1024)}, u32[]{:S(2)}) copy-start(f32[1024]{0:T(1024)} %param.21) | copy-start | bytes 12292
  9.9 25.6 %copy-start.6 = (s32[4,16,2]{1,2,0:T(2,128)S(1)}, s32[4,16,2]{1,2,0:T(2,128)}, u32[]{:S(2)}) copy-start(s32[4,16,2]{1,2,0:T(2,128)} %param.25) | copy-start | bytes 1540
  9.9 5.8 %collective-permute-start = (f32[64,384]{1,0:T(8,128)S(1)}, f32[64,384]{1,0:T(8,128)S(1)}, u32[]{:S(2)}, u32[]{:S(2)}) collective-permute-start(f32[64,384]{1,0:T(8,128)S(1)} %shard_map.136.one_ref), channel_id=1, source_target_pairs={{0,4},{4,0},{8,12},{12,8},{16,20},{20,16},{24,28},{28,24},{1,5},{5... | collective-permute-start | bytes 294920 | tf_op jit(solution)/shard_map/ppermute | solution.py:257
  15.9 4.7 %collective-permute-start.1 = (f32[64,384]{1,0:T(8,128)S(1)}, f32[64,384]{1,0:T(8,128)S(1)}, u32[]{:S(2)}, u32[]{:S(2)}) collective-permute-start(f32[64,384]{1,0:T(8,128)S(1)} %shard_map.137.one_ref), channel_id=1, source_target_pairs={{0,8},{4,12},{8,0},{12,4},{16,24},{20,28},{24,16},{28,20},{1,9},{5... | collective-permute-start | bytes 294920 | tf_op jit(solution)/shard_map/ppermute | solution.py:257
  20.8 5.6 %collective-permute-start.2 = (f32[64,384]{1,0:T(8,128)S(1)}, f32[64,384]{1,0:T(8,128)S(1)}, u32[]{:S(2)}, u32[]{:S(2)}) collective-permute-start(f32[64,384]{1,0:T(8,128)S(1)} %shard_map.138.one_ref), channel_id=1, source_target_pairs={{0,16},{4,20},{8,24},{12,28},{16,0},{20,4},{24,8},{28,12},{1,17},{... | collective-permute-start | bytes 294920 | tf_op jit(solution)/shard_map/ppermute | solution.py:257
  26.9 1.4 %collective-permute-start.3 = (f32[32,1024]{1,0:T(8,128)S(1)}, f32[32,1024]{1,0:T(8,128)S(1)}, u32[]{:S(2)}, u32[]{:S(2)}) collective-permute-start(f32[32,1024]{1,0:T(8,128)S(1)} %get-tuple-element.11), channel_id=1, source_target_pairs={{0,1},{1,0},{2,3},{3,2},{4,5},{5,4},{6,7},{7,6},{8,9},{9,8},{10,11... | collective-permute-start | bytes 393224 | tf_op jit(solution)/shard_map/ppermute | solution.py:257
  28.4 5.7 %collective-permute-start.4 = (f32[32,1024]{1,0:T(8,128)S(1)}, f32[32,1024]{1,0:T(8,128)S(1)}, u32[]{:S(2)}, u32[]{:S(2)}) collective-permute-start(f32[32,1024]{1,0:T(8,128)S(1)} %add.28), channel_id=1, source_target_pairs={{0,2},{1,3},{2,0},{3,1},{4,6},{5,7},{6,4},{7,5},{8,10},{9,11},{10,... | collective-permute-start | bytes 393224 | tf_op jit(solution)/shard_map/ppermute | solution.py:257
  34.1 1.4 %collective-permute-start.5 = (f32[32,1024]{1,0:T(8,128)S(1)}, f32[32,1024]{1,0:T(8,128)S(1)}, u32[]{:S(2)}, u32[]{:S(2)}) collective-permute-start(f32[32,1024]{1,0:T(8,128)S(1)} %add.29.half_ref), channel_id=1, source_target_pairs={{0,1},{1,0},{2,3},{3,2},{4,5},{5,4},{6,7},{7,6},{8,9},{9,8},{10,11... | collective-permute-start | bytes 393224 | tf_op jit(solution)/shard_map/ppermute | solution.py:257
  35.6 1.8 %copy-start.1 = (bf16[1408,1024]{1,0:T(8,128)(2,1)S(1)}, bf16[1408,1024]{1,0:T(8,128)(2,1)}, u32[]{:S(2)}) copy-start(bf16[1408,1024]{1,0:T(8,128)(2,1)} %down_ref.1) | copy-start | bytes 8650756
  40.6 1.4 %collective-permute-start.6 = (f32[32,1024]{1,0:T(8,128)S(1)}, f32[32,1024]{1,0:T(8,128)S(1)}, u32[]{:S(2)}, u32[]{:S(2)}) collective-permute-start(f32[32,1024]{1,0:T(8,128)S(1)} %get-tuple-element.14), channel_id=1, source_target_pairs={{0,1},{1,0},{2,3},{3,2},{4,5},{5,4},{6,7},{7,6},{8,9},{9,8},{10,11... | collective-permute-start | bytes 393224 | tf_op jit(solution)/shard_map/ppermute | solution.py:257
  42.0 5.6 %collective-permute-start.7 = (f32[32,1024]{1,0:T(8,128)S(1)}, f32[32,1024]{1,0:T(8,128)S(1)}, u32[]{:S(2)}, u32[]{:S(2)}) collective-permute-start(f32[32,1024]{1,0:T(8,128)S(1)} %add.31), channel_id=1, source_target_pairs={{0,2},{1,3},{2,0},{3,1},{4,6},{5,7},{6,4},{7,5},{8,10},{9,11},{10,... | collective-permute-start | bytes 393224 | tf_op jit(solution)/shard_map/ppermute | solution.py:257
  47.7 5.0 %collective-permute-start.8 = (f32[32,1024]{1,0:T(8,128)S(1)}, f32[32,1024]{1,0:T(8,128)S(1)}, u32[]{:S(2)}, u32[]{:S(2)}) collective-permute-start(f32[32,1024]{1,0:T(8,128)S(1)} %add.32), channel_id=1, source_target_pairs={{0,4},{4,0},{8,12},{12,8},{16,20},{20,16},{24,28},{28,24},{1,5},{5... | collective-permute-start | bytes 393224 | tf_op jit(solution)/shard_map/ppermute | solution.py:257
  52.7 5.0 %collective-permute-start.9 = (f32[32,1024]{1,0:T(8,128)S(1)}, f32[32,1024]{1,0:T(8,128)S(1)}, u32[]{:S(2)}, u32[]{:S(2)}) collective-permute-start(f32[32,1024]{1,0:T(8,128)S(1)} %add.33), channel_id=1, source_target_pairs={{0,8},{4,12},{8,0},{12,4},{16,24},{20,28},{24,16},{28,20},{1,9},{5... | collective-permute-start | bytes 393224 | tf_op jit(solution)/shard_map/ppermute | solution.py:257
  57.8 6.3 %collective-permute-start.10 = (f32[32,1024]{1,0:T(8,128)S(1)}, f32[32,1024]{1,0:T(8,128)S(1)}, u32[]{:S(2)}, u32[]{:S(2)}) collective-permute-start(f32[32,1024]{1,0:T(8,128)S(1)} %add.34), channel_id=1, source_target_pairs={{0,16},{4,20},{8,24},{12,28},{16,0},{20,4},{24,8},{28,12},{1,17},{... | collective-permute-start | bytes 393224 | tf_op jit(solution)/shard_map/ppermute | solution.py:257
  64.1 1.4 %collective-permute-start.11 = (f32[32,1024]{1,0:T(8,128)S(1)}, f32[32,1024]{1,0:T(8,128)S(1)}, u32[]{:S(2)}, u32[]{:S(2)}) collective-permute-start(f32[32,1024]{1,0:T(8,128)S(1)} %add.35), channel_id=1, source_target_pairs={{0,1},{1,0},{2,3},{3,2},{4,5},{5,4},{6,7},{7,6},{8,9},{9,8},{10,11... | collective-permute-start | bytes 393224 | tf_op jit(solution)/shard_map/ppermute | solution.py:257

commit v5 on v4

--- a/solution.py
+++ b/solution.py
@@ -141,9 +141,10 @@
     fresh_bias = jnp.concatenate([fresh_bias] * requests, axis=0)
     fresh_scores = jnp.where(fresh_live, dot_nt(spread, fresh_keys) + fresh_bias, NEG)
 
+    for copy in k_copies:
+        copy.wait()
     for r in range(requests):
         at = slice(r * group, (r + 1) * group)
-        k_copies[r].wait()
         score_buf[at, :] = dot_nt(spread[at], k_buf[r])
     scores = score_buf[...] + bias_buf[...]
     top = jnp.maximum(jnp.max(scores, axis=1, keepdims=True), jnp.max(fresh_scores, axis=1, keepdims=True))
@@ -152,47 +153,73 @@
     total = jnp.sum(weights, axis=1, keepdims=True) + jnp.sum(fresh_weights, axis=1, keepdims=True)
     weight_buf[...] = weights.astype(BF16)
     score_buf[...] = dot(fresh_weights.astype(BF16), fresh_values)
+    for copy in v_copies:
+        copy.wait()
     for r in range(requests):
         at = slice(r * group, (r + 1) * group)
-        v_copies[r].wait()
         score_buf[at, :] += dot(weight_buf[at, :], v_buf[r])
 
     sums = jnp.where(own_head, score_buf[...], 0.0)
     lane = iota((1, LANES), 1)
     stats = jnp.where(lane == row_head, top, jnp.where(lane == heads + row_head, total, 0.0))
     first = iota((8, 1), 0) < steps
-    for values, cols in ((sums, slice(0, features)), (stats, slice(features, features + LANES))):
+
+    def fold(values):
+        pairs = []
         for pair in range(requests // 2):
             folded = []
             for r in (2 * pair, 2 * pair + 1):
                 part = values[r * group : r * group + 8] + values[r * group + 8 : r * group + 16]
                 folded.append(part + pltpu.roll(part, steps, 0))
-            out_ref[8 * pair : 8 * pair + 8, cols] = jnp.where(first, folded[0], folded[1])
-
-
-def widen(stats, first, features):
-    heads = features // HEAD_DIM
-    lane_head = over(iota((1, features), 1), HEAD_DIM)
-    wide = jnp.broadcast_to(stats[:, first : first + 1], (stats.shape[0], features))
+            pairs.append(jnp.where(first, folded[0], folded[1]))
+        return jnp.concatenate(pairs, axis=0)
+
+    out_ref[:tokens, :] = fold(sums)
+    out_ref[tokens:, :] = jnp.zeros((2 * heads, features), F32)
+    out_ref[tokens:, :LANES] = turned(fold(stats))[: 2 * heads]
+
+
+def turned(value):
+    rows = value.shape[0]
+    if rows < LANES:
+        value = jnp.concatenate([value, jnp.zeros((LANES - rows, LANES), F32)], axis=0)
+    return value.T
+
+
+def widen(columns, first, heads):
+    lane_head = over(iota((1, heads * HEAD_DIM), 1), HEAD_DIM)
+    wide = jnp.broadcast_to(columns[:, first : first + 1], (columns.shape[0], heads * HEAD_DIM))
     for h in range(1, heads):
-        wide = jnp.where(lane_head == h, stats[:, first + h : first + h + 1], wide)
+        wide = jnp.where(lane_head == h, columns[:, first + h : first + h + 1], wide)
     return wide
 
 
-def merged(features, one_ref, two_ref):
-    heads = features // HEAD_DIM
-    one, two = one_ref[:, features:], two_ref[:, features:]
-    top = jnp.maximum(one, two)
-    scale_one, scale_two = jnp.exp(one - top), jnp.exp(two - top)
-    totals = one * pltpu.roll(scale_one, heads, 1) + two * pltpu.roll(scale_two, heads, 1)
-    sums = one_ref[:, :features] * widen(scale_one, 0, features) + two_ref[:, :features] * widen(scale_two, 0, features)
-    return sums, jnp.where(iota(top.shape, 1) < heads, top, totals)
-
-
-def merge_kernel(features, one_ref, two_ref, out_ref):
-    sums, stats = merged(features, one_ref, two_ref)
-    out_ref[:, :features] = sums
-    out_ref[:, features:] = stats
+def tree(operation, values):
+    while len(values) > 1:
+        values = [operation(*values[i : i + 2]) for i in range(0, len(values), 2)]
+    return values[0]
+
+
+def merge_parts(tokens, parts):
+    heads = parts[0].shape[1] // HEAD_DIM
+    stats = [part[tokens:, :LANES] for part in parts]
+    top = tree(jnp.maximum, stats)
+    scales = [jnp.exp(stat - top) for stat in stats]
+    totals = tree(jnp.add, [stat * pltpu.roll(scale, heads, 0) for stat, scale in zip(stats, scales)])
+    stat = jnp.where(iota((2 * heads, 1), 0) < heads, top, totals)
+    columns = turned(jnp.concatenate(scales + [stat], axis=0))[:tokens]
+    sums = tree(
+        jnp.add, [part[:tokens, :] * widen(columns, 2 * heads * i, heads) for i, part in enumerate(parts)]
+    )
+    return sums, stat, widen(columns, 2 * heads * len(parts) + heads, heads)
+
+
+def merge_kernel(tokens, *refs):
+    out_ref = refs[-1]
+    sums, stat, _ = merge_parts(tokens, refs[:-1])
+    out_ref[:tokens, :] = sums
+    out_ref[tokens:, :] = jnp.zeros((stat.shape[0], sums.shape[1]), F32)
+    out_ref[tokens:, :LANES] = stat
 
 
 def store_halves(value, bit, keep_ref, give_ref):
@@ -202,10 +229,10 @@
     give_ref[...] = jnp.where(low, value[half:], value[:half])
 
 
-def project_kernel(steps, requests, features, one_ref, two_ref, w_ref, keep_ref, give_ref):
-    sums, stats = merged(features, one_ref, two_ref)
-    attended = (sums / widen(stats, features // HEAD_DIM, features)).astype(BF16)
+def project_kernel(steps, requests, one_ref, two_ref, w_ref, keep_ref, give_ref):
     tokens = steps * requests
+    sums, _, totals = merge_parts(tokens, (one_ref, two_ref))
+    attended = (sums / totals).astype(BF16)
     row = iota((tokens, 1), 0)
     source = modulo(row, requests) * steps + over(row, requests)
     order = jnp.where(source == iota((1, tokens), 1), 1.0, 0.0).astype(BF16)
@@ -218,9 +245,15 @@
 
 
 def expert_kernel(
-    half_ref, back_ref, tokens_ref, gain_ref, router_ref, choice_ref, up_ref, down_ref, mid_ref, keep_ref, give_ref
+    half_ref, back_ref, tokens_ref, gain_ref, router_ref, choice_ref, up_ref, down_hbm,
+    mid_ref, keep_ref, give_ref, down_ref, down_sem,
 ):
     hidden_local = down_ref.shape[0]
+    chunks = chunks_of(hidden_local, 256)
+    copies = []
+    for i, (at, size) in enumerate(chunks):
+        copies.append(pltpu.make_async_copy(down_hbm.at[pl.ds(at, size)], down_ref.at[pl.ds(at, size)], down_sem.at[i]))
+        copies[-1].start()
     half = half_ref.shape[0]
     steps, _, requests = choice_ref.shape
     low = lax.axis_index("tp") % 2 == 0
@@ -243,31 +276,56 @@
     second = 1.0 - first
     device = lax.axis_index("seq") * lax.axis_size("tp") + lax.axis_index("tp")
     total = jnp.zeros(mid_ref.shape, F32)
-    for at, size in chunks_of(hidden_local, 256):
+    hiddens = []
+    for at, size in chunks:
         column_expert = (device * hidden_local + at + iota((1, size), 1)) // FF
         coef = jnp.where(column_expert == choices[0], first, jnp.where(column_expert == choices[1], second, 0.0))
         gate = dot_nt(moe_in, up_ref[0, at : at + size, :])
         up = dot_nt(moe_in, up_ref[1, at : at + size, :])
-        hidden = (jax.nn.gelu(gate, approximate=True) * up * coef).astype(BF16)
+        hiddens.append((jax.nn.gelu(gate, approximate=True) * up * coef).astype(BF16))
+    for copy in copies:
+        copy.wait()
+    for (at, size), hidden in zip(chunks, hiddens):
         total = total + dot(hidden, down_ref[at : at + size, :])
     store_halves(total, 1, keep_ref, give_ref)
 
 
-def swap(value, axis, bit):
-    return lax.ppermute(value, axis, [(i, i ^ bit) for i in range(lax.axis_size(axis))])
-
-
-def bits_of(axis):
+def device_bits(axis):
     size = lax.axis_size(axis)
     assert size & (size - 1) == 0
-    return [1 << k for k in range(size.bit_length() - 1)]
-
-
-def reduce_halves(keep, give, swaps):
-    half = keep + swap(give, *swaps[0])
-    for axis, bit in swaps[1:]:
-        half = half + swap(half, axis, bit)
-    return half, swap(half, *swaps[0])
+    return [(axis, 1 << k) for k in range(size.bit_length() - 1)]
+
+
+def swap(value, *bits):
+    sizes = {axis: lax.axis_size(axis) for axis in ("seq", "tp") if axis in dict(bits)}
+    flips = {axis: sum(bit for other, bit in bits if other == axis) for axis in sizes}
+    if len(sizes) == 1:
+        (axis,) = sizes
+        return lax.ppermute(value, axis, [(i, i ^ flips[axis]) for i in range(sizes[axis])])
+    (one, two) = sizes
+    flat = [i * sizes[two] + j for i in range(sizes[one]) for j in range(sizes[two])]
+    there = [(i ^ flips[one]) * sizes[two] + (j ^ flips[two]) for i in range(sizes[one]) for j in range(sizes[two])]
+    return lax.ppermute(value, (one, two), list(zip(flat, there)))
+
+
+def gathered(value, bits):
+    parts = [value]
+    for bit in bits:
+        parts.append(swap(value, bit))
+    if len(bits) == 2:
+        parts.append(swap(value, *bits))
+    return parts
+
+
+def stages(bits):
+    return [bits[:2]] + [[bit] for bit in bits[2:]] if len(bits) > 2 else [[bit] for bit in bits]
+
+
+def reduce_halves(keep, give, split, groups):
+    half = keep + swap(give, split)
+    for bits in groups:
+        half = tree(jnp.add, gathered(half, bits))
+    return half, swap(half, split)
 
 
 def in_hbm(value):
@@ -310,7 +368,7 @@
     rows = tokens * heads
     buckets = rel_bias.shape[0]
     hidden_local = w_down.shape[0]
-    packed_shape = (tokens, features + LANES)
+    packed_shape = (tokens + 2 * heads, features)
     flat_in = tokens_in.reshape(tokens, width)
     dma = pltpu.SemaphoreType.DMA
 
@@ -340,24 +398,31 @@
         ],
     )(*map(in_hbm, (cache_len, flat_in, attn_gain, bucket_table, rel_bias.T, w_qkv, key_cache, value_cache)))
 
-    seq_bits = bits_of("seq")
-    for bit in seq_bits[:-1]:
-        (packed,) = call(functools.partial(merge_kernel, features), [(packed_shape, F32)], [VMEM, VMEM], 2)(
-            packed, swap(packed, "seq", bit)
-        )
+    packed, w_gate_up = lax.optimization_barrier((packed, w_gate_up))
+    seq_bits, tp_bits = device_bits("seq"), device_bits("tp")
+    seq_stages = stages(seq_bits)
+    for bits in seq_stages[:-1]:
+        parts = gathered(packed, bits)
+        (packed,) = call(functools.partial(merge_kernel, tokens), [(packed_shape, F32)], [VMEM] * len(parts), 2)(*parts)
     half_shape = ((half, width), F32)
     keep, give = call(
-        functools.partial(project_kernel, steps, requests, features), [half_shape, half_shape], [VMEM] * 3, 4
-    )(packed, swap(packed, "seq", seq_bits[-1]), w_out)
-
-    tp_swaps = [("tp", bit) for bit in bits_of("tp")]
-    mine, other = reduce_halves(keep, give, tp_swaps)
-
-    mid, keep, give = call(expert_kernel, [((tokens, width), F32), half_shape, half_shape], [VMEM] * 8, 8)(
-        mine, other, flat_in, moe_gain[None], router.T, expert_choice.transpose(0, 2, 1), w_gate_up, w_down
+        functools.partial(project_kernel, steps, requests), [half_shape, half_shape], [VMEM] * 3, 4
+    )(packed, swap(packed, *seq_stages[-1]), w_out)
+
+    mine, other = reduce_halves(keep, give, tp_bits[0], [[bit] for bit in tp_bits[1:]])
+
+    n_chunks = len(chunks_of(hidden_local, 256))
+    mid, keep, give = call(
+        expert_kernel,
+        [((tokens, width), F32), half_shape, half_shape],
+        [VMEM] * 7 + [HBM],
+        12,
+        [pltpu.VMEM(w_down.shape, BF16), dma((n_chunks,))],
+    )(
+        mine, other, flat_in, moe_gain[None], router.T, expert_choice.transpose(0, 2, 1), w_gate_up, in_hbm(w_down)
     )
 
-    mine, other = reduce_halves(keep, give, tp_swaps + [("seq", bit) for bit in seq_bits])
+    mine, other = reduce_halves(keep, give, tp_bits[0], stages(tp_bits[1:] + seq_bits))
     low = lax.axis_index("tp") % 2 == 0
     mixture = jnp.concatenate([jnp.where(low, mine, other), jnp.where(low, other, mine)])
     return (mid + mixture).astype(BF16).reshape(steps, requests, width)

time: 66.9 us -> 62.6 us (0.936)
  waiting for transfers between devices: 30.2 us -> 35 us
  starting transfers between devices: 19.2 us -> 14.9 us
  Pallas kernels: 14 us -> 11.6 us
  local copies, waits for them, and re-layouts: 1.84 us -> 0.02 us
    ppermute x12 -> x14, waiting for transfers between devices: 30.2 us -> 35 us  [the longest x13 31.9 us: swap(): lax.ppermute(value, axis, [(i, i ^ flips[axis]) for i in range(sizes[axis...]
    ppermute x12 -> x14, starting transfers between devices: 19.2 us -> 14.9 us  [the longest x13 12.6 us: swap(): lax.ppermute(value, axis, [(i, i ^ flips[axis]) for i in range(sizes[axis...]
    pallas_call x1, Pallas kernels: 9.88 us -> 6.08 us  [on_device(): call(functools.partial(attend_kernel, steps, requests, heads), [(packed_s...]
    unnamed x14 -> x12, local copies, waits for them, and re-layouts: 1.84 us -> 0.02 us
    pallas_call x1, Pallas kernels: 3.22 us -> 4.56 us  [on_device(): call(expert_kernel, [((tokens, width), F32), half_shape, half_shape], [VM...]
  transfers between devices with their start and end apart: 12 -> 14, of which waited for: 12 -> 14; matrix products, arithmetic and copies ran while one was open for 0% -> 0% of each run, Pallas kernels for 0% -> 0%
where the time goes in v5:
time: 62.6 us; the launch traced here: 62.5 us
  waiting for transfers between devices  35 us (56%)
  starting transfers between devices  14.9 us (24%)
  Pallas kernels  11.6 us (19%)
  other arithmetic  0.83 us (1%)
    ppermute x13, waiting for transfers between devices, swap(): lax.ppermute(value, axis, [(i, i ^ flips[axis]) for i in range(sizes[axis...  31.9 us
    ppermute x13, starting transfers between devices, swap(): lax.ppermute(value, axis, [(i, i ^ flips[axis]) for i in range(sizes[axis...  12.6 us
    pallas_call x1, Pallas kernels, on_device(): call(functools.partial(attend_kernel, steps, requests, heads), [(packed_s...  6.08 us
    pallas_call x1, Pallas kernels, on_device(): call(expert_kernel, [((tokens, width), F32), half_shape, half_shape], [VM...  4.56 us
    ppermute x1, waiting for transfers between devices, swap(): return lax.ppermute(value, (one, two), list(zip(flat, there)))  3.08 us
    ppermute x1, starting transfers between devices, swap(): return lax.ppermute(value, (one, two), list(zip(flat, there)))  2.33 us
  transfers between devices with their start and end apart: 14, of which 14 were waited for; matrix products, arithmetic and copies ran while one was open for 0% of the time, Pallas kernels for 0%

profile of v5, /device:TPU:0, one launch (start us, length us, event | category | flops | bytes accessed | tf_op | source)
XLA Modules:
  0.0 62.5 jit_solution(4003758918295034290)
XLA Ops:
  0.0 6.1 %shard_map.136.refs_0_ = f32[72,256]{1,0:T(8,128)S(1)} custom-call(s32[16]{0:T(128)} %len_hbm.1, bf16[64,1024]{1,0:T(8,128)(2,1)} %bitcast.6, f32[1024]{0:T(1024)} %gain_hbm.1, s32[2052]{0:T(1024)} %table_hbm.1, f32[4,32]{1,0:T(4,128)} %bitcast.11, bf16[3,1024,256]{2,1,0:T(8,128)(2,1)} %w_hbm.1, bf16[16,256,256]{2,1,0:T(8,128)(2,1)} %k_hbm.1, ...), custom_call_target="tpu_custom_call" | custom-call | tf_op jit(solution)/shard_map/pallas_call | solution.py:375
  6.1 3.0 %collective-permute-start = (f32[72,256]{1,0:T(8,128)S(1)}, f32[72,256]{1,0:T(8,128)S(1)}, u32[]{:S(2)}, u32[]{:S(2)}) collective-permute-start(f32[72,256]{1,0:T(8,128)S(1)} %shard_map.136.refs_0_), channel_id=1, source_target_pairs={{0,4},{4,0},{8,12},{12,8},{16,20},{20,16},{24,28},{28,24},{1,5},{5... | collective-permute-start | bytes 221192 | tf_op jit(solution)/shard_map/ppermute | solution.py:304
  9.1 1.6 %collective-permute-start.1 = (f32[72,256]{1,0:T(8,128)S(1)}, f32[72,256]{1,0:T(8,128)S(1)}, u32[]{:S(2)}, u32[]{:S(2)}) collective-permute-start(f32[72,256]{1,0:T(8,128)S(1)} %shard_map.136.refs_0_), channel_id=1, source_target_pairs={{0,8},{4,12},{8,0},{12,4},{16,24},{20,28},{24,16},{28,20},{1,9},{5... | collective-permute-start | bytes 221192 | tf_op jit(solution)/shard_map/ppermute | solution.py:304
  10.7 0.8 %collective-permute-done.refs_1_ = f32[72,256]{1,0:T(8,128)S(1)} collective-permute-done((f32[72,256]{1,0:T(8,128)S(1)}, f32[72,256]{1,0:T(8,128)S(1)}, u32[]{:S(2)}, u32[]{:S(2)}) %collective-permute-start) | collective-permute-done | bytes 73760 | tf_op jit(solution)/shard_map/ppermute | solution.py:304
  11.5 2.7 %collective-permute-done.1.refs_2_ = f32[72,256]{1,0:T(8,128)S(1)} collective-permute-done((f32[72,256]{1,0:T(8,128)S(1)}, f32[72,256]{1,0:T(8,128)S(1)}, u32[]{:S(2)}, u32[]{:S(2)}) %collective-permute-start.1) | collective-permute-done | bytes 73760 | tf_op jit(solution)/shard_map/ppermute | solution.py:304
  14.1 1.8 %collective-permute-done.2.refs_3_ = f32[72,256]{1,0:T(8,128)S(1)} collective-permute-done((f32[72,256]{1,0:T(8,128)S(1)}, f32[72,256]{1,0:T(8,128)S(1)}, u32[]{:S(2)}, u32[]{:S(2)}) %collective-permute-start.2) | collective-permute-done | bytes 73760 | tf_op jit(solution)/shard_map/ppermute | solution.py:304
  16.0 0.3 shard_map.137.one_ref
  16.3 2.7 %collective-permute-start.3 = (f32[72,256]{1,0:T(8,128)S(1)}, f32[72,256]{1,0:T(8,128)S(1)}, u32[]{:S(2)}, u32[]{:S(2)}) collective-permute-start(f32[72,256]{1,0:T(8,128)S(1)} %shard_map.137.one_ref), channel_id=1, source_target_pairs={{0,16},{4,20},{8,24},{12,28},{16,0},{20,4},{24,8},{28,12},{1,17},{... | collective-permute-start | bytes 221192 | tf_op jit(solution)/shard_map/ppermute | solution.py:304
  19.0 3.3 %collective-permute-done.3.two_ref = f32[72,256]{1,0:T(8,128)S(1)} collective-permute-done((f32[72,256]{1,0:T(8,128)S(1)}, f32[72,256]{1,0:T(8,128)S(1)}, u32[]{:S(2)}, u32[]{:S(2)}) %collective-permute-start.3) | collective-permute-done | bytes 73760 | tf_op jit(solution)/shard_map/ppermute | solution.py:304
  22.3 0.6 shard_map.138
  22.9 0.1 collective-permute-start.4
  23.0 1.3 %collective-permute-done.4 = f32[32,1024]{1,0:T(8,128)S(1)} collective-permute-done((f32[32,1024]{1,0:T(8,128)S(1)}, f32[32,1024]{1,0:T(8,128)S(1)}, u32[]{:S(2)}, u32[]{:S(2)}) %collective-permute-start.4) | collective-permute-done | bytes 131104 | tf_op jit(solution)/shard_map/ppermute | solution.py:304
  24.4 1.6 %collective-permute-start.5 = (f32[32,1024]{1,0:T(8,128)S(1)}, f32[32,1024]{1,0:T(8,128)S(1)}, u32[]{:S(2)}, u32[]{:S(2)}) collective-permute-start(f32[32,1024]{1,0:T(8,128)S(1)} %add.31), channel_id=1, source_target_pairs={{0,2},{1,3},{2,0},{3,1},{4,6},{5,7},{6,4},{7,5},{8,10},{9,11},{10,... | collective-permute-start | bytes 393224 | tf_op jit(solution)/shard_map/ppermute | solution.py:304
  25.9 4.0 %collective-permute-done.5 = f32[32,1024]{1,0:T(8,128)S(1)} collective-permute-done((f32[32,1024]{1,0:T(8,128)S(1)}, f32[32,1024]{1,0:T(8,128)S(1)}, u32[]{:S(2)}, u32[]{:S(2)}) %collective-permute-start.5) | collective-permute-done | bytes 131104 | tf_op jit(solution)/shard_map/ppermute | solution.py:304
  30.0 0.1 collective-permute-start.6
  30.1 1.3 %collective-permute-done.6.back_ref = f32[32,1024]{1,0:T(8,128)S(1)} collective-permute-done((f32[32,1024]{1,0:T(8,128)S(1)}, f32[32,1024]{1,0:T(8,128)S(1)}, u32[]{:S(2)}, u32[]{:S(2)}) %collective-permute-start.6) | collective-permute-done | bytes 131104 | tf_op jit(solution)/shard_map/ppermute | solution.py:304
  31.4 4.6 %shard_map.139 = (f32[64,1024]{1,0:T(8,128)S(1)}, f32[32,1024]{1,0:T(8,128)S(1)}, f32[32,1024]{1,0:T(8,128)S(1)}) custom-call(f32[32,1024]{1,0:T(8,128)S(1)} %add.32.half_ref, f32[32,1024]{1,0:T(8,128)S(1)} %collective-permute-done.6.back_ref, bf16[64,1024]{1,0:T(8,128)(2,1)S(1)} %bitcast.7, f32[1,1024]{1,0:T(1,128)S(1)} %bitcast.9, ...), custom_call_target="tpu_custom_call" | custom-call | tf_op jit(solution)/shard_map/pallas_call | solution.py:415
  36.0 0.2 collective-permute-start.7
  36.2 1.2 %collective-permute-done.7 = f32[32,1024]{1,0:T(8,128)S(1)} collective-permute-done((f32[32,1024]{1,0:T(8,128)S(1)}, f32[32,1024]{1,0:T(8,128)S(1)}, u32[]{:S(2)}, u32[]{:S(2)}) %collective-permute-start.7) | collective-permute-done | bytes 131104 | tf_op jit(solution)/shard_map/ppermute | solution.py:304
  37.4 0.7 %collective-permute-start.9 = (f32[32,1024]{1,0:T(8,128)S(1)}, f32[32,1024]{1,0:T(8,128)S(1)}, u32[]{:S(2)}, u32[]{:S(2)}) collective-permute-start(f32[32,1024]{1,0:T(8,128)S(1)} %add.34), channel_id=1, source_target_pairs={{0,4},{4,0},{8,12},{12,8},{16,20},{20,16},{24,28},{28,24},{1,5},{5... | collective-permute-start | bytes 393224 | tf_op jit(solution)/shard_map/ppermute | solution.py:304
  38.2 2.3 %collective-permute-start.10 = (f32[32,1024]{1,0:T(8,128)S(1)}, f32[32,1024]{1,0:T(8,128)S(1)}, u32[]{:S(2)}, u32[]{:S(2)}) collective-permute-start(f32[32,1024]{1,0:T(8,128)S(1)} %add.34), channel_id=1, source_target_pairs={{0,6},{1,7},{2,4},{3,5},{4,2},{5,3},{6,0},{7,1},{8,14},{9,15},{10,... | collective-permute-start | bytes 393224 | tf_op jit(solution)/shard_map/ppermute | solution.py:308
  40.5 0.5 collective-permute-start.8
  41.0 2.9 %collective-permute-done.9 = f32[32,1024]{1,0:T(8,128)S(1)} collective-permute-done((f32[32,1024]{1,0:T(8,128)S(1)}, f32[32,1024]{1,0:T(8,128)S(1)}, u32[]{:S(2)}, u32[]{:S(2)}) %collective-permute-start.9) | collective-permute-done | bytes 131104 | tf_op jit(solution)/shard_map/ppermute | solution.py:304
  43.9 3.1 %collective-permute-done.10 = f32[32,1024]{1,0:T(8,128)S(1)} collective-permute-done((f32[32,1024]{1,0:T(8,128)S(1)}, f32[32,1024]{1,0:T(8,128)S(1)}, u32[]{:S(2)}, u32[]{:S(2)}) %collective-permute-start.10) | collective-permute-done | bytes 131104 | tf_op jit(solution)/shard_map/ppermute | solution.py:308
  46.9 1.4 %collective-permute-done.8 = f32[32,1024]{1,0:T(8,128)S(1)} collective-permute-done((f32[32,1024]{1,0:T(8,128)S(1)}, f32[32,1024]{1,0:T(8,128)S(1)}, u32[]{:S(2)}, u32[]{:S(2)}) %collective-permute-start.8) | collective-permute-done | bytes 131104 | tf_op jit(solution)/shard_map/ppermute | solution.py:304
  48.3 0.1 collective-permute-start.11
  48.4 5.0 %collective-permute-done.11 = f32[32,1024]{1,0:T(8,128)S(1)} collective-permute-done((f32[32,1024]{1,0:T(8,128)S(1)}, f32[32,1024]{1,0:T(8,128)S(1)}, u32[]{:S(2)}, u32[]{:S(2)}) %collective-permute-start.11) | collective-permute-done | bytes 131104 | tf_op jit(solution)/shard_map/ppermute | solution.py:304
  53.4 2.0 %collective-permute-start.12 = (f32[32,1024]{1,0:T(8,128)S(1)}, f32[32,1024]{1,0:T(8,128)S(1)}, u32[]{:S(2)}, u32[]{:S(2)}) collective-permute-start(f32[32,1024]{1,0:T(8,128)S(1)} %add.38), channel_id=1, source_target_pairs={{0,16},{4,20},{8,24},{12,28},{16,0},{20,4},{24,8},{28,12},{1,17},{... | collective-permute-start | bytes 393224 | tf_op jit(solution)/shard_map/ppermute | solution.py:304
  55.4 4.9 %collective-permute-done.12 = f32[32,1024]{1,0:T(8,128)S(1)} collective-permute-done((f32[32,1024]{1,0:T(8,128)S(1)}, f32[32,1024]{1,0:T(8,128)S(1)}, u32[]{:S(2)}, u32[]{:S(2)}) %collective-permute-start.12) | collective-permute-done | bytes 131104 | tf_op jit(solution)/shard_map/ppermute | solution.py:304
  60.4 0.1 collective-permute-start.13
  60.4 1.3 %collective-permute-done.13 = f32[32,1024]{1,0:T(8,128)S(1)} collective-permute-done((f32[32,1024]{1,0:T(8,128)S(1)}, f32[32,1024]{1,0:T(8,128)S(1)}, u32[]{:S(2)}, u32[]{:S(2)}) %collective-permute-start.13) | collective-permute-done | bytes 131104 | tf_op jit(solution)/shard_map/ppermute | solution.py:304
  61.8 0.7 %fusion = bf16[64,1024]{1,0:T(8,128)(2,1)} fusion(f32[64,1024]{1,0:T(8,128)S(1)} %get-tuple-element.16, f32[32,1024]{1,0:T(8,128)S(1)} %get-tuple-element.20, f32[32,1024]{1,0:T(8,128)S(1)} %get-tuple-element.19), kind=kLoop, calls=%fused_computation.1 | loop fusion | flops 196608 | bytes 655360 | tf_op jit(solution)/shard_map/convert_element_type | solution.py:428
  (20 shorter events, 0.2 us)
Async XLA Ops:
  0.0 22.3 %copy-start.1 = (bf16[256,1024]{1,0:T(8,128)(2,1)S(1)}, bf16[256,1024]{1,0:T(8,128)(2,1)}, u32[]{:S(2)}) copy-start(bf16[256,1024]{1,0:T(8,128)(2,1)} %w_ref.1) | copy-start | bytes 1572868
  0.0 31.4 %copy-start = (bf16[2,1408,1024]{2,1,0:T(8,128)(2,1)S(1)}, bf16[2,1408,1024]{2,1,0:T(8,128)(2,1)}, u32[]{:S(2)}) copy-start(bf16[2,1408,1024]{2,1,0:T(8,128)(2,1)} %up_ref) | copy-start | bytes 17301508
  0.0 31.4 %copy-start.2 = (bf16[4,16,1024]{2,1,0:T(8,128)(2,1)S(1)}, bf16[4,16,1024]{2,1,0:T(8,128)(2,1)}, u32[]{:S(2)}) copy-start(bf16[4,16,1024]{2,1,0:T(8,128)(2,1)} %param.14) | copy-start | bytes 393220
  0.0 31.4 %copy-start.3 = (bf16[1024,16]{0,1:T(8,128)(2,1)S(1)}, bf16[1024,16]{0,1:T(8,128)(2,1)}, u32[]{:S(2)}) copy-start(bf16[1024,16]{0,1:T(8,128)(2,1)} %param.24) | copy-start | bytes 98308
  0.0 31.4 %copy-start.4 = (f32[1024]{0:T(1024)S(1)}, f32[1024]{0:T(1024)}, u32[]{:S(2)}) copy-start(f32[1024]{0:T(1024)} %param.21) | copy-start | bytes 12292
  0.0 31.4 %copy-start.5 = (s32[4,16,2]{1,2,0:T(2,128)S(1)}, s32[4,16,2]{1,2,0:T(2,128)}, u32[]{:S(2)}) copy-start(s32[4,16,2]{1,2,0:T(2,128)} %param.25) | copy-start | bytes 1540
  6.1 5.4 %collective-permute-start = (f32[72,256]{1,0:T(8,128)S(1)}, f32[72,256]{1,0:T(8,128)S(1)}, u32[]{:S(2)}, u32[]{:S(2)}) collective-permute-start(f32[72,256]{1,0:T(8,128)S(1)} %shard_map.136.refs_0_), channel_id=1, source_target_pairs={{0,4},{4,0},{8,12},{12,8},{16,20},{20,16},{24,28},{28,24},{1,5},{5... | collective-permute-start | bytes 221192 | tf_op jit(solution)/shard_map/ppermute | solution.py:304
  9.1 5.0 %collective-permute-start.1 = (f32[72,256]{1,0:T(8,128)S(1)}, f32[72,256]{1,0:T(8,128)S(1)}, u32[]{:S(2)}, u32[]{:S(2)}) collective-permute-start(f32[72,256]{1,0:T(8,128)S(1)} %shard_map.136.refs_0_), channel_id=1, source_target_pairs={{0,8},{4,12},{8,0},{12,4},{16,24},{20,28},{24,16},{28,20},{1,9},{5... | collective-permute-start | bytes 221192 | tf_op jit(solution)/shard_map/ppermute | solution.py:304
  10.7 5.3 %collective-permute-start.2 = (f32[72,256]{1,0:T(8,128)S(1)}, f32[72,256]{1,0:T(8,128)S(1)}, u32[]{:S(2)}, u32[]{:S(2)}) collective-permute-start(f32[72,256]{1,0:T(8,128)S(1)} %shard_map.136.refs_0_), channel_id=1, source_target_pairs={{0,12},{4,8},{8,4},{12,0},{16,28},{20,24},{24,20},{28,16},{1,13},{... | collective-permute-start | bytes 221192 | tf_op jit(solution)/shard_map/ppermute | solution.py:304
  16.3 6.0 %collective-permute-start.3 = (f32[72,256]{1,0:T(8,128)S(1)}, f32[72,256]{1,0:T(8,128)S(1)}, u32[]{:S(2)}, u32[]{:S(2)}) collective-permute-start(f32[72,256]{1,0:T(8,128)S(1)} %shard_map.137.one_ref), channel_id=1, source_target_pairs={{0,16},{4,20},{8,24},{12,28},{16,0},{20,4},{24,8},{28,12},{1,17},{... | collective-permute-start | bytes 221192 | tf_op jit(solution)/shard_map/ppermute | solution.py:304
  22.9 1.4 %collective-permute-start.4 = (f32[32,1024]{1,0:T(8,128)S(1)}, f32[32,1024]{1,0:T(8,128)S(1)}, u32[]{:S(2)}, u32[]{:S(2)}) collective-permute-start(f32[32,1024]{1,0:T(8,128)S(1)} %get-tuple-element.14), channel_id=1, source_target_pairs={{0,1},{1,0},{2,3},{3,2},{4,5},{5,4},{6,7},{7,6},{8,9},{9,8},{10,11... | collective-permute-start | bytes 393224 | tf_op jit(solution)/shard_map/ppermute | solution.py:304
  24.4 5.6 %collective-permute-start.5 = (f32[32,1024]{1,0:T(8,128)S(1)}, f32[32,1024]{1,0:T(8,128)S(1)}, u32[]{:S(2)}, u32[]{:S(2)}) collective-permute-start(f32[32,1024]{1,0:T(8,128)S(1)} %add.31), channel_id=1, source_target_pairs={{0,2},{1,3},{2,0},{3,1},{4,6},{5,7},{6,4},{7,5},{8,10},{9,11},{10,... | collective-permute-start | bytes 393224 | tf_op jit(solution)/shard_map/ppermute | solution.py:304
  30.0 1.4 %collective-permute-start.6 = (f32[32,1024]{1,0:T(8,128)S(1)}, f32[32,1024]{1,0:T(8,128)S(1)}, u32[]{:S(2)}, u32[]{:S(2)}) collective-permute-start(f32[32,1024]{1,0:T(8,128)S(1)} %add.32.half_ref), channel_id=1, source_target_pairs={{0,1},{1,0},{2,3},{3,2},{4,5},{5,4},{6,7},{7,6},{8,9},{9,8},{10,11... | collective-permute-start | bytes 393224 | tf_op jit(solution)/shard_map/ppermute | solution.py:304
  36.0 1.4 %collective-permute-start.7 = (f32[32,1024]{1,0:T(8,128)S(1)}, f32[32,1024]{1,0:T(8,128)S(1)}, u32[]{:S(2)}, u32[]{:S(2)}) collective-permute-start(f32[32,1024]{1,0:T(8,128)S(1)} %get-tuple-element.18), channel_id=1, source_target_pairs={{0,1},{1,0},{2,3},{3,2},{4,5},{5,4},{6,7},{7,6},{8,9},{9,8},{10,11... | collective-permute-start | bytes 393224 | tf_op jit(solution)/shard_map/ppermute | solution.py:304
  37.4 6.4 %collective-permute-start.9 = (f32[32,1024]{1,0:T(8,128)S(1)}, f32[32,1024]{1,0:T(8,128)S(1)}, u32[]{:S(2)}, u32[]{:S(2)}) collective-permute-start(f32[32,1024]{1,0:T(8,128)S(1)} %add.34), channel_id=1, source_target_pairs={{0,4},{4,0},{8,12},{12,8},{16,20},{20,16},{24,28},{28,24},{1,5},{5... | collective-permute-start | bytes 393224 | tf_op jit(solution)/shard_map/ppermute | solution.py:304
  38.2 8.8 %collective-permute-start.10 = (f32[32,1024]{1,0:T(8,128)S(1)}, f32[32,1024]{1,0:T(8,128)S(1)}, u32[]{:S(2)}, u32[]{:S(2)}) collective-permute-start(f32[32,1024]{1,0:T(8,128)S(1)} %add.34), channel_id=1, source_target_pairs={{0,6},{1,7},{2,4},{3,5},{4,2},{5,3},{6,0},{7,1},{8,14},{9,15},{10,... | collective-permute-start | bytes 393224 | tf_op jit(solution)/shard_map/ppermute | solution.py:308
  40.5 7.8 %collective-permute-start.8 = (f32[32,1024]{1,0:T(8,128)S(1)}, f32[32,1024]{1,0:T(8,128)S(1)}, u32[]{:S(2)}, u32[]{:S(2)}) collective-permute-start(f32[32,1024]{1,0:T(8,128)S(1)} %add.34), channel_id=1, source_target_pairs={{0,2},{1,3},{2,0},{3,1},{4,6},{5,7},{6,4},{7,5},{8,10},{9,11},{10,... | collective-permute-start | bytes 393224 | tf_op jit(solution)/shard_map/ppermute | solution.py:304
  48.3 5.0 %collective-permute-start.11 = (f32[32,1024]{1,0:T(8,128)S(1)}, f32[32,1024]{1,0:T(8,128)S(1)}, u32[]{:S(2)}, u32[]{:S(2)}) collective-permute-start(f32[32,1024]{1,0:T(8,128)S(1)} %add_add_fusion), channel_id=1, source_target_pairs={{0,8},{4,12},{8,0},{12,4},{16,24},{20,28},{24,16},{28,20},{1,9},{5... | collective-permute-start | bytes 393224 | tf_op jit(solution)/shard_map/ppermute | solution.py:304
  53.4 7.0 %collective-permute-start.12 = (f32[32,1024]{1,0:T(8,128)S(1)}, f32[32,1024]{1,0:T(8,128)S(1)}, u32[]{:S(2)}, u32[]{:S(2)}) collective-permute-start(f32[32,1024]{1,0:T(8,128)S(1)} %add.38), channel_id=1, source_target_pairs={{0,16},{4,20},{8,24},{12,28},{16,0},{20,4},{24,8},{28,12},{1,17},{... | collective-permute-start | bytes 393224 | tf_op jit(solution)/shard_map/ppermute | solution.py:304
  60.4 1.4 %collective-permute-start.13 = (f32[32,1024]{1,0:T(8,128)S(1)}, f32[32,1024]{1,0:T(8,128)S(1)}, u32[]{:S(2)}, u32[]{:S(2)}) collective-permute-start(f32[32,1024]{1,0:T(8,128)S(1)} %add.39), channel_id=1, source_target_pairs={{0,1},{1,0},{2,3},{3,2},{4,5},{5,4},{6,7},{7,6},{8,9},{9,8},{10,11... | collective-permute-start | bytes 393224 | tf_op jit(solution)/shard_map/ppermute | solution.py:304

commit v6 on v5

--- a/solution.py
+++ b/solution.py
@@ -68,9 +68,11 @@
     )
     small_copies = [pltpu.make_async_copy(src, dst, small_sem.at[i]) for i, (src, dst) in enumerate(small)]
     w_copies = [pltpu.make_async_copy(w_hbm.at[k], w_buf.at[k], w_sem.at[k]) for k in range(3)]
-    k_copies = [pltpu.make_async_copy(k_hbm.at[r], k_buf.at[r], k_sem.at[r]) for r in range(requests)]
-    v_copies = [pltpu.make_async_copy(v_hbm.at[r], v_buf.at[r], v_sem.at[r]) for r in range(requests)]
-    for copy in small_copies + w_copies + k_copies + v_copies:
+    per_copy = requests // k_sem.shape[0]
+    blocks = [pl.ds(i * per_copy, per_copy) for i in range(k_sem.shape[0])]
+    k_copies = [pltpu.make_async_copy(k_hbm.at[b], k_buf.at[b], k_sem.at[i]) for i, b in enumerate(blocks)]
+    v_copies = [pltpu.make_async_copy(v_hbm.at[b], v_buf.at[b], v_sem.at[i]) for i, b in enumerate(blocks)]
+    for copy in small_copies + w_copies:
         copy.start()
 
     seq = lax.axis_index("seq")
@@ -115,7 +117,11 @@
             bias_buf[place] = jnp.where(distance > group_step, bias, NEG)
         return carry
 
+    for copy in k_copies:
+        copy.start()
     lax.fori_loop(0, requests // per_trip, fill_bias, 0)
+    for copy in v_copies:
+        copy.start()
 
     for copy in small_copies[3:]:
         copy.wait()
@@ -155,28 +161,27 @@
     score_buf[...] = dot(fresh_weights.astype(BF16), fresh_values)
     for copy in v_copies:
         copy.wait()
-    for r in range(requests):
-        at = slice(r * group, (r + 1) * group)
-        score_buf[at, :] += dot(weight_buf[at, :], v_buf[r])
-
-    sums = jnp.where(own_head, score_buf[...], 0.0)
+
     lane = iota((1, LANES), 1)
     stats = jnp.where(lane == row_head, top, jnp.where(lane == heads + row_head, total, 0.0))
+    group_own = own_head[:group]
     first = iota((8, 1), 0) < steps
 
-    def fold(values):
-        pairs = []
-        for pair in range(requests // 2):
-            folded = []
-            for r in (2 * pair, 2 * pair + 1):
-                part = values[r * group : r * group + 8] + values[r * group + 8 : r * group + 16]
-                folded.append(part + pltpu.roll(part, steps, 0))
-            pairs.append(jnp.where(first, folded[0], folded[1]))
-        return jnp.concatenate(pairs, axis=0)
-
-    out_ref[:tokens, :] = fold(sums)
+    def folded(part):
+        half = part[:8] + part[8:]
+        return half + pltpu.roll(half, steps, 0)
+
+    stat_pairs = []
+    for pair in range(requests // 2):
+        sums, stat_parts = [], []
+        for r in (2 * pair, 2 * pair + 1):
+            at = slice(r * group, (r + 1) * group)
+            sums.append(folded(jnp.where(group_own, dot(weight_buf[at, :], v_buf[r]) + score_buf[at, :], 0.0)))
+            stat_parts.append(folded(stats[at]))
+        out_ref[8 * pair : 8 * pair + 8, :] = jnp.where(first, sums[0], sums[1])
+        stat_pairs.append(jnp.where(first, stat_parts[0], stat_parts[1]))
     out_ref[tokens:, :] = jnp.zeros((2 * heads, features), F32)
-    out_ref[tokens:, :LANES] = turned(fold(stats))[: 2 * heads]
+    out_ref[tokens:, :LANES] = turned(jnp.concatenate(stat_pairs, axis=0))[: 2 * heads]
 
 
 def turned(value):
@@ -246,14 +251,12 @@
 
 def expert_kernel(
     half_ref, back_ref, tokens_ref, gain_ref, router_ref, choice_ref, up_ref, down_hbm,
-    mid_ref, keep_ref, give_ref, down_ref, down_sem,
+    mid_ref, one_ref, two_ref, three_ref, four_ref, down_ref, down_sem,
 ):
+    sum_refs = (one_ref, two_ref, three_ref, four_ref)
+    down_copy = pltpu.make_async_copy(down_hbm, down_ref, down_sem)
+    down_copy.start()
     hidden_local = down_ref.shape[0]
-    chunks = chunks_of(hidden_local, 256)
-    copies = []
-    for i, (at, size) in enumerate(chunks):
-        copies.append(pltpu.make_async_copy(down_hbm.at[pl.ds(at, size)], down_ref.at[pl.ds(at, size)], down_sem.at[i]))
-        copies[-1].start()
     half = half_ref.shape[0]
     steps, _, requests = choice_ref.shape
     low = lax.axis_index("tp") % 2 == 0
@@ -277,17 +280,19 @@
     device = lax.axis_index("seq") * lax.axis_size("tp") + lax.axis_index("tp")
     total = jnp.zeros(mid_ref.shape, F32)
     hiddens = []
+    chunks = chunks_of(hidden_local, 256)
     for at, size in chunks:
         column_expert = (device * hidden_local + at + iota((1, size), 1)) // FF
         coef = jnp.where(column_expert == choices[0], first, jnp.where(column_expert == choices[1], second, 0.0))
         gate = dot_nt(moe_in, up_ref[0, at : at + size, :])
         up = dot_nt(moe_in, up_ref[1, at : at + size, :])
         hiddens.append((jax.nn.gelu(gate, approximate=True) * up * coef).astype(BF16))
-    for copy in copies:
-        copy.wait()
+    down_copy.wait()
     for (at, size), hidden in zip(chunks, hiddens):
         total = total + dot(hidden, down_ref[at : at + size, :])
-    store_halves(total, 1, keep_ref, give_ref)
+    columns = total.shape[1] // 2
+    for i in range(2):
+        store_halves(total[:, i * columns : (i + 1) * columns], 1, sum_refs[i], sum_refs[2 + i])
 
 
 def device_bits(axis):
@@ -296,36 +301,23 @@
     return [(axis, 1 << k) for k in range(size.bit_length() - 1)]
 
 
-def swap(value, *bits):
-    sizes = {axis: lax.axis_size(axis) for axis in ("seq", "tp") if axis in dict(bits)}
-    flips = {axis: sum(bit for other, bit in bits if other == axis) for axis in sizes}
-    if len(sizes) == 1:
-        (axis,) = sizes
-        return lax.ppermute(value, axis, [(i, i ^ flips[axis]) for i in range(sizes[axis])])
-    (one, two) = sizes
-    flat = [i * sizes[two] + j for i in range(sizes[one]) for j in range(sizes[two])]
-    there = [(i ^ flips[one]) * sizes[two] + (j ^ flips[two]) for i in range(sizes[one]) for j in range(sizes[two])]
-    return lax.ppermute(value, (one, two), list(zip(flat, there)))
-
-
-def gathered(value, bits):
-    parts = [value]
+def swap(value, bit):
+    axis, flip = bit
+    return lax.ppermute(value, axis, [(i, i ^ flip) for i in range(lax.axis_size(axis))])
+
+
+def reduce_halves(keep, give, split, bits):
+    half = keep + swap(give, split)
     for bit in bits:
-        parts.append(swap(value, bit))
-    if len(bits) == 2:
-        parts.append(swap(value, *bits))
-    return parts
-
-
-def stages(bits):
-    return [bits[:2]] + [[bit] for bit in bits[2:]] if len(bits) > 2 else [[bit] for bit in bits]
-
-
-def reduce_halves(keep, give, split, groups):
-    half = keep + swap(give, split)
-    for bits in groups:
-        half = tree(jnp.add, gathered(half, bits))
+        half = half + swap(half, bit)
     return half, swap(half, split)
+
+
+def reduce_columns(keeps, gives, split, orders):
+    halves = [keep + swap(give, split) for keep, give in zip(keeps, gives)]
+    for bits in zip(*orders):
+        halves = [half + swap(half, bit) for half, bit in zip(halves, bits)]
+    return halves, [swap(half, split) for half in halves]
 
 
 def in_hbm(value):
@@ -393,37 +385,33 @@
             pltpu.VMEM((buckets, steps * heads, LANES), F32),
             dma((5,)),
             dma((3,)),
-            dma((requests,)),
-            dma((requests,)),
+            dma((requests // 4,)),
+            dma((requests // 4,)),
         ],
     )(*map(in_hbm, (cache_len, flat_in, attn_gain, bucket_table, rel_bias.T, w_qkv, key_cache, value_cache)))
 
-    packed, w_gate_up = lax.optimization_barrier((packed, w_gate_up))
+    packed, w_gate_up, w_down = lax.optimization_barrier((packed, w_gate_up, w_down))
     seq_bits, tp_bits = device_bits("seq"), device_bits("tp")
-    seq_stages = stages(seq_bits)
-    for bits in seq_stages[:-1]:
-        parts = gathered(packed, bits)
-        (packed,) = call(functools.partial(merge_kernel, tokens), [(packed_shape, F32)], [VMEM] * len(parts), 2)(*parts)
+    for bit in seq_bits[:-1]:
+        (packed,) = call(functools.partial(merge_kernel, tokens), [(packed_shape, F32)], [VMEM] * 2, 2)(
+            packed, swap(packed, bit)
+        )
     half_shape = ((half, width), F32)
     keep, give = call(
         functools.partial(project_kernel, steps, requests), [half_shape, half_shape], [VMEM] * 3, 4
-    )(packed, swap(packed, *seq_stages[-1]), w_out)
-
-    mine, other = reduce_halves(keep, give, tp_bits[0], [[bit] for bit in tp_bits[1:]])
-
-    n_chunks = len(chunks_of(hidden_local, 256))
-    mid, keep, give = call(
-        expert_kernel,
-        [((tokens, width), F32), half_shape, half_shape],
-        [VMEM] * 7 + [HBM],
-        12,
-        [pltpu.VMEM(w_down.shape, BF16), dma((n_chunks,))],
-    )(
+    )(packed, swap(packed, seq_bits[-1]), w_out)
+
+    mine, other = reduce_halves(keep, give, tp_bits[0], tp_bits[1:])
+
+    column_shape = ((half, width // 2), F32)
+    mid, *sums = call(expert_kernel, [((tokens, width), F32)] + [column_shape] * 4, [VMEM] * 7 + [HBM], 12, [pltpu.VMEM(w_down.shape, BF16), dma(())])(
         mine, other, flat_in, moe_gain[None], router.T, expert_choice.transpose(0, 2, 1), w_gate_up, in_hbm(w_down)
     )
-
-    mine, other = reduce_halves(keep, give, tp_bits[0], stages(tp_bits[1:] + seq_bits))
+    bits = tp_bits[1:] + seq_bits
+    swapped = [bits[i ^ 1] if i ^ 1 < len(bits) else bits[i] for i in range(len(bits))]
+    mine, other = reduce_columns(sums[:2], sums[2:], tp_bits[0], (bits, swapped))
     low = lax.axis_index("tp") % 2 == 0
+    mine, other = jnp.concatenate(mine, axis=1), jnp.concatenate(other, axis=1)
     mixture = jnp.concatenate([jnp.where(low, mine, other), jnp.where(low, other, mine)])
     return (mid + mixture).astype(BF16).reshape(steps, requests, width)
 

time: 62.6 us -> 60 us (0.958)
  waiting for transfers between devices: 35 us -> 22.3 us
  starting transfers between devices: 14.9 us -> 25.9 us
  Pallas kernels: 11.6 us -> 10.5 us
    ppermute x14 -> x18, waiting for transfers between devices: 35 us -> 22.3 us  [swap(): lax.ppermute(value, axis, [(i, i ^ flip) for i in range(lax.axis_size(axi...]
    ppermute x14 -> x18, starting transfers between devices: 14.9 us -> 25.9 us  [swap(): lax.ppermute(value, axis, [(i, i ^ flip) for i in range(lax.axis_size(axi...]
    pallas_call x1, Pallas kernels: 6.08 us -> 4.84 us  [on_device(): call(functools.partial(attend_kernel, steps, requests, heads), [(packed_s...]
  transfers between devices with their start and end apart: 14 -> 18, of which waited for: 14 -> 15; matrix products, arithmetic and copies ran while one was open for 0% -> 0% of each run, Pallas kernels for 0% -> 0%
where the time goes in v6:
time: 60 us; the launch traced here: 59.8 us
  starting transfers between devices  25.9 us (43%)
  waiting for transfers between devices  22.3 us (37%)
  Pallas kernels  10.5 us (18%)
  other arithmetic  0.86 us (1%)
    ppermute x18, starting transfers between devices, swap(): lax.ppermute(value, axis, [(i, i ^ flip) for i in range(lax.axis_size(axi...  25.9 us
    ppermute x18, waiting for transfers between devices, swap(): lax.ppermute(value, axis, [(i, i ^ flip) for i in range(lax.axis_size(axi...  22.3 us
    pallas_call x1, Pallas kernels, on_device(): call(functools.partial(attend_kernel, steps, requests, heads), [(packed_s...  4.84 us
    pallas_call x1, Pallas kernels, on_device(): call(expert_kernel, [((tokens, width), F32)] + [column_shape] * 4, [VMEM]...  4.59 us
  transfers between devices with their start and end apart: 18, of which 15 were waited for; matrix products, arithmetic and copies ran while one was open for 0% of the time, Pallas kernels for 0%

profile of v6, /device:TPU:0, one launch (start us, length us, event | category | flops | bytes accessed | tf_op | source)
XLA Modules:
  0.0 59.8 jit_solution(7324984724644118796)
XLA Ops:
  0.0 4.8 %shard_map.136.refs_0_ = f32[72,256]{1,0:T(8,128)S(1)} custom-call(s32[16]{0:T(128)} %len_hbm.1, bf16[64,1024]{1,0:T(8,128)(2,1)} %bitcast.6, f32[1024]{0:T(1024)} %gain_hbm.1, s32[2052]{0:T(1024)} %table_hbm.1, f32[4,32]{1,0:T(4,128)} %bitcast.11, bf16[3,1024,256]{2,1,0:T(8,128)(2,1)} %w_hbm.1, bf16[16,256,256]{2,1,0:T(8,128)(2,1)} %k_hbm.1, ...), custom_call_target="tpu_custom_call" | custom-call | tf_op jit(solution)/shard_map/pallas_call | solution.py:367
  4.9 3.0 %collective-permute-start = (f32[72,256]{1,0:T(8,128)S(1)}, f32[72,256]{1,0:T(8,128)S(1)}, u32[]{:S(2)}, u32[]{:S(2)}) collective-permute-start(f32[72,256]{1,0:T(8,128)S(1)} %shard_map.136.refs_0_), channel_id=1, source_target_pairs={{0,4},{4,0},{8,12},{12,8},{16,20},{20,16},{24,28},{28,24},{1,5},{5... | collective-permute-start | bytes 221192 | tf_op jit(solution)/shard_map/ppermute | solution.py:306
  7.9 2.3 %collective-permute-done.refs_1_ = f32[72,256]{1,0:T(8,128)S(1)} collective-permute-done((f32[72,256]{1,0:T(8,128)S(1)}, f32[72,256]{1,0:T(8,128)S(1)}, u32[]{:S(2)}, u32[]{:S(2)}) %collective-permute-start) | collective-permute-done | bytes 73760 | tf_op jit(solution)/shard_map/ppermute | solution.py:306
  10.2 0.3 shard_map.137.refs_0_
  10.5 2.2 %collective-permute-start.1 = (f32[72,256]{1,0:T(8,128)S(1)}, f32[72,256]{1,0:T(8,128)S(1)}, u32[]{:S(2)}, u32[]{:S(2)}) collective-permute-start(f32[72,256]{1,0:T(8,128)S(1)} %shard_map.137.refs_0_), channel_id=1, source_target_pairs={{0,8},{4,12},{8,0},{12,4},{16,24},{20,28},{24,16},{28,20},{1,9},{5... | collective-permute-start | bytes 221192 | tf_op jit(solution)/shard_map/ppermute | solution.py:306
  12.7 2.3 %collective-permute-done.1.refs_1_ = f32[72,256]{1,0:T(8,128)S(1)} collective-permute-done((f32[72,256]{1,0:T(8,128)S(1)}, f32[72,256]{1,0:T(8,128)S(1)}, u32[]{:S(2)}, u32[]{:S(2)}) %collective-permute-start.1) | collective-permute-done | bytes 73760 | tf_op jit(solution)/shard_map/ppermute | solution.py:306
  15.0 0.3 shard_map.138.one_ref
  15.2 3.1 %collective-permute-start.2 = (f32[72,256]{1,0:T(8,128)S(1)}, f32[72,256]{1,0:T(8,128)S(1)}, u32[]{:S(2)}, u32[]{:S(2)}) collective-permute-start(f32[72,256]{1,0:T(8,128)S(1)} %shard_map.138.one_ref), channel_id=1, source_target_pairs={{0,16},{4,20},{8,24},{12,28},{16,0},{20,4},{24,8},{28,12},{1,17},{... | collective-permute-start | bytes 221192 | tf_op jit(solution)/shard_map/ppermute | solution.py:306
  18.3 2.3 %collective-permute-done.2.two_ref = f32[72,256]{1,0:T(8,128)S(1)} collective-permute-done((f32[72,256]{1,0:T(8,128)S(1)}, f32[72,256]{1,0:T(8,128)S(1)}, u32[]{:S(2)}, u32[]{:S(2)}) %collective-permute-start.2) | collective-permute-done | bytes 73760 | tf_op jit(solution)/shard_map/ppermute | solution.py:306
  20.7 0.6 %shard_map.139 = (f32[32,1024]{1,0:T(8,128)S(1)}, f32[32,1024]{1,0:T(8,128)S(1)}) custom-call(f32[72,256]{1,0:T(8,128)S(1)} %shard_map.138.one_ref, f32[72,256]{1,0:T(8,128)S(1)} %collective-permute-done.2.two_ref, bf16[256,1024]{1,0:T(8,128)(2,1)S(1)} %copy-done.1), custom_call_target="tpu_custom_call" | custom-call | tf_op jit(solution)/shard_map/pallas_call | solution.py:400
  21.4 1.3 %collective-permute-done.3 = f32[32,1024]{1,0:T(8,128)S(1)} collective-permute-done((f32[32,1024]{1,0:T(8,128)S(1)}, f32[32,1024]{1,0:T(8,128)S(1)}, u32[]{:S(2)}, u32[]{:S(2)}) %collective-permute-start.3) | collective-permute-done | bytes 131104 | tf_op jit(solution)/shard_map/ppermute | solution.py:306
  22.7 1.9 %collective-permute-start.4 = (f32[32,1024]{1,0:T(8,128)S(1)}, f32[32,1024]{1,0:T(8,128)S(1)}, u32[]{:S(2)}, u32[]{:S(2)}) collective-permute-start(f32[32,1024]{1,0:T(8,128)S(1)} %add.43), channel_id=1, source_target_pairs={{0,2},{1,3},{2,0},{3,1},{4,6},{5,7},{6,4},{7,5},{8,10},{9,11},{10,... | collective-permute-start | bytes 393224 | tf_op jit(solution)/shard_map/ppermute | solution.py:306
  24.6 3.8 %collective-permute-done.4 = f32[32,1024]{1,0:T(8,128)S(1)} collective-permute-done((f32[32,1024]{1,0:T(8,128)S(1)}, f32[32,1024]{1,0:T(8,128)S(1)}, u32[]{:S(2)}, u32[]{:S(2)}) %collective-permute-start.4) | collective-permute-done | bytes 131104 | tf_op jit(solution)/shard_map/ppermute | solution.py:306
  28.6 1.3 %collective-permute-done.5.back_ref = f32[32,1024]{1,0:T(8,128)S(1)} collective-permute-done((f32[32,1024]{1,0:T(8,128)S(1)}, f32[32,1024]{1,0:T(8,128)S(1)}, u32[]{:S(2)}, u32[]{:S(2)}) %collective-permute-start.5) | collective-permute-done | bytes 131104 | tf_op jit(solution)/shard_map/ppermute | solution.py:306
  29.9 4.6 %shard_map.140 = (f32[64,1024]{1,0:T(8,128)S(1)}, f32[32,512]{1,0:T(8,128)S(1)}, f32[32,512]{1,0:T(8,128)S(1)}, f32[32,512]{1,0:T(8,128)S(1)}, f32[32,512]{1,0:T(8,128)S(1)}) custom-call(f32[32,1024]{1,0:T(8,128)S(1)} %add.44.half_ref, f32[32,1024]{1,0:T(8,128)S(1)} %collective-permute-done.5.back_ref, bf16[64,1024]{1,0:T(8,128)(2,1)S(1)} %bitcast.7, ...), custom_call_target="tpu_custom_call" | custom-call | tf_op jit(solution)/shard_map/pallas_call | solution.py:407
  34.7 0.4 collective-permute-start.11
  35.1 0.7 %collective-permute-done.6 = f32[32,512]{1,0:T(8,128)S(1)} collective-permute-done((f32[32,512]{1,0:T(8,128)S(1)}, f32[32,512]{1,0:T(8,128)S(1)}, u32[]{:S(2)}, u32[]{:S(2)}) %collective-permute-start.6) | collective-permute-done | bytes 65568 | tf_op jit(solution)/shard_map/ppermute | solution.py:306
  35.9 1.8 %collective-permute-start.7 = (f32[32,512]{1,0:T(8,128)S(1)}, f32[32,512]{1,0:T(8,128)S(1)}, u32[]{:S(2)}, u32[]{:S(2)}) collective-permute-start(f32[32,512]{1,0:T(8,128)S(1)} %add.46), channel_id=1, source_target_pairs={{0,2},{1,3},{2,0},{3,1},{4,6},{5,7},{6,4},{7,5},{8,10},{9,11},{10,... | collective-permute-start | bytes 196616 | tf_op jit(solution)/shard_map/ppermute | solution.py:306
  37.7 1.6 %collective-permute-start.12 = (f32[32,512]{1,0:T(8,128)S(1)}, f32[32,512]{1,0:T(8,128)S(1)}, u32[]{:S(2)}, u32[]{:S(2)}) collective-permute-start(f32[32,512]{1,0:T(8,128)S(1)} %add.51), channel_id=1, source_target_pairs={{0,4},{4,0},{8,12},{12,8},{16,20},{20,16},{24,28},{28,24},{1,5},{5... | collective-permute-start | bytes 196616 | tf_op jit(solution)/shard_map/ppermute | solution.py:306
  39.2 0.9 %collective-permute-done.7 = f32[32,512]{1,0:T(8,128)S(1)} collective-permute-done((f32[32,512]{1,0:T(8,128)S(1)}, f32[32,512]{1,0:T(8,128)S(1)}, u32[]{:S(2)}, u32[]{:S(2)}) %collective-permute-start.7) | collective-permute-done | bytes 65568 | tf_op jit(solution)/shard_map/ppermute | solution.py:306
  40.2 1.8 %collective-permute-start.8 = (f32[32,512]{1,0:T(8,128)S(1)}, f32[32,512]{1,0:T(8,128)S(1)}, u32[]{:S(2)}, u32[]{:S(2)}) collective-permute-start(f32[32,512]{1,0:T(8,128)S(1)} %add.47), channel_id=1, source_target_pairs={{0,4},{4,0},{8,12},{12,8},{16,20},{20,16},{24,28},{28,24},{1,5},{5... | collective-permute-start | bytes 196616 | tf_op jit(solution)/shard_map/ppermute | solution.py:306
  42.2 1.4 %collective-permute-start.13 = (f32[32,512]{1,0:T(8,128)S(1)}, f32[32,512]{1,0:T(8,128)S(1)}, u32[]{:S(2)}, u32[]{:S(2)}) collective-permute-start(f32[32,512]{1,0:T(8,128)S(1)} %add.52), channel_id=1, source_target_pairs={{0,2},{1,3},{2,0},{3,1},{4,6},{5,7},{6,4},{7,5},{8,10},{9,11},{10,... | collective-permute-start | bytes 196616 | tf_op jit(solution)/shard_map/ppermute | solution.py:306
  43.6 0.9 %collective-permute-done.8 = f32[32,512]{1,0:T(8,128)S(1)} collective-permute-done((f32[32,512]{1,0:T(8,128)S(1)}, f32[32,512]{1,0:T(8,128)S(1)}, u32[]{:S(2)}, u32[]{:S(2)}) %collective-permute-start.8) | collective-permute-done | bytes 65568 | tf_op jit(solution)/shard_map/ppermute | solution.py:306
  44.5 1.9 %collective-permute-start.9 = (f32[32,512]{1,0:T(8,128)S(1)}, f32[32,512]{1,0:T(8,128)S(1)}, u32[]{:S(2)}, u32[]{:S(2)}) collective-permute-start(f32[32,512]{1,0:T(8,128)S(1)} %add.48), channel_id=1, source_target_pairs={{0,8},{4,12},{8,0},{12,4},{16,24},{20,28},{24,16},{28,20},{1,9},{5... | collective-permute-start | bytes 196616 | tf_op jit(solution)/shard_map/ppermute | solution.py:306
  46.6 3.2 %collective-permute-start.14 = (f32[32,512]{1,0:T(8,128)S(1)}, f32[32,512]{1,0:T(8,128)S(1)}, u32[]{:S(2)}, u32[]{:S(2)}) collective-permute-start(f32[32,512]{1,0:T(8,128)S(1)} %add.53), channel_id=1, source_target_pairs={{0,16},{4,20},{8,24},{12,28},{16,0},{20,4},{24,8},{28,12},{1,17},{... | collective-permute-start | bytes 196616 | tf_op jit(solution)/shard_map/ppermute | solution.py:306
  49.8 2.2 %collective-permute-start.10 = (f32[32,512]{1,0:T(8,128)S(1)}, f32[32,512]{1,0:T(8,128)S(1)}, u32[]{:S(2)}, u32[]{:S(2)}) collective-permute-start(f32[32,512]{1,0:T(8,128)S(1)} %add.49), channel_id=1, source_target_pairs={{0,16},{4,20},{8,24},{12,28},{16,0},{20,4},{24,8},{28,12},{1,17},{... | collective-permute-start | bytes 196616 | tf_op jit(solution)/shard_map/ppermute | solution.py:306
  52.0 1.4 %collective-permute-done.14 = f32[32,512]{1,0:T(8,128)S(1)} collective-permute-done((f32[32,512]{1,0:T(8,128)S(1)}, f32[32,512]{1,0:T(8,128)S(1)}, u32[]{:S(2)}, u32[]{:S(2)}) %collective-permute-start.14) | collective-permute-done | bytes 65568 | tf_op jit(solution)/shard_map/ppermute | solution.py:306
  53.5 1.1 %collective-permute-start.15 = (f32[32,512]{1,0:T(8,128)S(1)}, f32[32,512]{1,0:T(8,128)S(1)}, u32[]{:S(2)}, u32[]{:S(2)}) collective-permute-start(f32[32,512]{1,0:T(8,128)S(1)} %add.54), channel_id=1, source_target_pairs={{0,8},{4,12},{8,0},{12,4},{16,24},{20,28},{24,16},{28,20},{1,9},{5... | collective-permute-start | bytes 196616 | tf_op jit(solution)/shard_map/ppermute | solution.py:306
  54.5 0.5 collective-permute-done.10
  55.1 2.7 %collective-permute-done.15 = f32[32,512]{1,0:T(8,128)S(1)} collective-permute-done((f32[32,512]{1,0:T(8,128)S(1)}, f32[32,512]{1,0:T(8,128)S(1)}, u32[]{:S(2)}, u32[]{:S(2)}) %collective-permute-start.15) | collective-permute-done | bytes 65568 | tf_op jit(solution)/shard_map/ppermute | solution.py:306
  57.9 1.2 %collective-permute-done.17 = f32[32,512]{1,0:T(8,128)S(1)} collective-permute-done((f32[32,512]{1,0:T(8,128)S(1)}, f32[32,512]{1,0:T(8,128)S(1)}, u32[]{:S(2)}, u32[]{:S(2)}) %collective-permute-start.17) | collective-permute-done | bytes 65568 | tf_op jit(solution)/shard_map/ppermute | solution.py:306
  59.1 0.7 %fusion = bf16[64,1024]{1,0:T(8,128)(2,1)} fusion(f32[64,1024]{1,0:T(8,128)S(1)} %get-tuple-element.20, f32[32,1024]{1,0:T(8,128)S(1)} %get-tuple-element.26, f32[32,1024]{1,0:T(8,128)S(1)} %get-tuple-element.25), kind=kLoop, calls=%fused_computation.1 | loop fusion | flops 196608 | bytes 655360 | tf_op jit(solution)/shard_map/convert_element_type | solution.py:416
  (37 shorter events, 1.1 us)
Async XLA Ops:
  0.0 20.7 %copy-start.1 = (bf16[256,1024]{1,0:T(8,128)(2,1)S(1)}, bf16[256,1024]{1,0:T(8,128)(2,1)}, u32[]{:S(2)}) copy-start(bf16[256,1024]{1,0:T(8,128)(2,1)} %w_ref.1) | copy-start | bytes 1572868
  0.0 29.9 %copy-start = (bf16[2,1408,1024]{2,1,0:T(8,128)(2,1)S(1)}, bf16[2,1408,1024]{2,1,0:T(8,128)(2,1)}, u32[]{:S(2)}) copy-start(bf16[2,1408,1024]{2,1,0:T(8,128)(2,1)} %up_ref) | copy-start | bytes 17301508
  0.0 29.9 %copy-start.2 = (bf16[4,16,1024]{2,1,0:T(8,128)(2,1)S(1)}, bf16[4,16,1024]{2,1,0:T(8,128)(2,1)}, u32[]{:S(2)}) copy-start(bf16[4,16,1024]{2,1,0:T(8,128)(2,1)} %param.14) | copy-start | bytes 393220
  0.0 29.9 %copy-start.3 = (bf16[1024,16]{0,1:T(8,128)(2,1)S(1)}, bf16[1024,16]{0,1:T(8,128)(2,1)}, u32[]{:S(2)}) copy-start(bf16[1024,16]{0,1:T(8,128)(2,1)} %param.24) | copy-start | bytes 98308
  0.0 29.9 %copy-start.4 = (f32[1024]{0:T(1024)S(1)}, f32[1024]{0:T(1024)}, u32[]{:S(2)}) copy-start(f32[1024]{0:T(1024)} %param.21) | copy-start | bytes 12292
  0.0 29.9 %copy-start.5 = (s32[4,16,2]{1,2,0:T(2,128)S(1)}, s32[4,16,2]{1,2,0:T(2,128)}, u32[]{:S(2)}) copy-start(s32[4,16,2]{1,2,0:T(2,128)} %param.25) | copy-start | bytes 1540
  4.9 5.4 %collective-permute-start = (f32[72,256]{1,0:T(8,128)S(1)}, f32[72,256]{1,0:T(8,128)S(1)}, u32[]{:S(2)}, u32[]{:S(2)}) collective-permute-start(f32[72,256]{1,0:T(8,128)S(1)} %shard_map.136.refs_0_), channel_id=1, source_target_pairs={{0,4},{4,0},{8,12},{12,8},{16,20},{20,16},{24,28},{28,24},{1,5},{5... | collective-permute-start | bytes 221192 | tf_op jit(solution)/shard_map/ppermute | solution.py:306
  10.5 4.5 %collective-permute-start.1 = (f32[72,256]{1,0:T(8,128)S(1)}, f32[72,256]{1,0:T(8,128)S(1)}, u32[]{:S(2)}, u32[]{:S(2)}) collective-permute-start(f32[72,256]{1,0:T(8,128)S(1)} %shard_map.137.refs_0_), channel_id=1, source_target_pairs={{0,8},{4,12},{8,0},{12,4},{16,24},{20,28},{24,16},{28,20},{1,9},{5... | collective-permute-start | bytes 221192 | tf_op jit(solution)/shard_map/ppermute | solution.py:306
  15.2 5.4 %collective-permute-start.2 = (f32[72,256]{1,0:T(8,128)S(1)}, f32[72,256]{1,0:T(8,128)S(1)}, u32[]{:S(2)}, u32[]{:S(2)}) collective-permute-start(f32[72,256]{1,0:T(8,128)S(1)} %shard_map.138.one_ref), channel_id=1, source_target_pairs={{0,16},{4,20},{8,24},{12,28},{16,0},{20,4},{24,8},{28,12},{1,17},{... | collective-permute-start | bytes 221192 | tf_op jit(solution)/shard_map/ppermute | solution.py:306
  21.3 1.4 %collective-permute-start.3 = (f32[32,1024]{1,0:T(8,128)S(1)}, f32[32,1024]{1,0:T(8,128)S(1)}, u32[]{:S(2)}, u32[]{:S(2)}) collective-permute-start(f32[32,1024]{1,0:T(8,128)S(1)} %get-tuple-element.17), channel_id=1, source_target_pairs={{0,1},{1,0},{2,3},{3,2},{4,5},{5,4},{6,7},{7,6},{8,9},{9,8},{10,11... | collective-permute-start | bytes 393224 | tf_op jit(solution)/shard_map/ppermute | solution.py:306
  22.7 5.7 %collective-permute-start.4 = (f32[32,1024]{1,0:T(8,128)S(1)}, f32[32,1024]{1,0:T(8,128)S(1)}, u32[]{:S(2)}, u32[]{:S(2)}) collective-permute-start(f32[32,1024]{1,0:T(8,128)S(1)} %add.43), channel_id=1, source_target_pairs={{0,2},{1,3},{2,0},{3,1},{4,6},{5,7},{6,4},{7,5},{8,10},{9,11},{10,... | collective-permute-start | bytes 393224 | tf_op jit(solution)/shard_map/ppermute | solution.py:306
  28.5 1.4 %collective-permute-start.5 = (f32[32,1024]{1,0:T(8,128)S(1)}, f32[32,1024]{1,0:T(8,128)S(1)}, u32[]{:S(2)}, u32[]{:S(2)}) collective-permute-start(f32[32,1024]{1,0:T(8,128)S(1)} %add.44.half_ref), channel_id=1, source_target_pairs={{0,1},{1,0},{2,3},{3,2},{4,5},{5,4},{6,7},{7,6},{8,9},{9,8},{10,11... | collective-permute-start | bytes 393224 | tf_op jit(solution)/shard_map/ppermute | solution.py:306
  34.5 1.3 %collective-permute-start.6 = (f32[32,512]{1,0:T(8,128)S(1)}, f32[32,512]{1,0:T(8,128)S(1)}, u32[]{:S(2)}, u32[]{:S(2)}) collective-permute-start(f32[32,512]{1,0:T(8,128)S(1)} %get-tuple-element.22), channel_id=1, source_target_pairs={{0,1},{1,0},{2,3},{3,2},{4,5},{5,4},{6,7},{7,6},{8,9},{9,8},{10,11... | collective-permute-start | bytes 196616 | tf_op jit(solution)/shard_map/ppermute | solution.py:306
  34.7 2.9 %collective-permute-start.11 = (f32[32,512]{1,0:T(8,128)S(1)}, f32[32,512]{1,0:T(8,128)S(1)}, u32[]{:S(2)}, u32[]{:S(2)}) collective-permute-start(f32[32,512]{1,0:T(8,128)S(1)} %get-tuple-element.24), channel_id=1, source_target_pairs={{0,1},{1,0},{2,3},{3,2},{4,5},{5,4},{6,7},{7,6},{8,9},{9,8},{10,11... | collective-permute-start | bytes 196616 | tf_op jit(solution)/shard_map/ppermute | solution.py:306
  35.9 4.3 %collective-permute-start.7 = (f32[32,512]{1,0:T(8,128)S(1)}, f32[32,512]{1,0:T(8,128)S(1)}, u32[]{:S(2)}, u32[]{:S(2)}) collective-permute-start(f32[32,512]{1,0:T(8,128)S(1)} %add.46), channel_id=1, source_target_pairs={{0,2},{1,3},{2,0},{3,1},{4,6},{5,7},{6,4},{7,5},{8,10},{9,11},{10,... | collective-permute-start | bytes 196616 | tf_op jit(solution)/shard_map/ppermute | solution.py:306
  37.7 4.5 %collective-permute-start.12 = (f32[32,512]{1,0:T(8,128)S(1)}, f32[32,512]{1,0:T(8,128)S(1)}, u32[]{:S(2)}, u32[]{:S(2)}) collective-permute-start(f32[32,512]{1,0:T(8,128)S(1)} %add.51), channel_id=1, source_target_pairs={{0,4},{4,0},{8,12},{12,8},{16,20},{20,16},{24,28},{28,24},{1,5},{5... | collective-permute-start | bytes 196616 | tf_op jit(solution)/shard_map/ppermute | solution.py:306
  40.2 4.3 %collective-permute-start.8 = (f32[32,512]{1,0:T(8,128)S(1)}, f32[32,512]{1,0:T(8,128)S(1)}, u32[]{:S(2)}, u32[]{:S(2)}) collective-permute-start(f32[32,512]{1,0:T(8,128)S(1)} %add.47), channel_id=1, source_target_pairs={{0,4},{4,0},{8,12},{12,8},{16,20},{20,16},{24,28},{28,24},{1,5},{5... | collective-permute-start | bytes 196616 | tf_op jit(solution)/shard_map/ppermute | solution.py:306
  42.2 4.3 %collective-permute-start.13 = (f32[32,512]{1,0:T(8,128)S(1)}, f32[32,512]{1,0:T(8,128)S(1)}, u32[]{:S(2)}, u32[]{:S(2)}) collective-permute-start(f32[32,512]{1,0:T(8,128)S(1)} %add.52), channel_id=1, source_target_pairs={{0,2},{1,3},{2,0},{3,1},{4,6},{5,7},{6,4},{7,5},{8,10},{9,11},{10,... | collective-permute-start | bytes 196616 | tf_op jit(solution)/shard_map/ppermute | solution.py:306
  44.5 5.2 %collective-permute-start.9 = (f32[32,512]{1,0:T(8,128)S(1)}, f32[32,512]{1,0:T(8,128)S(1)}, u32[]{:S(2)}, u32[]{:S(2)}) collective-permute-start(f32[32,512]{1,0:T(8,128)S(1)} %add.48), channel_id=1, source_target_pairs={{0,8},{4,12},{8,0},{12,4},{16,24},{20,28},{24,16},{28,20},{1,9},{5... | collective-permute-start | bytes 196616 | tf_op jit(solution)/shard_map/ppermute | solution.py:306
  46.6 6.9 %collective-permute-start.14 = (f32[32,512]{1,0:T(8,128)S(1)}, f32[32,512]{1,0:T(8,128)S(1)}, u32[]{:S(2)}, u32[]{:S(2)}) collective-permute-start(f32[32,512]{1,0:T(8,128)S(1)} %add.53), channel_id=1, source_target_pairs={{0,16},{4,20},{8,24},{12,28},{16,0},{20,4},{24,8},{28,12},{1,17},{... | collective-permute-start | bytes 196616 | tf_op jit(solution)/shard_map/ppermute | solution.py:306
  49.8 5.2 %collective-permute-start.10 = (f32[32,512]{1,0:T(8,128)S(1)}, f32[32,512]{1,0:T(8,128)S(1)}, u32[]{:S(2)}, u32[]{:S(2)}) collective-permute-start(f32[32,512]{1,0:T(8,128)S(1)} %add.49), channel_id=1, source_target_pairs={{0,16},{4,20},{8,24},{12,28},{16,0},{20,4},{24,8},{28,12},{1,17},{... | collective-permute-start | bytes 196616 | tf_op jit(solution)/shard_map/ppermute | solution.py:306
  53.5 4.3 %collective-permute-start.15 = (f32[32,512]{1,0:T(8,128)S(1)}, f32[32,512]{1,0:T(8,128)S(1)}, u32[]{:S(2)}, u32[]{:S(2)}) collective-permute-start(f32[32,512]{1,0:T(8,128)S(1)} %add.54), channel_id=1, source_target_pairs={{0,8},{4,12},{8,0},{12,4},{16,24},{20,28},{24,16},{28,20},{1,9},{5... | collective-permute-start | bytes 196616 | tf_op jit(solution)/shard_map/ppermute | solution.py:306
  55.0 2.9 %collective-permute-start.16 = (f32[32,512]{1,0:T(8,128)S(1)}, f32[32,512]{1,0:T(8,128)S(1)}, u32[]{:S(2)}, u32[]{:S(2)}) collective-permute-start(f32[32,512]{1,0:T(8,128)S(1)} %add.50), channel_id=1, source_target_pairs={{0,1},{1,0},{2,3},{3,2},{4,5},{5,4},{6,7},{7,6},{8,9},{9,8},{10,11... | collective-permute-start | bytes 196616 | tf_op jit(solution)/shard_map/ppermute | solution.py:306
  57.8 1.3 %collective-permute-start.17 = (f32[32,512]{1,0:T(8,128)S(1)}, f32[32,512]{1,0:T(8,128)S(1)}, u32[]{:S(2)}, u32[]{:S(2)}) collective-permute-start(f32[32,512]{1,0:T(8,128)S(1)} %add.55), channel_id=1, source_target_pairs={{0,1},{1,0},{2,3},{3,2},{4,5},{5,4},{6,7},{7,6},{8,9},{9,8},{10,11... | collective-permute-start | bytes 196616 | tf_op jit(solution)/shard_map/ppermute | solution.py:306

commit v7 on v6

--- a/solution.py
+++ b/solution.py
@@ -219,9 +219,8 @@
     return sums, stat, widen(columns, 2 * heads * len(parts) + heads, heads)
 
 
-def merge_kernel(tokens, *refs):
-    out_ref = refs[-1]
-    sums, stat, _ = merge_parts(tokens, refs[:-1])
+def merge_kernel(tokens, one_ref, two_ref, _, out_ref):
+    sums, stat, _ = merge_parts(tokens, (one_ref, two_ref))
     out_ref[:tokens, :] = sums
     out_ref[tokens:, :] = jnp.zeros((stat.shape[0], sums.shape[1]), F32)
     out_ref[tokens:, :LANES] = stat
@@ -234,7 +233,7 @@
     give_ref[...] = jnp.where(low, value[half:], value[:half])
 
 
-def project_kernel(steps, requests, one_ref, two_ref, w_ref, keep_ref, give_ref):
+def project_kernel(steps, requests, one_ref, two_ref, w_ref, _, keep_ref, give_ref):
     tokens = steps * requests
     sums, _, totals = merge_parts(tokens, (one_ref, two_ref))
     attended = (sums / totals).astype(BF16)
@@ -249,13 +248,37 @@
     return [(at, min(size, total - at)) for at in range(0, total, size)]
 
 
+def add_kernel(one_ref, two_ref, _, out_ref):
+    out_ref[...] = one_ref[...] + two_ref[...]
+
+
+def fetch_kernel(index, after_ref, weights_hbm, out_ref, done_ref, sems):
+    del after_ref
+    source = weights_hbm if index is None else weights_hbm.at[index]
+    copies = []
+    for i, (at, size) in enumerate(chunks_of(out_ref.shape[0], 384)):
+        rows = pl.ds(at, size)
+        copies.append(pltpu.make_async_copy(source.at[rows], out_ref.at[rows], sems.at[i]))
+        copies[-1].start()
+    done_ref[...] = jnp.zeros_like(done_ref)
+    for copy in copies:
+        copy.wait()
+
+
+def fetch(after, weights, index=None):
+    shape = weights.shape[-2:]
+    return call(
+        functools.partial(fetch_kernel, index),
+        [(shape, BF16), ((8, LANES), F32)],
+        [VMEM, HBM],
+        1,
+        [pltpu.SemaphoreType.DMA((len(chunks_of(shape[0], 384)),))],
+    )(after, in_hbm(weights))
+
+
 def expert_kernel(
-    half_ref, back_ref, tokens_ref, gain_ref, router_ref, choice_ref, up_ref, down_hbm,
-    mid_ref, one_ref, two_ref, three_ref, four_ref, down_ref, down_sem,
+    half_ref, back_ref, tokens_ref, gain_ref, router_ref, choice_ref, gate_ref, up_ref, down_ref, mid_ref, *sum_refs
 ):
-    sum_refs = (one_ref, two_ref, three_ref, four_ref)
-    down_copy = pltpu.make_async_copy(down_hbm, down_ref, down_sem)
-    down_copy.start()
     hidden_local = down_ref.shape[0]
     half = half_ref.shape[0]
     steps, _, requests = choice_ref.shape
@@ -279,16 +302,12 @@
     second = 1.0 - first
     device = lax.axis_index("seq") * lax.axis_size("tp") + lax.axis_index("tp")
     total = jnp.zeros(mid_ref.shape, F32)
-    hiddens = []
-    chunks = chunks_of(hidden_local, 256)
-    for at, size in chunks:
+    for at, size in chunks_of(hidden_local, 256):
         column_expert = (device * hidden_local + at + iota((1, size), 1)) // FF
         coef = jnp.where(column_expert == choices[0], first, jnp.where(column_expert == choices[1], second, 0.0))
-        gate = dot_nt(moe_in, up_ref[0, at : at + size, :])
-        up = dot_nt(moe_in, up_ref[1, at : at + size, :])
-        hiddens.append((jax.nn.gelu(gate, approximate=True) * up * coef).astype(BF16))
-    down_copy.wait()
-    for (at, size), hidden in zip(chunks, hiddens):
+        gate = dot_nt(moe_in, gate_ref[at : at + size, :])
+        up = dot_nt(moe_in, up_ref[at : at + size, :])
+        hidden = (jax.nn.gelu(gate, approximate=True) * up * coef).astype(BF16)
         total = total + dot(hidden, down_ref[at : at + size, :])
     columns = total.shape[1] // 2
     for i in range(2):
@@ -304,13 +323,6 @@
 def swap(value, bit):
     axis, flip = bit
     return lax.ppermute(value, axis, [(i, i ^ flip) for i in range(lax.axis_size(axis))])
-
-
-def reduce_halves(keep, give, split, bits):
-    half = keep + swap(give, split)
-    for bit in bits:
-        half = half + swap(half, bit)
-    return half, swap(half, split)
 
 
 def reduce_columns(keeps, gives, split, orders):
@@ -390,22 +402,35 @@
         ],
     )(*map(in_hbm, (cache_len, flat_in, attn_gain, bucket_table, rel_bias.T, w_qkv, key_cache, value_cache)))
 
-    packed, w_gate_up, w_down = lax.optimization_barrier((packed, w_gate_up, w_down))
     seq_bits, tp_bits = device_bits("seq"), device_bits("tp")
-    for bit in seq_bits[:-1]:
-        (packed,) = call(functools.partial(merge_kernel, tokens), [(packed_shape, F32)], [VMEM] * 2, 2)(
-            packed, swap(packed, bit)
-        )
+    staged = []
+    token = jnp.zeros((8, LANES), F32)
+    for i, bit in enumerate(seq_bits):
+        other = swap(packed, bit)
+        if i >= len(seq_bits) - 2:
+            weights, token = fetch(packed, w_gate_up, len(staged))
+            staged.append(weights)
+        if i < len(seq_bits) - 1:
+            (packed,) = call(functools.partial(merge_kernel, tokens), [(packed_shape, F32)], [VMEM] * 3, 2)(
+                packed, other, token
+            )
     half_shape = ((half, width), F32)
     keep, give = call(
-        functools.partial(project_kernel, steps, requests), [half_shape, half_shape], [VMEM] * 3, 4
-    )(packed, swap(packed, seq_bits[-1]), w_out)
-
-    mine, other = reduce_halves(keep, give, tp_bits[0], tp_bits[1:])
+        functools.partial(project_kernel, steps, requests), [half_shape, half_shape], [VMEM] * 4, 4
+    )(packed, other, w_out, token)
+
+    half_sum = keep + swap(give, tp_bits[0])
+    for bit in tp_bits[1:]:
+        other = swap(half_sum, bit)
+        if len(staged) == 2:
+            weights, token = fetch(half_sum, w_down)
+            staged.append(weights)
+        (half_sum,) = call(add_kernel, [half_shape], [VMEM] * 3, 1)(half_sum, other, token)
+    mine, other = half_sum, swap(half_sum, tp_bits[0])
 
     column_shape = ((half, width // 2), F32)
-    mid, *sums = call(expert_kernel, [((tokens, width), F32)] + [column_shape] * 4, [VMEM] * 7 + [HBM], 12, [pltpu.VMEM(w_down.shape, BF16), dma(())])(
-        mine, other, flat_in, moe_gain[None], router.T, expert_choice.transpose(0, 2, 1), w_gate_up, in_hbm(w_down)
+    mid, *sums = call(expert_kernel, [((tokens, width), F32)] + [column_shape] * 4, [VMEM] * 9, 8)(
+        mine, other, flat_in, moe_gain[None], router.T, expert_choice.transpose(0, 2, 1), *staged
     )
     bits = tp_bits[1:] + seq_bits
     swapped = [bits[i ^ 1] if i ^ 1 < len(bits) else bits[i] for i in range(len(bits))]

time: 60 us -> 58.4 us (0.973)
  waiting for transfers between devices: 22.3 us -> 16.9 us
  Pallas kernels: 10.5 us -> 14.3 us
    ppermute x18, waiting for transfers between devices: 22.3 us -> 16.9 us  [swap(): lax.ppermute(value, axis, [(i, i ^ flip) for i in range(lax.axis_size(axi...]
    pallas_call x0 -> x4, Pallas kernels: none -> 5.37 us  [the longest x3 5.36 us: fetch(): call(functools.partial(fetch_kernel, index), [(shape, BF16), ((8, LANES),...]
    pallas_call x1, Pallas kernels: 4.59 us -> 3.24 us  [on_device(): call(expert_kernel, [((tokens, width), F32)] + [column_shape] * 4, [VMEM]...]
  transfers between devices with their start and end apart: 18 -> 18, of which waited for: 15 -> 15; matrix products, arithmetic and copies ran while one was open for 0% -> 0% of each run, Pallas kernels for 0% -> 9%
where the time goes in v7:
time: 58.4 us; the launch traced here: 58.2 us
  starting transfers between devices  25.8 us (44%)
  waiting for transfers between devices  16.9 us (29%)
  Pallas kernels  14.3 us (24%)
  other arithmetic  0.83 us (1%)
    ppermute x18, starting transfers between devices, swap(): lax.ppermute(value, axis, [(i, i ^ flip) for i in range(lax.axis_size(axi...  25.8 us
    ppermute x18, waiting for transfers between devices, swap(): lax.ppermute(value, axis, [(i, i ^ flip) for i in range(lax.axis_size(axi...  16.9 us
    pallas_call x3, Pallas kernels, fetch(): call(functools.partial(fetch_kernel, index), [(shape, BF16), ((8, LANES),...  5.36 us
    pallas_call x1, Pallas kernels, on_device(): call(functools.partial(attend_kernel, steps, requests, heads), [(packed_s...  4.59 us
    pallas_call x1, Pallas kernels, on_device(): call(expert_kernel, [((tokens, width), F32)] + [column_shape] * 4, [VMEM]...  3.24 us
  transfers between devices with their start and end apart: 18, of which 15 were waited for; matrix products, arithmetic and copies ran while one was open for 0% of the time, Pallas kernels for 9%

profile of v7, /device:TPU:0, one launch (start us, length us, event | category | flops | bytes accessed | tf_op | source)
XLA Modules:
  0.0 58.2 jit_solution(6642969820560470502)
XLA Ops:
  0.0 4.6 %shard_map.136.one_ref = f32[72,256]{1,0:T(8,128)S(1)} custom-call(s32[16]{0:T(128)} %len_hbm.1, bf16[64,1024]{1,0:T(8,128)(2,1)} %bitcast.6, f32[1024]{0:T(1024)} %gain_hbm.1, s32[2052]{0:T(1024)} %table_hbm.1, f32[4,32]{1,0:T(4,128)} %bitcast.11, bf16[3,1024,256]{2,1,0:T(8,128)(2,1)} %w_hbm.1, bf16[16,256,256]{2,1,0:T(8,128)(2,1)} %k_hbm.1, ...), custom_call_target="tpu_custom_call" | custom-call | tf_op jit(solution)/shard_map/pallas_call | solution.py:379
  4.6 3.0 %collective-permute-start = (f32[72,256]{1,0:T(8,128)S(1)}, f32[72,256]{1,0:T(8,128)S(1)}, u32[]{:S(2)}, u32[]{:S(2)}) collective-permute-start(f32[72,256]{1,0:T(8,128)S(1)} %shard_map.136.one_ref), channel_id=1, source_target_pairs={{0,4},{4,0},{8,12},{12,8},{16,20},{20,16},{24,28},{28,24},{1,5},{5... | collective-permute-start | bytes 221192 | tf_op jit(solution)/shard_map/ppermute | solution.py:325
  7.6 2.3 %collective-permute-done.two_ref = f32[72,256]{1,0:T(8,128)S(1)} collective-permute-done((f32[72,256]{1,0:T(8,128)S(1)}, f32[72,256]{1,0:T(8,128)S(1)}, u32[]{:S(2)}, u32[]{:S(2)}) %collective-permute-start) | collective-permute-done | bytes 73760 | tf_op jit(solution)/shard_map/ppermute | solution.py:325
  10.2 2.2 %collective-permute-start.1 = (f32[72,256]{1,0:T(8,128)S(1)}, f32[72,256]{1,0:T(8,128)S(1)}, u32[]{:S(2)}, u32[]{:S(2)}) collective-permute-start(f32[72,256]{1,0:T(8,128)S(1)} %shard_map.137.after_ref.one_ref), channel_id=1, source_target_pairs={{0,8},{4,12},{8,0},{12,4},{16,24},{20,28},{24,16},{28,20},{1,9},{5... | collective-permute-start | bytes 221192 | tf_op jit(solution)/shard_map/ppermute | solution.py:325
  12.4 1.8 %shard_map.138 = (bf16[1408,1024]{1,0:T(8,128)(2,1)S(1)}, f32[8,128]{1,0:T(8,128)S(1)}) custom-call(f32[72,256]{1,0:T(8,128)S(1)} %shard_map.137.after_ref.one_ref, bf16[2,1408,1024]{2,1,0:T(8,128)(2,1)} %weights_hbm.4), custom_call_target="tpu_custom_call" | custom-call | tf_op jit(solution)/shard_map/pallas_call | solution.py:270
  14.2 0.5 collective-permute-done.1.two_ref
  15.0 3.1 %collective-permute-start.2 = (f32[72,256]{1,0:T(8,128)S(1)}, f32[72,256]{1,0:T(8,128)S(1)}, u32[]{:S(2)}, u32[]{:S(2)}) collective-permute-start(f32[72,256]{1,0:T(8,128)S(1)} %shard_map.139.after_ref.one_ref), channel_id=1, source_target_pairs={{0,16},{4,20},{8,24},{12,28},{16,0},{20,4},{24,8},{28,12},{1,17},{... | collective-permute-start | bytes 221192 | tf_op jit(solution)/shard_map/ppermute | solution.py:325
  18.1 1.8 %shard_map.140 = (bf16[1408,1024]{1,0:T(8,128)(2,1)S(1)}, f32[8,128]{1,0:T(8,128)S(1)}) custom-call(f32[72,256]{1,0:T(8,128)S(1)} %shard_map.139.after_ref.one_ref, bf16[2,1408,1024]{2,1,0:T(8,128)(2,1)} %weights_hbm.4), custom_call_target="tpu_custom_call" | custom-call | tf_op jit(solution)/shard_map/pallas_call | solution.py:270
  19.9 0.5 collective-permute-done.2.two_ref
  20.4 0.6 %shard_map.141 = (f32[32,1024]{1,0:T(8,128)S(1)}, f32[32,1024]{1,0:T(8,128)S(1)}) custom-call(f32[72,256]{1,0:T(8,128)S(1)} %shard_map.139.after_ref.one_ref, f32[72,256]{1,0:T(8,128)S(1)} %collective-permute-done.2.two_ref, bf16[256,1024]{1,0:T(8,128)(2,1)S(1)} %copy-done, f32[8,128]{1,0:T(8,128)S(1)} %get-tuple-element.19._), custom_call_target="tpu_custom_call" | custom-call | tf_op jit(solution)/shard_map/pallas_call | solution.py:418
  21.1 1.3 %collective-permute-done.3 = f32[32,1024]{1,0:T(8,128)S(1)} collective-permute-done((f32[32,1024]{1,0:T(8,128)S(1)}, f32[32,1024]{1,0:T(8,128)S(1)}, u32[]{:S(2)}, u32[]{:S(2)}) %collective-permute-start.3) | collective-permute-done | bytes 131104 | tf_op jit(solution)/shard_map/ppermute | solution.py:325
  22.5 1.9 %collective-permute-start.4 = (f32[32,1024]{1,0:T(8,128)S(1)}, f32[32,1024]{1,0:T(8,128)S(1)}, u32[]{:S(2)}, u32[]{:S(2)}) collective-permute-start(f32[32,1024]{1,0:T(8,128)S(1)} %add.40.after_ref.one_ref), channel_id=1, source_target_pairs={{0,2},{1,3},{2,0},{3,1},{4,6},{5,7},{6,4},{7,5},{8,10},{9,11},{10,... | collective-permute-start | bytes 393224 | tf_op jit(solution)/shard_map/ppermute | solution.py:325
  24.4 1.8 %shard_map.142 = (bf16[1408,1024]{1,0:T(8,128)(2,1)S(1)}, f32[8,128]{1,0:T(8,128)S(1)}) custom-call(f32[32,1024]{1,0:T(8,128)S(1)} %add.40.after_ref.one_ref, bf16[1408,1024]{1,0:T(8,128)(2,1)} %weights_hbm.5), custom_call_target="tpu_custom_call" | custom-call | tf_op jit(solution)/shard_map/pallas_call | solution.py:270
  26.2 2.0 %collective-permute-done.4.two_ref = f32[32,1024]{1,0:T(8,128)S(1)} collective-permute-done((f32[32,1024]{1,0:T(8,128)S(1)}, f32[32,1024]{1,0:T(8,128)S(1)}, u32[]{:S(2)}, u32[]{:S(2)}) %collective-permute-start.4) | collective-permute-done | bytes 131104 | tf_op jit(solution)/shard_map/ppermute | solution.py:325
  28.3 1.3 %collective-permute-done.5.back_ref = f32[32,1024]{1,0:T(8,128)S(1)} collective-permute-done((f32[32,1024]{1,0:T(8,128)S(1)}, f32[32,1024]{1,0:T(8,128)S(1)}, u32[]{:S(2)}, u32[]{:S(2)}) %collective-permute-start.5) | collective-permute-done | bytes 131104 | tf_op jit(solution)/shard_map/ppermute | solution.py:325
  29.6 3.2 %shard_map.144 = (f32[64,1024]{1,0:T(8,128)S(1)}, f32[32,512]{1,0:T(8,128)S(1)}, f32[32,512]{1,0:T(8,128)S(1)}, f32[32,512]{1,0:T(8,128)S(1)}, f32[32,512]{1,0:T(8,128)S(1)}) custom-call(f32[32,1024]{1,0:T(8,128)S(1)} %shard_map.143.half_ref, f32[32,1024]{1,0:T(8,128)S(1)} %collective-permute-done.5.back_ref, bf16[64,1024]{1,0:T(8,128)(2,1)S(1)} %bitcast.7, ...), custom_call_target="tpu_custom_call" | custom-call | tf_op jit(solution)/shard_map/pallas_call | solution.py:432
  33.5 0.7 %collective-permute-done.6 = f32[32,512]{1,0:T(8,128)S(1)} collective-permute-done((f32[32,512]{1,0:T(8,128)S(1)}, f32[32,512]{1,0:T(8,128)S(1)}, u32[]{:S(2)}, u32[]{:S(2)}) %collective-permute-start.6) | collective-permute-done | bytes 65568 | tf_op jit(solution)/shard_map/ppermute | solution.py:325
  34.2 1.8 %collective-permute-start.7 = (f32[32,512]{1,0:T(8,128)S(1)}, f32[32,512]{1,0:T(8,128)S(1)}, u32[]{:S(2)}, u32[]{:S(2)}) collective-permute-start(f32[32,512]{1,0:T(8,128)S(1)} %add.42), channel_id=1, source_target_pairs={{0,2},{1,3},{2,0},{3,1},{4,6},{5,7},{6,4},{7,5},{8,10},{9,11},{10,... | collective-permute-start | bytes 196616 | tf_op jit(solution)/shard_map/ppermute | solution.py:325
  36.0 1.6 %collective-permute-start.12 = (f32[32,512]{1,0:T(8,128)S(1)}, f32[32,512]{1,0:T(8,128)S(1)}, u32[]{:S(2)}, u32[]{:S(2)}) collective-permute-start(f32[32,512]{1,0:T(8,128)S(1)} %add.47), channel_id=1, source_target_pairs={{0,4},{4,0},{8,12},{12,8},{16,20},{20,16},{24,28},{28,24},{1,5},{5... | collective-permute-start | bytes 196616 | tf_op jit(solution)/shard_map/ppermute | solution.py:325
  37.6 1.0 %collective-permute-done.7 = f32[32,512]{1,0:T(8,128)S(1)} collective-permute-done((f32[32,512]{1,0:T(8,128)S(1)}, f32[32,512]{1,0:T(8,128)S(1)}, u32[]{:S(2)}, u32[]{:S(2)}) %collective-permute-start.7) | collective-permute-done | bytes 65568 | tf_op jit(solution)/shard_map/ppermute | solution.py:325
  38.6 1.8 %collective-permute-start.8 = (f32[32,512]{1,0:T(8,128)S(1)}, f32[32,512]{1,0:T(8,128)S(1)}, u32[]{:S(2)}, u32[]{:S(2)}) collective-permute-start(f32[32,512]{1,0:T(8,128)S(1)} %add.43), channel_id=1, source_target_pairs={{0,4},{4,0},{8,12},{12,8},{16,20},{20,16},{24,28},{28,24},{1,5},{5... | collective-permute-start | bytes 196616 | tf_op jit(solution)/shard_map/ppermute | solution.py:325
  40.6 1.4 %collective-permute-start.13 = (f32[32,512]{1,0:T(8,128)S(1)}, f32[32,512]{1,0:T(8,128)S(1)}, u32[]{:S(2)}, u32[]{:S(2)}) collective-permute-start(f32[32,512]{1,0:T(8,128)S(1)} %add.48), channel_id=1, source_target_pairs={{0,2},{1,3},{2,0},{3,1},{4,6},{5,7},{6,4},{7,5},{8,10},{9,11},{10,... | collective-permute-start | bytes 196616 | tf_op jit(solution)/shard_map/ppermute | solution.py:325
  41.9 1.0 %collective-permute-done.8 = f32[32,512]{1,0:T(8,128)S(1)} collective-permute-done((f32[32,512]{1,0:T(8,128)S(1)}, f32[32,512]{1,0:T(8,128)S(1)}, u32[]{:S(2)}, u32[]{:S(2)}) %collective-permute-start.8) | collective-permute-done | bytes 65568 | tf_op jit(solution)/shard_map/ppermute | solution.py:325
  42.9 1.9 %collective-permute-start.9 = (f32[32,512]{1,0:T(8,128)S(1)}, f32[32,512]{1,0:T(8,128)S(1)}, u32[]{:S(2)}, u32[]{:S(2)}) collective-permute-start(f32[32,512]{1,0:T(8,128)S(1)} %add.44), channel_id=1, source_target_pairs={{0,8},{4,12},{8,0},{12,4},{16,24},{20,28},{24,16},{28,20},{1,9},{5... | collective-permute-start | bytes 196616 | tf_op jit(solution)/shard_map/ppermute | solution.py:325
  44.9 3.2 %collective-permute-start.14 = (f32[32,512]{1,0:T(8,128)S(1)}, f32[32,512]{1,0:T(8,128)S(1)}, u32[]{:S(2)}, u32[]{:S(2)}) collective-permute-start(f32[32,512]{1,0:T(8,128)S(1)} %add.49), channel_id=1, source_target_pairs={{0,16},{4,20},{8,24},{12,28},{16,0},{20,4},{24,8},{28,12},{1,17},{... | collective-permute-start | bytes 196616 | tf_op jit(solution)/shard_map/ppermute | solution.py:325
  48.1 2.2 %collective-permute-start.10 = (f32[32,512]{1,0:T(8,128)S(1)}, f32[32,512]{1,0:T(8,128)S(1)}, u32[]{:S(2)}, u32[]{:S(2)}) collective-permute-start(f32[32,512]{1,0:T(8,128)S(1)} %add.45), channel_id=1, source_target_pairs={{0,16},{4,20},{8,24},{12,28},{16,0},{20,4},{24,8},{28,12},{1,17},{... | collective-permute-start | bytes 196616 | tf_op jit(solution)/shard_map/ppermute | solution.py:325
  50.4 1.4 %collective-permute-done.14 = f32[32,512]{1,0:T(8,128)S(1)} collective-permute-done((f32[32,512]{1,0:T(8,128)S(1)}, f32[32,512]{1,0:T(8,128)S(1)}, u32[]{:S(2)}, u32[]{:S(2)}) %collective-permute-start.14) | collective-permute-done | bytes 65568 | tf_op jit(solution)/shard_map/ppermute | solution.py:325
  51.8 1.1 %collective-permute-start.15 = (f32[32,512]{1,0:T(8,128)S(1)}, f32[32,512]{1,0:T(8,128)S(1)}, u32[]{:S(2)}, u32[]{:S(2)}) collective-permute-start(f32[32,512]{1,0:T(8,128)S(1)} %add.50), channel_id=1, source_target_pairs={{0,8},{4,12},{8,0},{12,4},{16,24},{20,28},{24,16},{28,20},{1,9},{5... | collective-permute-start | bytes 196616 | tf_op jit(solution)/shard_map/ppermute | solution.py:325
  52.9 0.5 collective-permute-done.10
  53.5 2.7 %collective-permute-done.15 = f32[32,512]{1,0:T(8,128)S(1)} collective-permute-done((f32[32,512]{1,0:T(8,128)S(1)}, f32[32,512]{1,0:T(8,128)S(1)}, u32[]{:S(2)}, u32[]{:S(2)}) %collective-permute-start.15) | collective-permute-done | bytes 65568 | tf_op jit(solution)/shard_map/ppermute | solution.py:325
  56.3 1.2 %collective-permute-done.17 = f32[32,512]{1,0:T(8,128)S(1)} collective-permute-done((f32[32,512]{1,0:T(8,128)S(1)}, f32[32,512]{1,0:T(8,128)S(1)}, u32[]{:S(2)}, u32[]{:S(2)}) %collective-permute-start.17) | collective-permute-done | bytes 65568 | tf_op jit(solution)/shard_map/ppermute | solution.py:325
  57.5 0.7 %fusion = bf16[64,1024]{1,0:T(8,128)(2,1)} fusion(f32[64,1024]{1,0:T(8,128)S(1)} %get-tuple-element.26, f32[32,1024]{1,0:T(8,128)S(1)} %get-tuple-element.32, f32[32,1024]{1,0:T(8,128)S(1)} %get-tuple-element.31), kind=kLoop, calls=%fused_computation.1 | loop fusion | flops 196608 | bytes 655360 | tf_op jit(solution)/shard_map/convert_element_type | solution.py:441
  (39 shorter events, 2.0 us)
Async XLA Ops:
  4.6 5.3 %collective-permute-start = (f32[72,256]{1,0:T(8,128)S(1)}, f32[72,256]{1,0:T(8,128)S(1)}, u32[]{:S(2)}, u32[]{:S(2)}) collective-permute-start(f32[72,256]{1,0:T(8,128)S(1)} %shard_map.136.one_ref), channel_id=1, source_target_pairs={{0,4},{4,0},{8,12},{12,8},{16,20},{20,16},{24,28},{28,24},{1,5},{5... | collective-permute-start | bytes 221192 | tf_op jit(solution)/shard_map/ppermute | solution.py:325
  10.2 4.5 %collective-permute-start.1 = (f32[72,256]{1,0:T(8,128)S(1)}, f32[72,256]{1,0:T(8,128)S(1)}, u32[]{:S(2)}, u32[]{:S(2)}) collective-permute-start(f32[72,256]{1,0:T(8,128)S(1)} %shard_map.137.after_ref.one_ref), channel_id=1, source_target_pairs={{0,8},{4,12},{8,0},{12,4},{16,24},{20,28},{24,16},{28,20},{1,9},{5... | collective-permute-start | bytes 221192 | tf_op jit(solution)/shard_map/ppermute | solution.py:325
  15.0 5.4 %copy-start = (bf16[256,1024]{1,0:T(8,128)(2,1)S(1)}, bf16[256,1024]{1,0:T(8,128)(2,1)}, u32[]{:S(2)}) copy-start(bf16[256,1024]{1,0:T(8,128)(2,1)} %w_ref.1) | copy-start | bytes 1572868
  15.0 5.4 %collective-permute-start.2 = (f32[72,256]{1,0:T(8,128)S(1)}, f32[72,256]{1,0:T(8,128)S(1)}, u32[]{:S(2)}, u32[]{:S(2)}) collective-permute-start(f32[72,256]{1,0:T(8,128)S(1)} %shard_map.139.after_ref.one_ref), channel_id=1, source_target_pairs={{0,16},{4,20},{8,24},{12,28},{16,0},{20,4},{24,8},{28,12},{1,17},{... | collective-permute-start | bytes 221192 | tf_op jit(solution)/shard_map/ppermute | solution.py:325
  19.9 9.8 %copy-start.1 = (bf16[4,16,1024]{2,1,0:T(8,128)(2,1)S(1)}, bf16[4,16,1024]{2,1,0:T(8,128)(2,1)}, u32[]{:S(2)}) copy-start(bf16[4,16,1024]{2,1,0:T(8,128)(2,1)} %param.14) | copy-start | bytes 393220
  19.9 9.8 %copy-start.2 = (bf16[1024,16]{0,1:T(8,128)(2,1)S(1)}, bf16[1024,16]{0,1:T(8,128)(2,1)}, u32[]{:S(2)}) copy-start(bf16[1024,16]{0,1:T(8,128)(2,1)} %param.24) | copy-start | bytes 98308
  19.9 9.7 %copy-start.3 = (f32[1024]{0:T(1024)S(1)}, f32[1024]{0:T(1024)}, u32[]{:S(2)}) copy-start(f32[1024]{0:T(1024)} %param.21) | copy-start | bytes 12292
  19.9 9.7 %copy-start.4 = (s32[4,16,2]{1,2,0:T(2,128)S(1)}, s32[4,16,2]{1,2,0:T(2,128)}, u32[]{:S(2)}) copy-start(s32[4,16,2]{1,2,0:T(2,128)} %param.25) | copy-start | bytes 1540
  21.0 1.4 %collective-permute-start.3 = (f32[32,1024]{1,0:T(8,128)S(1)}, f32[32,1024]{1,0:T(8,128)S(1)}, u32[]{:S(2)}, u32[]{:S(2)}) collective-permute-start(f32[32,1024]{1,0:T(8,128)S(1)} %get-tuple-element.21), channel_id=1, source_target_pairs={{0,1},{1,0},{2,3},{3,2},{4,5},{5,4},{6,7},{7,6},{8,9},{9,8},{10,11... | collective-permute-start | bytes 393224 | tf_op jit(solution)/shard_map/ppermute | solution.py:325
  22.5 5.7 %collective-permute-start.4 = (f32[32,1024]{1,0:T(8,128)S(1)}, f32[32,1024]{1,0:T(8,128)S(1)}, u32[]{:S(2)}, u32[]{:S(2)}) collective-permute-start(f32[32,1024]{1,0:T(8,128)S(1)} %add.40.after_ref.one_ref), channel_id=1, source_target_pairs={{0,2},{1,3},{2,0},{3,1},{4,6},{5,7},{6,4},{7,5},{8,10},{9,11},{10,... | collective-permute-start | bytes 393224 | tf_op jit(solution)/shard_map/ppermute | solution.py:325
  28.2 1.4 %collective-permute-start.5 = (f32[32,1024]{1,0:T(8,128)S(1)}, f32[32,1024]{1,0:T(8,128)S(1)}, u32[]{:S(2)}, u32[]{:S(2)}) collective-permute-start(f32[32,1024]{1,0:T(8,128)S(1)} %shard_map.143.half_ref), channel_id=1, source_target_pairs={{0,1},{1,0},{2,3},{3,2},{4,5},{5,4},{6,7},{7,6},{8,9},{9,8},{10,11... | collective-permute-start | bytes 393224 | tf_op jit(solution)/shard_map/ppermute | solution.py:325
  32.9 1.3 %collective-permute-start.6 = (f32[32,512]{1,0:T(8,128)S(1)}, f32[32,512]{1,0:T(8,128)S(1)}, u32[]{:S(2)}, u32[]{:S(2)}) collective-permute-start(f32[32,512]{1,0:T(8,128)S(1)} %get-tuple-element.28), channel_id=1, source_target_pairs={{0,1},{1,0},{2,3},{3,2},{4,5},{5,4},{6,7},{7,6},{8,9},{9,8},{10,11... | collective-permute-start | bytes 196616 | tf_op jit(solution)/shard_map/ppermute | solution.py:325
  33.1 2.9 %collective-permute-start.11 = (f32[32,512]{1,0:T(8,128)S(1)}, f32[32,512]{1,0:T(8,128)S(1)}, u32[]{:S(2)}, u32[]{:S(2)}) collective-permute-start(f32[32,512]{1,0:T(8,128)S(1)} %get-tuple-element.30), channel_id=1, source_target_pairs={{0,1},{1,0},{2,3},{3,2},{4,5},{5,4},{6,7},{7,6},{8,9},{9,8},{10,11... | collective-permute-start | bytes 196616 | tf_op jit(solution)/shard_map/ppermute | solution.py:325
  34.2 4.3 %collective-permute-start.7 = (f32[32,512]{1,0:T(8,128)S(1)}, f32[32,512]{1,0:T(8,128)S(1)}, u32[]{:S(2)}, u32[]{:S(2)}) collective-permute-start(f32[32,512]{1,0:T(8,128)S(1)} %add.42), channel_id=1, source_target_pairs={{0,2},{1,3},{2,0},{3,1},{4,6},{5,7},{6,4},{7,5},{8,10},{9,11},{10,... | collective-permute-start | bytes 196616 | tf_op jit(solution)/shard_map/ppermute | solution.py:325
  36.0 4.5 %collective-permute-start.12 = (f32[32,512]{1,0:T(8,128)S(1)}, f32[32,512]{1,0:T(8,128)S(1)}, u32[]{:S(2)}, u32[]{:S(2)}) collective-permute-start(f32[32,512]{1,0:T(8,128)S(1)} %add.47), channel_id=1, source_target_pairs={{0,4},{4,0},{8,12},{12,8},{16,20},{20,16},{24,28},{28,24},{1,5},{5... | collective-permute-start | bytes 196616 | tf_op jit(solution)/shard_map/ppermute | solution.py:325
  38.6 4.3 %collective-permute-start.8 = (f32[32,512]{1,0:T(8,128)S(1)}, f32[32,512]{1,0:T(8,128)S(1)}, u32[]{:S(2)}, u32[]{:S(2)}) collective-permute-start(f32[32,512]{1,0:T(8,128)S(1)} %add.43), channel_id=1, source_target_pairs={{0,4},{4,0},{8,12},{12,8},{16,20},{20,16},{24,28},{28,24},{1,5},{5... | collective-permute-start | bytes 196616 | tf_op jit(solution)/shard_map/ppermute | solution.py:325
  40.6 4.3 %collective-permute-start.13 = (f32[32,512]{1,0:T(8,128)S(1)}, f32[32,512]{1,0:T(8,128)S(1)}, u32[]{:S(2)}, u32[]{:S(2)}) collective-permute-start(f32[32,512]{1,0:T(8,128)S(1)} %add.48), channel_id=1, source_target_pairs={{0,2},{1,3},{2,0},{3,1},{4,6},{5,7},{6,4},{7,5},{8,10},{9,11},{10,... | collective-permute-start | bytes 196616 | tf_op jit(solution)/shard_map/ppermute | solution.py:325
  42.9 5.2 %collective-permute-start.9 = (f32[32,512]{1,0:T(8,128)S(1)}, f32[32,512]{1,0:T(8,128)S(1)}, u32[]{:S(2)}, u32[]{:S(2)}) collective-permute-start(f32[32,512]{1,0:T(8,128)S(1)} %add.44), channel_id=1, source_target_pairs={{0,8},{4,12},{8,0},{12,4},{16,24},{20,28},{24,16},{28,20},{1,9},{5... | collective-permute-start | bytes 196616 | tf_op jit(solution)/shard_map/ppermute | solution.py:325
  44.9 6.9 %collective-permute-start.14 = (f32[32,512]{1,0:T(8,128)S(1)}, f32[32,512]{1,0:T(8,128)S(1)}, u32[]{:S(2)}, u32[]{:S(2)}) collective-permute-start(f32[32,512]{1,0:T(8,128)S(1)} %add.49), channel_id=1, source_target_pairs={{0,16},{4,20},{8,24},{12,28},{16,0},{20,4},{24,8},{28,12},{1,17},{... | collective-permute-start | bytes 196616 | tf_op jit(solution)/shard_map/ppermute | solution.py:325
  48.1 5.2 %collective-permute-start.10 = (f32[32,512]{1,0:T(8,128)S(1)}, f32[32,512]{1,0:T(8,128)S(1)}, u32[]{:S(2)}, u32[]{:S(2)}) collective-permute-start(f32[32,512]{1,0:T(8,128)S(1)} %add.45), channel_id=1, source_target_pairs={{0,16},{4,20},{8,24},{12,28},{16,0},{20,4},{24,8},{28,12},{1,17},{... | collective-permute-start | bytes 196616 | tf_op jit(solution)/shard_map/ppermute | solution.py:325
  51.8 4.3 %collective-permute-start.15 = (f32[32,512]{1,0:T(8,128)S(1)}, f32[32,512]{1,0:T(8,128)S(1)}, u32[]{:S(2)}, u32[]{:S(2)}) collective-permute-start(f32[32,512]{1,0:T(8,128)S(1)} %add.50), channel_id=1, source_target_pairs={{0,8},{4,12},{8,0},{12,4},{16,24},{20,28},{24,16},{28,20},{1,9},{5... | collective-permute-start | bytes 196616 | tf_op jit(solution)/shard_map/ppermute | solution.py:325
  53.4 2.9 %collective-permute-start.16 = (f32[32,512]{1,0:T(8,128)S(1)}, f32[32,512]{1,0:T(8,128)S(1)}, u32[]{:S(2)}, u32[]{:S(2)}) collective-permute-start(f32[32,512]{1,0:T(8,128)S(1)} %add.46), channel_id=1, source_target_pairs={{0,1},{1,0},{2,3},{3,2},{4,5},{5,4},{6,7},{7,6},{8,9},{9,8},{10,11... | collective-permute-start | bytes 196616 | tf_op jit(solution)/shard_map/ppermute | solution.py:325
  56.2 1.3 %collective-permute-start.17 = (f32[32,512]{1,0:T(8,128)S(1)}, f32[32,512]{1,0:T(8,128)S(1)}, u32[]{:S(2)}, u32[]{:S(2)}) collective-permute-start(f32[32,512]{1,0:T(8,128)S(1)} %add.51), channel_id=1, source_target_pairs={{0,1},{1,0},{2,3},{3,2},{4,5},{5,4},{6,7},{7,6},{8,9},{9,8},{10,11... | collective-permute-start | bytes 196616 | tf_op jit(solution)/shard_map/ppermute | solution.py:325

commit v8 on v7

--- a/solution.py
+++ b/solution.py
@@ -277,7 +277,8 @@
 
 
 def expert_kernel(
-    half_ref, back_ref, tokens_ref, gain_ref, router_ref, choice_ref, gate_ref, up_ref, down_ref, mid_ref, *sum_refs
+    half_ref, back_ref, tokens_ref, gain_ref, router_ref, choice_ref, gate_ref, up_ref, down_ref,
+    mid_ref, hidden_ref, keep_ref, give_ref,
 ):
     hidden_local = down_ref.shape[0]
     half = half_ref.shape[0]
@@ -301,17 +302,17 @@
     first = 1.0 / (1.0 + jnp.exp(chosen[1] - chosen[0]))
     second = 1.0 - first
     device = lax.axis_index("seq") * lax.axis_size("tp") + lax.axis_index("tp")
-    total = jnp.zeros(mid_ref.shape, F32)
-    for at, size in chunks_of(hidden_local, 256):
-        column_expert = (device * hidden_local + at + iota((1, size), 1)) // FF
-        coef = jnp.where(column_expert == choices[0], first, jnp.where(column_expert == choices[1], second, 0.0))
-        gate = dot_nt(moe_in, gate_ref[at : at + size, :])
-        up = dot_nt(moe_in, up_ref[at : at + size, :])
-        hidden = (jax.nn.gelu(gate, approximate=True) * up * coef).astype(BF16)
-        total = total + dot(hidden, down_ref[at : at + size, :])
-    columns = total.shape[1] // 2
-    for i in range(2):
-        store_halves(total[:, i * columns : (i + 1) * columns], 1, sum_refs[i], sum_refs[2 + i])
+    column_expert = (device * hidden_local + iota((1, hidden_local), 1)) // FF
+    coef = jnp.where(column_expert == choices[0], first, jnp.where(column_expert == choices[1], second, 0.0))
+    gate = dot_nt(moe_in, gate_ref[...])
+    up = dot_nt(moe_in, up_ref[...])
+    hidden = (jax.nn.gelu(gate, approximate=True) * up * coef).astype(BF16)
+    hidden_ref[...] = hidden
+    store_halves(dot(hidden, down_ref[:, : keep_ref.shape[1]]), 1, keep_ref, give_ref)
+
+
+def down_kernel(hidden_ref, down_ref, keep_ref, give_ref):
+    store_halves(dot(hidden_ref[...], down_ref[:, keep_ref.shape[1] :]), 1, keep_ref, give_ref)
 
 
 def device_bits(axis):
@@ -325,8 +326,7 @@
     return lax.ppermute(value, axis, [(i, i ^ flip) for i in range(lax.axis_size(axis))])
 
 
-def reduce_columns(keeps, gives, split, orders):
-    halves = [keep + swap(give, split) for keep, give in zip(keeps, gives)]
+def reduce_columns(halves, split, orders):
     for bits in zip(*orders):
         halves = [half + swap(half, bit) for half, bit in zip(halves, bits)]
     return halves, [swap(half, split) for half in halves]
@@ -429,12 +429,16 @@
     mine, other = half_sum, swap(half_sum, tp_bits[0])
 
     column_shape = ((half, width // 2), F32)
-    mid, *sums = call(expert_kernel, [((tokens, width), F32)] + [column_shape] * 4, [VMEM] * 9, 8)(
+    expert_shapes = [((tokens, width), F32), ((tokens, hidden_local), BF16), column_shape, column_shape]
+    mid, hidden, keep, give = call(expert_kernel, expert_shapes, [VMEM] * 9, 8)(
         mine, other, flat_in, moe_gain[None], router.T, expert_choice.transpose(0, 2, 1), *staged
     )
+    back = swap(give, tp_bits[0])
+    keep_two, give_two = call(down_kernel, [column_shape] * 2, [VMEM] * 2, 4)(hidden, staged[2])
+    blocks = [keep + back, keep_two + swap(give_two, tp_bits[0])]
     bits = tp_bits[1:] + seq_bits
     swapped = [bits[i ^ 1] if i ^ 1 < len(bits) else bits[i] for i in range(len(bits))]
-    mine, other = reduce_columns(sums[:2], sums[2:], tp_bits[0], (bits, swapped))
+    mine, other = reduce_columns(blocks, tp_bits[0], (bits, swapped))
     low = lax.axis_index("tp") % 2 == 0
     mine, other = jnp.concatenate(mine, axis=1), jnp.concatenate(other, axis=1)
     mixture = jnp.concatenate([jnp.where(low, mine, other), jnp.where(low, other, mine)])

time: 58.4 us -> 57.4 us (0.983)
  Pallas kernels: 14.3 us -> 13.7 us
    pallas_call x1 -> x2, Pallas kernels: 3.24 us -> 2.64 us  [the longest x1 2.27 us: on_device(): call(expert_kernel, expert_shapes, [VMEM] * 9, 8)]
  transfers between devices with their start and end apart: 18 -> 18, of which waited for: 15 -> 15; matrix products, arithmetic and copies ran while one was open for 0% -> 0% of each run, Pallas kernels for 9% -> 10%
where the time goes in v8:
time: 57.4 us; the launch traced here: 57.2 us
  starting transfers between devices  25.9 us (45%)
  waiting for transfers between devices  16.5 us (29%)
  Pallas kernels  13.7 us (24%)
  other arithmetic  0.84 us (1%)
    ppermute x18, starting transfers between devices, swap(): lax.ppermute(value, axis, [(i, i ^ flip) for i in range(lax.axis_size(axi...  25.9 us
    ppermute x18, waiting for transfers between devices, swap(): lax.ppermute(value, axis, [(i, i ^ flip) for i in range(lax.axis_size(axi...  16.5 us
    pallas_call x3, Pallas kernels, fetch(): call(functools.partial(fetch_kernel, index), [(shape, BF16), ((8, LANES),...  5.36 us
    pallas_call x1, Pallas kernels, on_device(): call(functools.partial(attend_kernel, steps, requests, heads), [(packed_s...  4.59 us
    pallas_call x1, Pallas kernels, on_device(): call(expert_kernel, expert_shapes, [VMEM] * 9, 8)  2.27 us
  transfers between devices with their start and end apart: 18, of which 15 were waited for; matrix products, arithmetic and copies ran while one was open for 0% of the time, Pallas kernels for 10%

profile of v8, /device:TPU:0, one launch (start us, length us, event | category | flops | bytes accessed | tf_op | source)
XLA Modules:
  0.0 57.2 jit_solution(492766540705927615)
XLA Ops:
  0.0 4.6 %shard_map.136.one_ref = f32[72,256]{1,0:T(8,128)S(1)} custom-call(s32[16]{0:T(128)} %len_hbm.1, bf16[64,1024]{1,0:T(8,128)(2,1)} %bitcast.6, f32[1024]{0:T(1024)} %gain_hbm.1, s32[2052]{0:T(1024)} %table_hbm.1, f32[4,32]{1,0:T(4,128)} %bitcast.11, bf16[3,1024,256]{2,1,0:T(8,128)(2,1)} %w_hbm.1, bf16[16,256,256]{2,1,0:T(8,128)(2,1)} %k_hbm.1, ...), custom_call_target="tpu_custom_call" | custom-call | tf_op jit(solution)/shard_map/pallas_call | solution.py:379
  4.6 3.0 %collective-permute-start = (f32[72,256]{1,0:T(8,128)S(1)}, f32[72,256]{1,0:T(8,128)S(1)}, u32[]{:S(2)}, u32[]{:S(2)}) collective-permute-start(f32[72,256]{1,0:T(8,128)S(1)} %shard_map.136.one_ref), channel_id=1, source_target_pairs={{0,4},{4,0},{8,12},{12,8},{16,20},{20,16},{24,28},{28,24},{1,5},{5... | collective-permute-start | bytes 221192 | tf_op jit(solution)/shard_map/ppermute | solution.py:326
  7.6 2.3 %collective-permute-done.two_ref = f32[72,256]{1,0:T(8,128)S(1)} collective-permute-done((f32[72,256]{1,0:T(8,128)S(1)}, f32[72,256]{1,0:T(8,128)S(1)}, u32[]{:S(2)}, u32[]{:S(2)}) %collective-permute-start) | collective-permute-done | bytes 73760 | tf_op jit(solution)/shard_map/ppermute | solution.py:326
  10.2 2.2 %collective-permute-start.1 = (f32[72,256]{1,0:T(8,128)S(1)}, f32[72,256]{1,0:T(8,128)S(1)}, u32[]{:S(2)}, u32[]{:S(2)}) collective-permute-start(f32[72,256]{1,0:T(8,128)S(1)} %shard_map.137.after_ref.one_ref), channel_id=1, source_target_pairs={{0,8},{4,12},{8,0},{12,4},{16,24},{20,28},{24,16},{28,20},{1,9},{5... | collective-permute-start | bytes 221192 | tf_op jit(solution)/shard_map/ppermute | solution.py:326
  12.4 1.8 %shard_map.138 = (bf16[1408,1024]{1,0:T(8,128)(2,1)S(1)}, f32[8,128]{1,0:T(8,128)S(1)}) custom-call(f32[72,256]{1,0:T(8,128)S(1)} %shard_map.137.after_ref.one_ref, bf16[2,1408,1024]{2,1,0:T(8,128)(2,1)} %weights_hbm.4), custom_call_target="tpu_custom_call" | custom-call | tf_op jit(solution)/shard_map/pallas_call | solution.py:270
  14.2 0.5 collective-permute-done.1.two_ref
  15.0 3.1 %collective-permute-start.2 = (f32[72,256]{1,0:T(8,128)S(1)}, f32[72,256]{1,0:T(8,128)S(1)}, u32[]{:S(2)}, u32[]{:S(2)}) collective-permute-start(f32[72,256]{1,0:T(8,128)S(1)} %shard_map.139.after_ref.one_ref), channel_id=1, source_target_pairs={{0,16},{4,20},{8,24},{12,28},{16,0},{20,4},{24,8},{28,12},{1,17},{... | collective-permute-start | bytes 221192 | tf_op jit(solution)/shard_map/ppermute | solution.py:326
  18.1 1.8 %shard_map.140 = (bf16[1408,1024]{1,0:T(8,128)(2,1)S(1)}, f32[8,128]{1,0:T(8,128)S(1)}) custom-call(f32[72,256]{1,0:T(8,128)S(1)} %shard_map.139.after_ref.one_ref, bf16[2,1408,1024]{2,1,0:T(8,128)(2,1)} %weights_hbm.4), custom_call_target="tpu_custom_call" | custom-call | tf_op jit(solution)/shard_map/pallas_call | solution.py:270
  19.9 0.5 collective-permute-done.2.two_ref
  20.4 0.6 %shard_map.141 = (f32[32,1024]{1,0:T(8,128)S(1)}, f32[32,1024]{1,0:T(8,128)S(1)}) custom-call(f32[72,256]{1,0:T(8,128)S(1)} %shard_map.139.after_ref.one_ref, f32[72,256]{1,0:T(8,128)S(1)} %collective-permute-done.2.two_ref, bf16[256,1024]{1,0:T(8,128)(2,1)S(1)} %copy-done, f32[8,128]{1,0:T(8,128)S(1)} %get-tuple-element.20._), custom_call_target="tpu_custom_call" | custom-call | tf_op jit(solution)/shard_map/pallas_call | solution.py:418
  21.1 1.3 %collective-permute-done.3 = f32[32,1024]{1,0:T(8,128)S(1)} collective-permute-done((f32[32,1024]{1,0:T(8,128)S(1)}, f32[32,1024]{1,0:T(8,128)S(1)}, u32[]{:S(2)}, u32[]{:S(2)}) %collective-permute-start.3) | collective-permute-done | bytes 131104 | tf_op jit(solution)/shard_map/ppermute | solution.py:326
  22.5 1.9 %collective-permute-start.4 = (f32[32,1024]{1,0:T(8,128)S(1)}, f32[32,1024]{1,0:T(8,128)S(1)}, u32[]{:S(2)}, u32[]{:S(2)}) collective-permute-start(f32[32,1024]{1,0:T(8,128)S(1)} %add.40.after_ref.one_ref), channel_id=1, source_target_pairs={{0,2},{1,3},{2,0},{3,1},{4,6},{5,7},{6,4},{7,5},{8,10},{9,11},{10,... | collective-permute-start | bytes 393224 | tf_op jit(solution)/shard_map/ppermute | solution.py:326
  24.4 1.8 %shard_map.142 = (bf16[1408,1024]{1,0:T(8,128)(2,1)S(1)}, f32[8,128]{1,0:T(8,128)S(1)}) custom-call(f32[32,1024]{1,0:T(8,128)S(1)} %add.40.after_ref.one_ref, bf16[1408,1024]{1,0:T(8,128)(2,1)} %weights_hbm.5), custom_call_target="tpu_custom_call" | custom-call | tf_op jit(solution)/shard_map/pallas_call | solution.py:270
  26.2 2.0 %collective-permute-done.4.two_ref = f32[32,1024]{1,0:T(8,128)S(1)} collective-permute-done((f32[32,1024]{1,0:T(8,128)S(1)}, f32[32,1024]{1,0:T(8,128)S(1)}, u32[]{:S(2)}, u32[]{:S(2)}) %collective-permute-start.4) | collective-permute-done | bytes 131104 | tf_op jit(solution)/shard_map/ppermute | solution.py:326
  28.3 1.3 %collective-permute-done.5.back_ref = f32[32,1024]{1,0:T(8,128)S(1)} collective-permute-done((f32[32,1024]{1,0:T(8,128)S(1)}, f32[32,1024]{1,0:T(8,128)S(1)}, u32[]{:S(2)}, u32[]{:S(2)}) %collective-permute-start.5) | collective-permute-done | bytes 131104 | tf_op jit(solution)/shard_map/ppermute | solution.py:326
  29.6 2.3 %shard_map.144 = (f32[64,1024]{1,0:T(8,128)S(1)}, bf16[64,1408]{1,0:T(8,128)(2,1)S(1)}, f32[32,512]{1,0:T(8,128)S(1)}, f32[32,512]{1,0:T(8,128)S(1)}) custom-call(f32[32,1024]{1,0:T(8,128)S(1)} %shard_map.143.half_ref, f32[32,1024]{1,0:T(8,128)S(1)} %collective-permute-done.5.back_ref, bf16[64,1024]{1,0:T(8,128)(2,1)S(1)} %bitcast.7, f32[1,1024]{1,0:T(1,128)S(1)} %bitcast.9, ...), custom_call_target="tpu_custom_call" | custom-call | tf_op jit(solution)/shard_map/pallas_call | solution.py:433
  32.5 0.4 collective-permute-start.11
  33.2 1.8 %collective-permute-start.7 = (f32[32,512]{1,0:T(8,128)S(1)}, f32[32,512]{1,0:T(8,128)S(1)}, u32[]{:S(2)}, u32[]{:S(2)}) collective-permute-start(f32[32,512]{1,0:T(8,128)S(1)} %add.42), channel_id=1, source_target_pairs={{0,2},{1,3},{2,0},{3,1},{4,6},{5,7},{6,4},{7,5},{8,10},{9,11},{10,... | collective-permute-start | bytes 196616 | tf_op jit(solution)/shard_map/ppermute | solution.py:326
  35.1 1.6 %collective-permute-start.12 = (f32[32,512]{1,0:T(8,128)S(1)}, f32[32,512]{1,0:T(8,128)S(1)}, u32[]{:S(2)}, u32[]{:S(2)}) collective-permute-start(f32[32,512]{1,0:T(8,128)S(1)} %add.47), channel_id=1, source_target_pairs={{0,4},{4,0},{8,12},{12,8},{16,20},{20,16},{24,28},{28,24},{1,5},{5... | collective-permute-start | bytes 196616 | tf_op jit(solution)/shard_map/ppermute | solution.py:326
  36.6 1.0 %collective-permute-done.7 = f32[32,512]{1,0:T(8,128)S(1)} collective-permute-done((f32[32,512]{1,0:T(8,128)S(1)}, f32[32,512]{1,0:T(8,128)S(1)}, u32[]{:S(2)}, u32[]{:S(2)}) %collective-permute-start.7) | collective-permute-done | bytes 65568 | tf_op jit(solution)/shard_map/ppermute | solution.py:326
  37.6 1.8 %collective-permute-start.8 = (f32[32,512]{1,0:T(8,128)S(1)}, f32[32,512]{1,0:T(8,128)S(1)}, u32[]{:S(2)}, u32[]{:S(2)}) collective-permute-start(f32[32,512]{1,0:T(8,128)S(1)} %add.43), channel_id=1, source_target_pairs={{0,4},{4,0},{8,12},{12,8},{16,20},{20,16},{24,28},{28,24},{1,5},{5... | collective-permute-start | bytes 196616 | tf_op jit(solution)/shard_map/ppermute | solution.py:326
  39.6 1.4 %collective-permute-start.13 = (f32[32,512]{1,0:T(8,128)S(1)}, f32[32,512]{1,0:T(8,128)S(1)}, u32[]{:S(2)}, u32[]{:S(2)}) collective-permute-start(f32[32,512]{1,0:T(8,128)S(1)} %add.48), channel_id=1, source_target_pairs={{0,2},{1,3},{2,0},{3,1},{4,6},{5,7},{6,4},{7,5},{8,10},{9,11},{10,... | collective-permute-start | bytes 196616 | tf_op jit(solution)/shard_map/ppermute | solution.py:326
  41.0 1.0 %collective-permute-done.8 = f32[32,512]{1,0:T(8,128)S(1)} collective-permute-done((f32[32,512]{1,0:T(8,128)S(1)}, f32[32,512]{1,0:T(8,128)S(1)}, u32[]{:S(2)}, u32[]{:S(2)}) %collective-permute-start.8) | collective-permute-done | bytes 65568 | tf_op jit(solution)/shard_map/ppermute | solution.py:326
  41.9 1.9 %collective-permute-start.9 = (f32[32,512]{1,0:T(8,128)S(1)}, f32[32,512]{1,0:T(8,128)S(1)}, u32[]{:S(2)}, u32[]{:S(2)}) collective-permute-start(f32[32,512]{1,0:T(8,128)S(1)} %add.44), channel_id=1, source_target_pairs={{0,8},{4,12},{8,0},{12,4},{16,24},{20,28},{24,16},{28,20},{1,9},{5... | collective-permute-start | bytes 196616 | tf_op jit(solution)/shard_map/ppermute | solution.py:326
  44.0 3.2 %collective-permute-start.14 = (f32[32,512]{1,0:T(8,128)S(1)}, f32[32,512]{1,0:T(8,128)S(1)}, u32[]{:S(2)}, u32[]{:S(2)}) collective-permute-start(f32[32,512]{1,0:T(8,128)S(1)} %add.49), channel_id=1, source_target_pairs={{0,16},{4,20},{8,24},{12,28},{16,0},{20,4},{24,8},{28,12},{1,17},{... | collective-permute-start | bytes 196616 | tf_op jit(solution)/shard_map/ppermute | solution.py:326
  47.2 2.2 %collective-permute-start.10 = (f32[32,512]{1,0:T(8,128)S(1)}, f32[32,512]{1,0:T(8,128)S(1)}, u32[]{:S(2)}, u32[]{:S(2)}) collective-permute-start(f32[32,512]{1,0:T(8,128)S(1)} %add.45), channel_id=1, source_target_pairs={{0,16},{4,20},{8,24},{12,28},{16,0},{20,4},{24,8},{28,12},{1,17},{... | collective-permute-start | bytes 196616 | tf_op jit(solution)/shard_map/ppermute | solution.py:326
  49.4 1.4 %collective-permute-done.14 = f32[32,512]{1,0:T(8,128)S(1)} collective-permute-done((f32[32,512]{1,0:T(8,128)S(1)}, f32[32,512]{1,0:T(8,128)S(1)}, u32[]{:S(2)}, u32[]{:S(2)}) %collective-permute-start.14) | collective-permute-done | bytes 65568 | tf_op jit(solution)/shard_map/ppermute | solution.py:326
  50.8 1.1 %collective-permute-start.15 = (f32[32,512]{1,0:T(8,128)S(1)}, f32[32,512]{1,0:T(8,128)S(1)}, u32[]{:S(2)}, u32[]{:S(2)}) collective-permute-start(f32[32,512]{1,0:T(8,128)S(1)} %add.50), channel_id=1, source_target_pairs={{0,8},{4,12},{8,0},{12,4},{16,24},{20,28},{24,16},{28,20},{1,9},{5... | collective-permute-start | bytes 196616 | tf_op jit(solution)/shard_map/ppermute | solution.py:326
  51.9 0.5 collective-permute-done.10
  52.5 2.7 %collective-permute-done.15 = f32[32,512]{1,0:T(8,128)S(1)} collective-permute-done((f32[32,512]{1,0:T(8,128)S(1)}, f32[32,512]{1,0:T(8,128)S(1)}, u32[]{:S(2)}, u32[]{:S(2)}) %collective-permute-start.15) | collective-permute-done | bytes 65568 | tf_op jit(solution)/shard_map/ppermute | solution.py:326
  55.3 1.2 %collective-permute-done.17 = f32[32,512]{1,0:T(8,128)S(1)} collective-permute-done((f32[32,512]{1,0:T(8,128)S(1)}, f32[32,512]{1,0:T(8,128)S(1)}, u32[]{:S(2)}, u32[]{:S(2)}) %collective-permute-start.17) | collective-permute-done | bytes 65568 | tf_op jit(solution)/shard_map/ppermute | solution.py:326
  56.5 0.7 %fusion = bf16[64,1024]{1,0:T(8,128)(2,1)} fusion(f32[64,1024]{1,0:T(8,128)S(1)} %get-tuple-element.27, f32[32,1024]{1,0:T(8,128)S(1)} %get-tuple-element.34, f32[32,1024]{1,0:T(8,128)S(1)} %get-tuple-element.33), kind=kLoop, calls=%fused_computation.1 | loop fusion | flops 196608 | bytes 655360 | tf_op jit(solution)/shard_map/convert_element_type | solution.py:445
  (40 shorter events, 2.3 us)
Async XLA Ops:
  4.6 5.3 %collective-permute-start = (f32[72,256]{1,0:T(8,128)S(1)}, f32[72,256]{1,0:T(8,128)S(1)}, u32[]{:S(2)}, u32[]{:S(2)}) collective-permute-start(f32[72,256]{1,0:T(8,128)S(1)} %shard_map.136.one_ref), channel_id=1, source_target_pairs={{0,4},{4,0},{8,12},{12,8},{16,20},{20,16},{24,28},{28,24},{1,5},{5... | collective-permute-start | bytes 221192 | tf_op jit(solution)/shard_map/ppermute | solution.py:326
  10.2 4.5 %collective-permute-start.1 = (f32[72,256]{1,0:T(8,128)S(1)}, f32[72,256]{1,0:T(8,128)S(1)}, u32[]{:S(2)}, u32[]{:S(2)}) collective-permute-start(f32[72,256]{1,0:T(8,128)S(1)} %shard_map.137.after_ref.one_ref), channel_id=1, source_target_pairs={{0,8},{4,12},{8,0},{12,4},{16,24},{20,28},{24,16},{28,20},{1,9},{5... | collective-permute-start | bytes 221192 | tf_op jit(solution)/shard_map/ppermute | solution.py:326
  15.0 5.4 %copy-start = (bf16[256,1024]{1,0:T(8,128)(2,1)S(1)}, bf16[256,1024]{1,0:T(8,128)(2,1)}, u32[]{:S(2)}) copy-start(bf16[256,1024]{1,0:T(8,128)(2,1)} %w_ref.1) | copy-start | bytes 1572868
  15.0 5.4 %collective-permute-start.2 = (f32[72,256]{1,0:T(8,128)S(1)}, f32[72,256]{1,0:T(8,128)S(1)}, u32[]{:S(2)}, u32[]{:S(2)}) collective-permute-start(f32[72,256]{1,0:T(8,128)S(1)} %shard_map.139.after_ref.one_ref), channel_id=1, source_target_pairs={{0,16},{4,20},{8,24},{12,28},{16,0},{20,4},{24,8},{28,12},{1,17},{... | collective-permute-start | bytes 221192 | tf_op jit(solution)/shard_map/ppermute | solution.py:326
  19.9 9.8 %copy-start.1 = (bf16[4,16,1024]{2,1,0:T(8,128)(2,1)S(1)}, bf16[4,16,1024]{2,1,0:T(8,128)(2,1)}, u32[]{:S(2)}) copy-start(bf16[4,16,1024]{2,1,0:T(8,128)(2,1)} %param.14) | copy-start | bytes 393220
  19.9 9.8 %copy-start.2 = (bf16[1024,16]{0,1:T(8,128)(2,1)S(1)}, bf16[1024,16]{0,1:T(8,128)(2,1)}, u32[]{:S(2)}) copy-start(bf16[1024,16]{0,1:T(8,128)(2,1)} %param.24) | copy-start | bytes 98308
  19.9 9.7 %copy-start.3 = (f32[1024]{0:T(1024)S(1)}, f32[1024]{0:T(1024)}, u32[]{:S(2)}) copy-start(f32[1024]{0:T(1024)} %param.21) | copy-start | bytes 12292
  19.9 9.7 %copy-start.4 = (s32[4,16,2]{1,2,0:T(2,128)S(1)}, s32[4,16,2]{1,2,0:T(2,128)}, u32[]{:S(2)}) copy-start(s32[4,16,2]{1,2,0:T(2,128)} %param.25) | copy-start | bytes 1540
  21.0 1.4 %collective-permute-start.3 = (f32[32,1024]{1,0:T(8,128)S(1)}, f32[32,1024]{1,0:T(8,128)S(1)}, u32[]{:S(2)}, u32[]{:S(2)}) collective-permute-start(f32[32,1024]{1,0:T(8,128)S(1)} %get-tuple-element.22), channel_id=1, source_target_pairs={{0,1},{1,0},{2,3},{3,2},{4,5},{5,4},{6,7},{7,6},{8,9},{9,8},{10,11... | collective-permute-start | bytes 393224 | tf_op jit(solution)/shard_map/ppermute | solution.py:326
  22.5 5.7 %collective-permute-start.4 = (f32[32,1024]{1,0:T(8,128)S(1)}, f32[32,1024]{1,0:T(8,128)S(1)}, u32[]{:S(2)}, u32[]{:S(2)}) collective-permute-start(f32[32,1024]{1,0:T(8,128)S(1)} %add.40.after_ref.one_ref), channel_id=1, source_target_pairs={{0,2},{1,3},{2,0},{3,1},{4,6},{5,7},{6,4},{7,5},{8,10},{9,11},{10,... | collective-permute-start | bytes 393224 | tf_op jit(solution)/shard_map/ppermute | solution.py:326
  28.2 1.4 %collective-permute-start.5 = (f32[32,1024]{1,0:T(8,128)S(1)}, f32[32,1024]{1,0:T(8,128)S(1)}, u32[]{:S(2)}, u32[]{:S(2)}) collective-permute-start(f32[32,1024]{1,0:T(8,128)S(1)} %shard_map.143.half_ref), channel_id=1, source_target_pairs={{0,1},{1,0},{2,3},{3,2},{4,5},{5,4},{6,7},{7,6},{8,9},{9,8},{10,11... | collective-permute-start | bytes 393224 | tf_op jit(solution)/shard_map/ppermute | solution.py:326
  31.9 1.3 %collective-permute-start.6 = (f32[32,512]{1,0:T(8,128)S(1)}, f32[32,512]{1,0:T(8,128)S(1)}, u32[]{:S(2)}, u32[]{:S(2)}) collective-permute-start(f32[32,512]{1,0:T(8,128)S(1)} %get-tuple-element.29), channel_id=1, source_target_pairs={{0,1},{1,0},{2,3},{3,2},{4,5},{5,4},{6,7},{7,6},{8,9},{9,8},{10,11... | collective-permute-start | bytes 196616 | tf_op jit(solution)/shard_map/ppermute | solution.py:326
  32.5 2.6 %collective-permute-start.11 = (f32[32,512]{1,0:T(8,128)S(1)}, f32[32,512]{1,0:T(8,128)S(1)}, u32[]{:S(2)}, u32[]{:S(2)}) collective-permute-start(f32[32,512]{1,0:T(8,128)S(1)} %get-tuple-element.32), channel_id=1, source_target_pairs={{0,1},{1,0},{2,3},{3,2},{4,5},{5,4},{6,7},{7,6},{8,9},{9,8},{10,11... | collective-permute-start | bytes 196616 | tf_op jit(solution)/shard_map/ppermute | solution.py:326
  33.2 4.3 %collective-permute-start.7 = (f32[32,512]{1,0:T(8,128)S(1)}, f32[32,512]{1,0:T(8,128)S(1)}, u32[]{:S(2)}, u32[]{:S(2)}) collective-permute-start(f32[32,512]{1,0:T(8,128)S(1)} %add.42), channel_id=1, source_target_pairs={{0,2},{1,3},{2,0},{3,1},{4,6},{5,7},{6,4},{7,5},{8,10},{9,11},{10,... | collective-permute-start | bytes 196616 | tf_op jit(solution)/shard_map/ppermute | solution.py:326
  35.1 4.5 %collective-permute-start.12 = (f32[32,512]{1,0:T(8,128)S(1)}, f32[32,512]{1,0:T(8,128)S(1)}, u32[]{:S(2)}, u32[]{:S(2)}) collective-permute-start(f32[32,512]{1,0:T(8,128)S(1)} %add.47), channel_id=1, source_target_pairs={{0,4},{4,0},{8,12},{12,8},{16,20},{20,16},{24,28},{28,24},{1,5},{5... | collective-permute-start | bytes 196616 | tf_op jit(solution)/shard_map/ppermute | solution.py:326
  37.6 4.3 %collective-permute-start.8 = (f32[32,512]{1,0:T(8,128)S(1)}, f32[32,512]{1,0:T(8,128)S(1)}, u32[]{:S(2)}, u32[]{:S(2)}) collective-permute-start(f32[32,512]{1,0:T(8,128)S(1)} %add.43), channel_id=1, source_target_pairs={{0,4},{4,0},{8,12},{12,8},{16,20},{20,16},{24,28},{28,24},{1,5},{5... | collective-permute-start | bytes 196616 | tf_op jit(solution)/shard_map/ppermute | solution.py:326
  39.6 4.3 %collective-permute-start.13 = (f32[32,512]{1,0:T(8,128)S(1)}, f32[32,512]{1,0:T(8,128)S(1)}, u32[]{:S(2)}, u32[]{:S(2)}) collective-permute-start(f32[32,512]{1,0:T(8,128)S(1)} %add.48), channel_id=1, source_target_pairs={{0,2},{1,3},{2,0},{3,1},{4,6},{5,7},{6,4},{7,5},{8,10},{9,11},{10,... | collective-permute-start | bytes 196616 | tf_op jit(solution)/shard_map/ppermute | solution.py:326
  41.9 5.2 %collective-permute-start.9 = (f32[32,512]{1,0:T(8,128)S(1)}, f32[32,512]{1,0:T(8,128)S(1)}, u32[]{:S(2)}, u32[]{:S(2)}) collective-permute-start(f32[32,512]{1,0:T(8,128)S(1)} %add.44), channel_id=1, source_target_pairs={{0,8},{4,12},{8,0},{12,4},{16,24},{20,28},{24,16},{28,20},{1,9},{5... | collective-permute-start | bytes 196616 | tf_op jit(solution)/shard_map/ppermute | solution.py:326
  44.0 6.9 %collective-permute-start.14 = (f32[32,512]{1,0:T(8,128)S(1)}, f32[32,512]{1,0:T(8,128)S(1)}, u32[]{:S(2)}, u32[]{:S(2)}) collective-permute-start(f32[32,512]{1,0:T(8,128)S(1)} %add.49), channel_id=1, source_target_pairs={{0,16},{4,20},{8,24},{12,28},{16,0},{20,4},{24,8},{28,12},{1,17},{... | collective-permute-start | bytes 196616 | tf_op jit(solution)/shard_map/ppermute | solution.py:326
  47.2 5.2 %collective-permute-start.10 = (f32[32,512]{1,0:T(8,128)S(1)}, f32[32,512]{1,0:T(8,128)S(1)}, u32[]{:S(2)}, u32[]{:S(2)}) collective-permute-start(f32[32,512]{1,0:T(8,128)S(1)} %add.45), channel_id=1, source_target_pairs={{0,16},{4,20},{8,24},{12,28},{16,0},{20,4},{24,8},{28,12},{1,17},{... | collective-permute-start | bytes 196616 | tf_op jit(solution)/shard_map/ppermute | solution.py:326
  50.8 4.3 %collective-permute-start.15 = (f32[32,512]{1,0:T(8,128)S(1)}, f32[32,512]{1,0:T(8,128)S(1)}, u32[]{:S(2)}, u32[]{:S(2)}) collective-permute-start(f32[32,512]{1,0:T(8,128)S(1)} %add.50), channel_id=1, source_target_pairs={{0,8},{4,12},{8,0},{12,4},{16,24},{20,28},{24,16},{28,20},{1,9},{5... | collective-permute-start | bytes 196616 | tf_op jit(solution)/shard_map/ppermute | solution.py:326
  52.4 2.9 %collective-permute-start.16 = (f32[32,512]{1,0:T(8,128)S(1)}, f32[32,512]{1,0:T(8,128)S(1)}, u32[]{:S(2)}, u32[]{:S(2)}) collective-permute-start(f32[32,512]{1,0:T(8,128)S(1)} %add.46), channel_id=1, source_target_pairs={{0,1},{1,0},{2,3},{3,2},{4,5},{5,4},{6,7},{7,6},{8,9},{9,8},{10,11... | collective-permute-start | bytes 196616 | tf_op jit(solution)/shard_map/ppermute | solution.py:326
  55.2 1.3 %collective-permute-start.17 = (f32[32,512]{1,0:T(8,128)S(1)}, f32[32,512]{1,0:T(8,128)S(1)}, u32[]{:S(2)}, u32[]{:S(2)}) collective-permute-start(f32[32,512]{1,0:T(8,128)S(1)} %add.51), channel_id=1, source_target_pairs={{0,1},{1,0},{2,3},{3,2},{4,5},{5,4},{6,7},{7,6},{8,9},{9,8},{10,11... | collective-permute-start | bytes 196616 | tf_op jit(solution)/shard_map/ppermute | solution.py:326

commit v9 on v8

--- a/solution.py
+++ b/solution.py
@@ -128,8 +128,9 @@
     x = tokens_ref[...].astype(F32)
     normed = rms_scale(x, gain_ref[...]).astype(BF16)
     projected = []
+    for copy in w_copies:
+        copy.wait()
     for k in range(3):
-        w_copies[k].wait()
         projected.append(dot(normed, w_buf[k]).astype(BF16))
     queries, fresh_keys, fresh_values = projected
 
@@ -276,29 +277,41 @@
     )(after, in_hbm(weights))
 
 
+def own_half_kernel(half_ref, tokens_ref, gain_ref, choice_ref, mid_ref, moe_ref, picks_ref):
+    half = half_ref.shape[0]
+    steps, _, requests = choice_ref.shape
+    low = lax.axis_index("tp") % 2 == 0
+    tokens = jnp.where(low, tokens_ref[:half].astype(F32), tokens_ref[half:].astype(F32))
+    mid_ref[...] = tokens + half_ref[...]
+    moe_ref[...] = rms_scale(mid_ref[...], gain_ref[...]).astype(BF16)
+    own = iota((requests, 1), 0) == iota((1, requests), 1)
+    lane = iota((1, LANES), 1)
+    for t in range(steps):
+        columns = [
+            jnp.sum(jnp.where(own, choice_ref[t, pick : pick + 1, :].astype(F32), 0.0), axis=1, keepdims=True)
+            for pick in range(2)
+        ]
+        picks_ref[t * requests : (t + 1) * requests, :] = jnp.where(lane == 0, columns[0], columns[1])
+
+
 def expert_kernel(
-    half_ref, back_ref, tokens_ref, gain_ref, router_ref, choice_ref, gate_ref, up_ref, down_ref,
+    mid_own_ref, moe_own_ref, picks_ref, back_ref, tokens_ref, gain_ref, router_ref, gate_ref, up_ref, down_ref,
     mid_ref, hidden_ref, keep_ref, give_ref,
 ):
     hidden_local = down_ref.shape[0]
-    half = half_ref.shape[0]
-    steps, _, requests = choice_ref.shape
+    half = back_ref.shape[0]
     low = lax.axis_index("tp") % 2 == 0
-    mine, other = half_ref[...], back_ref[...]
-    mid_ref[:half] = tokens_ref[:half].astype(F32) + jnp.where(low, mine, other)
-    mid_ref[half:] = tokens_ref[half:].astype(F32) + jnp.where(low, other, mine)
-    moe_in = rms_scale(mid_ref[...], gain_ref[...]).astype(BF16)
+    mid_own, moe_own = mid_own_ref[...], moe_own_ref[...]
+    tokens = jnp.where(low, tokens_ref[half:].astype(F32), tokens_ref[:half].astype(F32))
+    mid_other = tokens + back_ref[...]
+    moe_other = rms_scale(mid_other, gain_ref[...]).astype(BF16)
+    mid_ref[:half] = jnp.where(low, mid_own, mid_other)
+    mid_ref[half:] = jnp.where(low, mid_other, mid_own)
+    moe_in = jnp.concatenate([jnp.where(low, moe_own, moe_other), jnp.where(low, moe_other, moe_own)], axis=0)
     logits = dot_nt(moe_in, router_ref[...])
     expert = iota((1, logits.shape[1]), 1)
-    own = iota((requests, 1), 0) == iota((1, requests), 1)
-    choices, chosen = [], []
-    for pick in range(2):
-        column = [
-            jnp.sum(jnp.where(own, choice_ref[t, pick : pick + 1, :].astype(F32), 0.0), axis=1, keepdims=True)
-            for t in range(steps)
-        ]
-        choices.append(jnp.concatenate(column, axis=0).astype(jnp.int32))
-        chosen.append(jnp.sum(jnp.where(expert == choices[pick], logits, 0.0), axis=1, keepdims=True))
+    choices = [picks_ref[:, pick : pick + 1].astype(jnp.int32) for pick in range(2)]
+    chosen = [jnp.sum(jnp.where(expert == choice, logits, 0.0), axis=1, keepdims=True) for choice in choices]
     first = 1.0 / (1.0 + jnp.exp(chosen[1] - chosen[0]))
     second = 1.0 - first
     device = lax.axis_index("seq") * lax.axis_size("tp") + lax.axis_index("tp")
@@ -426,12 +439,17 @@
             weights, token = fetch(half_sum, w_down)
             staged.append(weights)
         (half_sum,) = call(add_kernel, [half_shape], [VMEM] * 3, 1)(half_sum, other, token)
-    mine, other = half_sum, swap(half_sum, tp_bits[0])
+    other = swap(half_sum, tp_bits[0])
+    gain = moe_gain[None]
+    own_shapes = [half_shape, ((half, width), BF16), ((tokens, LANES), F32)]
+    mid_own, moe_own, picks = call(own_half_kernel, own_shapes, [VMEM] * 4, 2)(
+        half_sum, flat_in, gain, expert_choice.transpose(0, 2, 1)
+    )
 
     column_shape = ((half, width // 2), F32)
     expert_shapes = [((tokens, width), F32), ((tokens, hidden_local), BF16), column_shape, column_shape]
-    mid, hidden, keep, give = call(expert_kernel, expert_shapes, [VMEM] * 9, 8)(
-        mine, other, flat_in, moe_gain[None], router.T, expert_choice.transpose(0, 2, 1), *staged
+    mid, hidden, keep, give = call(expert_kernel, expert_shapes, [VMEM] * 10, 8)(
+        mid_own, moe_own, picks, other, flat_in, gain, router.T, *staged
     )
     back = swap(give, tp_bits[0])
     keep_two, give_two = call(down_kernel, [column_shape] * 2, [VMEM] * 2, 4)(hidden, staged[2])

time: 57.4 us -> 56.9 us (level)
    pallas_call x1 -> x2, Pallas kernels: 2.27 us -> 2.2 us  [the longest x1 2.07 us: on_device(): call(expert_kernel, expert_shapes, [VMEM] * 10, 8)]
where the time goes in v9:
time: 56.9 us; the launch traced here: 56.6 us
  starting transfers between devices  25.9 us (46%)
  waiting for transfers between devices  16.3 us (29%)
  Pallas kernels  13.3 us (23%)
  other arithmetic  0.84 us (1%)
    ppermute x18, starting transfers between devices, swap(): lax.ppermute(value, axis, [(i, i ^ flip) for i in range(lax.axis_size(axi...  25.9 us
    ppermute x18, waiting for transfers between devices, swap(): lax.ppermute(value, axis, [(i, i ^ flip) for i in range(lax.axis_size(axi...  16.3 us
    pallas_call x3, Pallas kernels, fetch(): call(functools.partial(fetch_kernel, index), [(shape, BF16), ((8, LANES),...  5.36 us
    pallas_call x1, Pallas kernels, on_device(): call(functools.partial(attend_kernel, steps, requests, heads), [(packed_s...  4.22 us
    pallas_call x1, Pallas kernels, on_device(): call(expert_kernel, expert_shapes, [VMEM] * 10, 8)  2.07 us
  transfers between devices with their start and end apart: 18, of which 15 were waited for; matrix products, arithmetic and copies ran while one was open for 0% of the time, Pallas kernels for 10%

profile of v9, /device:TPU:0, one launch (start us, length us, event | category | flops | bytes accessed | tf_op | source)
XLA Modules:
  0.0 56.6 jit_solution(5098661256754556559)
XLA Ops:
  0.0 4.2 %shard_map.136.one_ref = f32[72,256]{1,0:T(8,128)S(1)} custom-call(s32[16]{0:T(128)} %len_hbm.1, bf16[64,1024]{1,0:T(8,128)(2,1)} %bitcast.6, f32[1024]{0:T(1024)} %gain_hbm.1, s32[2052]{0:T(1024)} %table_hbm.1, f32[4,32]{1,0:T(4,128)} %bitcast.13, bf16[3,1024,256]{2,1,0:T(8,128)(2,1)} %w_hbm.1, bf16[16,256,256]{2,1,0:T(8,128)(2,1)} %k_hbm.1, ...), custom_call_target="tpu_custom_call" | custom-call | tf_op jit(solution)/shard_map/pallas_call | solution.py:392
  4.2 3.0 %collective-permute-start = (f32[72,256]{1,0:T(8,128)S(1)}, f32[72,256]{1,0:T(8,128)S(1)}, u32[]{:S(2)}, u32[]{:S(2)}) collective-permute-start(f32[72,256]{1,0:T(8,128)S(1)} %shard_map.136.one_ref), channel_id=1, source_target_pairs={{0,4},{4,0},{8,12},{12,8},{16,20},{20,16},{24,28},{28,24},{1,5},{5... | collective-permute-start | bytes 221192 | tf_op jit(solution)/shard_map/ppermute | solution.py:339
  7.2 2.3 %collective-permute-done.two_ref = f32[72,256]{1,0:T(8,128)S(1)} collective-permute-done((f32[72,256]{1,0:T(8,128)S(1)}, f32[72,256]{1,0:T(8,128)S(1)}, u32[]{:S(2)}, u32[]{:S(2)}) %collective-permute-start) | collective-permute-done | bytes 73760 | tf_op jit(solution)/shard_map/ppermute | solution.py:339
  9.8 2.2 %collective-permute-start.1 = (f32[72,256]{1,0:T(8,128)S(1)}, f32[72,256]{1,0:T(8,128)S(1)}, u32[]{:S(2)}, u32[]{:S(2)}) collective-permute-start(f32[72,256]{1,0:T(8,128)S(1)} %shard_map.137.after_ref.one_ref), channel_id=1, source_target_pairs={{0,8},{4,12},{8,0},{12,4},{16,24},{20,28},{24,16},{28,20},{1,9},{5... | collective-permute-start | bytes 221192 | tf_op jit(solution)/shard_map/ppermute | solution.py:339
  12.0 1.8 %shard_map.138 = (bf16[1408,1024]{1,0:T(8,128)(2,1)S(1)}, f32[8,128]{1,0:T(8,128)S(1)}) custom-call(f32[72,256]{1,0:T(8,128)S(1)} %shard_map.137.after_ref.one_ref, bf16[2,1408,1024]{2,1,0:T(8,128)(2,1)} %weights_hbm.4), custom_call_target="tpu_custom_call" | custom-call | tf_op jit(solution)/shard_map/pallas_call | solution.py:271
  13.8 0.5 collective-permute-done.1.two_ref
  14.6 3.1 %collective-permute-start.2 = (f32[72,256]{1,0:T(8,128)S(1)}, f32[72,256]{1,0:T(8,128)S(1)}, u32[]{:S(2)}, u32[]{:S(2)}) collective-permute-start(f32[72,256]{1,0:T(8,128)S(1)} %shard_map.139.after_ref.one_ref), channel_id=1, source_target_pairs={{0,16},{4,20},{8,24},{12,28},{16,0},{20,4},{24,8},{28,12},{1,17},{... | collective-permute-start | bytes 221192 | tf_op jit(solution)/shard_map/ppermute | solution.py:339
  17.7 1.8 %shard_map.140 = (bf16[1408,1024]{1,0:T(8,128)(2,1)S(1)}, f32[8,128]{1,0:T(8,128)S(1)}) custom-call(f32[72,256]{1,0:T(8,128)S(1)} %shard_map.139.after_ref.one_ref, bf16[2,1408,1024]{2,1,0:T(8,128)(2,1)} %weights_hbm.4), custom_call_target="tpu_custom_call" | custom-call | tf_op jit(solution)/shard_map/pallas_call | solution.py:271
  19.5 0.5 collective-permute-done.2.two_ref
  20.0 0.6 %shard_map.141 = (f32[32,1024]{1,0:T(8,128)S(1)}, f32[32,1024]{1,0:T(8,128)S(1)}) custom-call(f32[72,256]{1,0:T(8,128)S(1)} %shard_map.139.after_ref.one_ref, f32[72,256]{1,0:T(8,128)S(1)} %collective-permute-done.2.two_ref, bf16[256,1024]{1,0:T(8,128)(2,1)S(1)} %copy-done.1, f32[8,128]{1,0:T(8,128)S(1)} %get-tuple-element.23._), custom_call_target="tpu_custom_call" | custom-call | tf_op jit(solution)/shard_map/pallas_call | solution.py:431
  20.7 1.3 %collective-permute-done.3 = f32[32,1024]{1,0:T(8,128)S(1)} collective-permute-done((f32[32,1024]{1,0:T(8,128)S(1)}, f32[32,1024]{1,0:T(8,128)S(1)}, u32[]{:S(2)}, u32[]{:S(2)}) %collective-permute-start.3) | collective-permute-done | bytes 131104 | tf_op jit(solution)/shard_map/ppermute | solution.py:339
  22.1 1.9 %collective-permute-start.4 = (f32[32,1024]{1,0:T(8,128)S(1)}, f32[32,1024]{1,0:T(8,128)S(1)}, u32[]{:S(2)}, u32[]{:S(2)}) collective-permute-start(f32[32,1024]{1,0:T(8,128)S(1)} %add.40.after_ref.one_ref), channel_id=1, source_target_pairs={{0,2},{1,3},{2,0},{3,1},{4,6},{5,7},{6,4},{7,5},{8,10},{9,11},{10,... | collective-permute-start | bytes 393224 | tf_op jit(solution)/shard_map/ppermute | solution.py:339
  24.0 1.8 %shard_map.142 = (bf16[1408,1024]{1,0:T(8,128)(2,1)S(1)}, f32[8,128]{1,0:T(8,128)S(1)}) custom-call(f32[32,1024]{1,0:T(8,128)S(1)} %add.40.after_ref.one_ref, bf16[1408,1024]{1,0:T(8,128)(2,1)} %weights_hbm.5), custom_call_target="tpu_custom_call" | custom-call | tf_op jit(solution)/shard_map/pallas_call | solution.py:271
  25.8 2.0 %collective-permute-done.4.two_ref = f32[32,1024]{1,0:T(8,128)S(1)} collective-permute-done((f32[32,1024]{1,0:T(8,128)S(1)}, f32[32,1024]{1,0:T(8,128)S(1)}, u32[]{:S(2)}, u32[]{:S(2)}) %collective-permute-start.4) | collective-permute-done | bytes 131104 | tf_op jit(solution)/shard_map/ppermute | solution.py:339
  28.1 1.2 %collective-permute-done.5.back_ref = f32[32,1024]{1,0:T(8,128)S(1)} collective-permute-done((f32[32,1024]{1,0:T(8,128)S(1)}, f32[32,1024]{1,0:T(8,128)S(1)}, u32[]{:S(2)}, u32[]{:S(2)}) %collective-permute-start.5) | collective-permute-done | bytes 131104 | tf_op jit(solution)/shard_map/ppermute | solution.py:339
  29.2 2.1 %shard_map.145 = (f32[64,1024]{1,0:T(8,128)S(1)}, bf16[64,1408]{1,0:T(8,128)(2,1)S(1)}, f32[32,512]{1,0:T(8,128)S(1)}, f32[32,512]{1,0:T(8,128)S(1)}) custom-call(f32[32,1024]{1,0:T(8,128)S(1)} %get-tuple-element.27.mid_own_ref, bf16[32,1024]{1,0:T(8,128)(2,1)S(1)} %get-tuple-element.28.moe_own_ref, f32[64,128]{1,0:T(8,128)S(1)} %get-tuple-element.29.picks_ref, ...), custom_call_target="tpu_custom_call" | custom-call | tf_op jit(solution)/shard_map/pallas_call | solution.py:451
  31.9 0.4 collective-permute-start.11
  32.7 1.8 %collective-permute-start.7 = (f32[32,512]{1,0:T(8,128)S(1)}, f32[32,512]{1,0:T(8,128)S(1)}, u32[]{:S(2)}, u32[]{:S(2)}) collective-permute-start(f32[32,512]{1,0:T(8,128)S(1)} %add.42), channel_id=1, source_target_pairs={{0,2},{1,3},{2,0},{3,1},{4,6},{5,7},{6,4},{7,5},{8,10},{9,11},{10,... | collective-permute-start | bytes 196616 | tf_op jit(solution)/shard_map/ppermute | solution.py:339
  34.5 1.6 %collective-permute-start.12 = (f32[32,512]{1,0:T(8,128)S(1)}, f32[32,512]{1,0:T(8,128)S(1)}, u32[]{:S(2)}, u32[]{:S(2)}) collective-permute-start(f32[32,512]{1,0:T(8,128)S(1)} %add.47), channel_id=1, source_target_pairs={{0,4},{4,0},{8,12},{12,8},{16,20},{20,16},{24,28},{28,24},{1,5},{5... | collective-permute-start | bytes 196616 | tf_op jit(solution)/shard_map/ppermute | solution.py:339
  36.0 1.0 %collective-permute-done.7 = f32[32,512]{1,0:T(8,128)S(1)} collective-permute-done((f32[32,512]{1,0:T(8,128)S(1)}, f32[32,512]{1,0:T(8,128)S(1)}, u32[]{:S(2)}, u32[]{:S(2)}) %collective-permute-start.7) | collective-permute-done | bytes 65568 | tf_op jit(solution)/shard_map/ppermute | solution.py:339
  37.0 1.8 %collective-permute-start.8 = (f32[32,512]{1,0:T(8,128)S(1)}, f32[32,512]{1,0:T(8,128)S(1)}, u32[]{:S(2)}, u32[]{:S(2)}) collective-permute-start(f32[32,512]{1,0:T(8,128)S(1)} %add.43), channel_id=1, source_target_pairs={{0,4},{4,0},{8,12},{12,8},{16,20},{20,16},{24,28},{28,24},{1,5},{5... | collective-permute-start | bytes 196616 | tf_op jit(solution)/shard_map/ppermute | solution.py:339
  39.0 1.4 %collective-permute-start.13 = (f32[32,512]{1,0:T(8,128)S(1)}, f32[32,512]{1,0:T(8,128)S(1)}, u32[]{:S(2)}, u32[]{:S(2)}) collective-permute-start(f32[32,512]{1,0:T(8,128)S(1)} %add.48), channel_id=1, source_target_pairs={{0,2},{1,3},{2,0},{3,1},{4,6},{5,7},{6,4},{7,5},{8,10},{9,11},{10,... | collective-permute-start | bytes 196616 | tf_op jit(solution)/shard_map/ppermute | solution.py:339
  40.4 1.0 %collective-permute-done.8 = f32[32,512]{1,0:T(8,128)S(1)} collective-permute-done((f32[32,512]{1,0:T(8,128)S(1)}, f32[32,512]{1,0:T(8,128)S(1)}, u32[]{:S(2)}, u32[]{:S(2)}) %collective-permute-start.8) | collective-permute-done | bytes 65568 | tf_op jit(solution)/shard_map/ppermute | solution.py:339
  41.3 1.9 %collective-permute-start.9 = (f32[32,512]{1,0:T(8,128)S(1)}, f32[32,512]{1,0:T(8,128)S(1)}, u32[]{:S(2)}, u32[]{:S(2)}) collective-permute-start(f32[32,512]{1,0:T(8,128)S(1)} %add.44), channel_id=1, source_target_pairs={{0,8},{4,12},{8,0},{12,4},{16,24},{20,28},{24,16},{28,20},{1,9},{5... | collective-permute-start | bytes 196616 | tf_op jit(solution)/shard_map/ppermute | solution.py:339
  43.4 3.2 %collective-permute-start.14 = (f32[32,512]{1,0:T(8,128)S(1)}, f32[32,512]{1,0:T(8,128)S(1)}, u32[]{:S(2)}, u32[]{:S(2)}) collective-permute-start(f32[32,512]{1,0:T(8,128)S(1)} %add.49), channel_id=1, source_target_pairs={{0,16},{4,20},{8,24},{12,28},{16,0},{20,4},{24,8},{28,12},{1,17},{... | collective-permute-start | bytes 196616 | tf_op jit(solution)/shard_map/ppermute | solution.py:339
  46.6 2.2 %collective-permute-start.10 = (f32[32,512]{1,0:T(8,128)S(1)}, f32[32,512]{1,0:T(8,128)S(1)}, u32[]{:S(2)}, u32[]{:S(2)}) collective-permute-start(f32[32,512]{1,0:T(8,128)S(1)} %add.45), channel_id=1, source_target_pairs={{0,16},{4,20},{8,24},{12,28},{16,0},{20,4},{24,8},{28,12},{1,17},{... | collective-permute-start | bytes 196616 | tf_op jit(solution)/shard_map/ppermute | solution.py:339
  48.8 1.4 %collective-permute-done.14 = f32[32,512]{1,0:T(8,128)S(1)} collective-permute-done((f32[32,512]{1,0:T(8,128)S(1)}, f32[32,512]{1,0:T(8,128)S(1)}, u32[]{:S(2)}, u32[]{:S(2)}) %collective-permute-start.14) | collective-permute-done | bytes 65568 | tf_op jit(solution)/shard_map/ppermute | solution.py:339
  50.3 1.1 %collective-permute-start.15 = (f32[32,512]{1,0:T(8,128)S(1)}, f32[32,512]{1,0:T(8,128)S(1)}, u32[]{:S(2)}, u32[]{:S(2)}) collective-permute-start(f32[32,512]{1,0:T(8,128)S(1)} %add.50), channel_id=1, source_target_pairs={{0,8},{4,12},{8,0},{12,4},{16,24},{20,28},{24,16},{28,20},{1,9},{5... | collective-permute-start | bytes 196616 | tf_op jit(solution)/shard_map/ppermute | solution.py:339
  51.3 0.5 collective-permute-done.10
  51.9 2.7 %collective-permute-done.15 = f32[32,512]{1,0:T(8,128)S(1)} collective-permute-done((f32[32,512]{1,0:T(8,128)S(1)}, f32[32,512]{1,0:T(8,128)S(1)}, u32[]{:S(2)}, u32[]{:S(2)}) %collective-permute-start.15) | collective-permute-done | bytes 65568 | tf_op jit(solution)/shard_map/ppermute | solution.py:339
  54.7 1.2 %collective-permute-done.17 = f32[32,512]{1,0:T(8,128)S(1)} collective-permute-done((f32[32,512]{1,0:T(8,128)S(1)}, f32[32,512]{1,0:T(8,128)S(1)}, u32[]{:S(2)}, u32[]{:S(2)}) %collective-permute-start.17) | collective-permute-done | bytes 65568 | tf_op jit(solution)/shard_map/ppermute | solution.py:339
  56.0 0.7 %fusion = bf16[64,1024]{1,0:T(8,128)(2,1)} fusion(f32[64,1024]{1,0:T(8,128)S(1)} %get-tuple-element.33, f32[32,1024]{1,0:T(8,128)S(1)} %get-tuple-element.40, f32[32,1024]{1,0:T(8,128)S(1)} %get-tuple-element.39), kind=kLoop, calls=%fused_computation.1 | loop fusion | flops 196608 | bytes 655360 | tf_op jit(solution)/shard_map/convert_element_type | solution.py:463
  (41 shorter events, 2.4 us)
Async XLA Ops:
  4.2 5.3 %collective-permute-start = (f32[72,256]{1,0:T(8,128)S(1)}, f32[72,256]{1,0:T(8,128)S(1)}, u32[]{:S(2)}, u32[]{:S(2)}) collective-permute-start(f32[72,256]{1,0:T(8,128)S(1)} %shard_map.136.one_ref), channel_id=1, source_target_pairs={{0,4},{4,0},{8,12},{12,8},{16,20},{20,16},{24,28},{28,24},{1,5},{5... | collective-permute-start | bytes 221192 | tf_op jit(solution)/shard_map/ppermute | solution.py:339
  9.8 4.5 %collective-permute-start.1 = (f32[72,256]{1,0:T(8,128)S(1)}, f32[72,256]{1,0:T(8,128)S(1)}, u32[]{:S(2)}, u32[]{:S(2)}) collective-permute-start(f32[72,256]{1,0:T(8,128)S(1)} %shard_map.137.after_ref.one_ref), channel_id=1, source_target_pairs={{0,8},{4,12},{8,0},{12,4},{16,24},{20,28},{24,16},{28,20},{1,9},{5... | collective-permute-start | bytes 221192 | tf_op jit(solution)/shard_map/ppermute | solution.py:339
  14.6 5.4 %copy-start.1 = (bf16[256,1024]{1,0:T(8,128)(2,1)S(1)}, bf16[256,1024]{1,0:T(8,128)(2,1)}, u32[]{:S(2)}) copy-start(bf16[256,1024]{1,0:T(8,128)(2,1)} %w_ref.1) | copy-start | bytes 1572868
  14.6 5.4 %collective-permute-start.2 = (f32[72,256]{1,0:T(8,128)S(1)}, f32[72,256]{1,0:T(8,128)S(1)}, u32[]{:S(2)}, u32[]{:S(2)}) collective-permute-start(f32[72,256]{1,0:T(8,128)S(1)} %shard_map.139.after_ref.one_ref), channel_id=1, source_target_pairs={{0,16},{4,20},{8,24},{12,28},{16,0},{20,4},{24,8},{28,12},{1,17},{... | collective-permute-start | bytes 221192 | tf_op jit(solution)/shard_map/ppermute | solution.py:339
  19.5 8.4 %copy-start = (bf16[4,16,1024]{2,1,0:T(8,128)(2,1)S(1)}, bf16[4,16,1024]{2,1,0:T(8,128)(2,1)}, u32[]{:S(2)}) copy-start(bf16[4,16,1024]{2,1,0:T(8,128)(2,1)} %param.14) | copy-start | bytes 393220
  19.5 8.4 %copy-start.3 = (f32[1024]{0:T(1024)S(1)}, f32[1024]{0:T(1024)}, u32[]{:S(2)}) copy-start(f32[1024]{0:T(1024)} %param.21) | copy-start | bytes 12292
  19.5 8.4 %copy-start.4 = (s32[4,16,2]{1,2,0:T(2,128)S(1)}, s32[4,16,2]{1,2,0:T(2,128)}, u32[]{:S(2)}) copy-start(s32[4,16,2]{1,2,0:T(2,128)} %param.25) | copy-start | bytes 1540
  19.5 9.7 %copy-start.2 = (bf16[1024,16]{0,1:T(8,128)(2,1)S(1)}, bf16[1024,16]{0,1:T(8,128)(2,1)}, u32[]{:S(2)}) copy-start(bf16[1024,16]{0,1:T(8,128)(2,1)} %param.24) | copy-start | bytes 98308
  20.7 1.4 %collective-permute-start.3 = (f32[32,1024]{1,0:T(8,128)S(1)}, f32[32,1024]{1,0:T(8,128)S(1)}, u32[]{:S(2)}, u32[]{:S(2)}) collective-permute-start(f32[32,1024]{1,0:T(8,128)S(1)} %get-tuple-element.25), channel_id=1, source_target_pairs={{0,1},{1,0},{2,3},{3,2},{4,5},{5,4},{6,7},{7,6},{8,9},{9,8},{10,11... | collective-permute-start | bytes 393224 | tf_op jit(solution)/shard_map/ppermute | solution.py:339
  22.1 5.7 %collective-permute-start.4 = (f32[32,1024]{1,0:T(8,128)S(1)}, f32[32,1024]{1,0:T(8,128)S(1)}, u32[]{:S(2)}, u32[]{:S(2)}) collective-permute-start(f32[32,1024]{1,0:T(8,128)S(1)} %add.40.after_ref.one_ref), channel_id=1, source_target_pairs={{0,2},{1,3},{2,0},{3,1},{4,6},{5,7},{6,4},{7,5},{8,10},{9,11},{10,... | collective-permute-start | bytes 393224 | tf_op jit(solution)/shard_map/ppermute | solution.py:339
  27.8 1.4 %collective-permute-start.5 = (f32[32,1024]{1,0:T(8,128)S(1)}, f32[32,1024]{1,0:T(8,128)S(1)}, u32[]{:S(2)}, u32[]{:S(2)}) collective-permute-start(f32[32,1024]{1,0:T(8,128)S(1)} %shard_map.143.half_ref), channel_id=1, source_target_pairs={{0,1},{1,0},{2,3},{3,2},{4,5},{5,4},{6,7},{7,6},{8,9},{9,8},{10,11... | collective-permute-start | bytes 393224 | tf_op jit(solution)/shard_map/ppermute | solution.py:339
  31.3 1.3 %collective-permute-start.6 = (f32[32,512]{1,0:T(8,128)S(1)}, f32[32,512]{1,0:T(8,128)S(1)}, u32[]{:S(2)}, u32[]{:S(2)}) collective-permute-start(f32[32,512]{1,0:T(8,128)S(1)} %get-tuple-element.35), channel_id=1, source_target_pairs={{0,1},{1,0},{2,3},{3,2},{4,5},{5,4},{6,7},{7,6},{8,9},{9,8},{10,11... | collective-permute-start | bytes 196616 | tf_op jit(solution)/shard_map/ppermute | solution.py:339
  31.9 2.5 %collective-permute-start.11 = (f32[32,512]{1,0:T(8,128)S(1)}, f32[32,512]{1,0:T(8,128)S(1)}, u32[]{:S(2)}, u32[]{:S(2)}) collective-permute-start(f32[32,512]{1,0:T(8,128)S(1)} %get-tuple-element.38), channel_id=1, source_target_pairs={{0,1},{1,0},{2,3},{3,2},{4,5},{5,4},{6,7},{7,6},{8,9},{9,8},{10,11... | collective-permute-start | bytes 196616 | tf_op jit(solution)/shard_map/ppermute | solution.py:339
  32.7 4.3 %collective-permute-start.7 = (f32[32,512]{1,0:T(8,128)S(1)}, f32[32,512]{1,0:T(8,128)S(1)}, u32[]{:S(2)}, u32[]{:S(2)}) collective-permute-start(f32[32,512]{1,0:T(8,128)S(1)} %add.42), channel_id=1, source_target_pairs={{0,2},{1,3},{2,0},{3,1},{4,6},{5,7},{6,4},{7,5},{8,10},{9,11},{10,... | collective-permute-start | bytes 196616 | tf_op jit(solution)/shard_map/ppermute | solution.py:339
  34.5 4.5 %collective-permute-start.12 = (f32[32,512]{1,0:T(8,128)S(1)}, f32[32,512]{1,0:T(8,128)S(1)}, u32[]{:S(2)}, u32[]{:S(2)}) collective-permute-start(f32[32,512]{1,0:T(8,128)S(1)} %add.47), channel_id=1, source_target_pairs={{0,4},{4,0},{8,12},{12,8},{16,20},{20,16},{24,28},{28,24},{1,5},{5... | collective-permute-start | bytes 196616 | tf_op jit(solution)/shard_map/ppermute | solution.py:339
  37.0 4.3 %collective-permute-start.8 = (f32[32,512]{1,0:T(8,128)S(1)}, f32[32,512]{1,0:T(8,128)S(1)}, u32[]{:S(2)}, u32[]{:S(2)}) collective-permute-start(f32[32,512]{1,0:T(8,128)S(1)} %add.43), channel_id=1, source_target_pairs={{0,4},{4,0},{8,12},{12,8},{16,20},{20,16},{24,28},{28,24},{1,5},{5... | collective-permute-start | bytes 196616 | tf_op jit(solution)/shard_map/ppermute | solution.py:339
  39.0 4.3 %collective-permute-start.13 = (f32[32,512]{1,0:T(8,128)S(1)}, f32[32,512]{1,0:T(8,128)S(1)}, u32[]{:S(2)}, u32[]{:S(2)}) collective-permute-start(f32[32,512]{1,0:T(8,128)S(1)} %add.48), channel_id=1, source_target_pairs={{0,2},{1,3},{2,0},{3,1},{4,6},{5,7},{6,4},{7,5},{8,10},{9,11},{10,... | collective-permute-start | bytes 196616 | tf_op jit(solution)/shard_map/ppermute | solution.py:339
  41.3 5.2 %collective-permute-start.9 = (f32[32,512]{1,0:T(8,128)S(1)}, f32[32,512]{1,0:T(8,128)S(1)}, u32[]{:S(2)}, u32[]{:S(2)}) collective-permute-start(f32[32,512]{1,0:T(8,128)S(1)} %add.44), channel_id=1, source_target_pairs={{0,8},{4,12},{8,0},{12,4},{16,24},{20,28},{24,16},{28,20},{1,9},{5... | collective-permute-start | bytes 196616 | tf_op jit(solution)/shard_map/ppermute | solution.py:339
  43.4 6.9 %collective-permute-start.14 = (f32[32,512]{1,0:T(8,128)S(1)}, f32[32,512]{1,0:T(8,128)S(1)}, u32[]{:S(2)}, u32[]{:S(2)}) collective-permute-start(f32[32,512]{1,0:T(8,128)S(1)} %add.49), channel_id=1, source_target_pairs={{0,16},{4,20},{8,24},{12,28},{16,0},{20,4},{24,8},{28,12},{1,17},{... | collective-permute-start | bytes 196616 | tf_op jit(solution)/shard_map/ppermute | solution.py:339
  46.6 5.2 %collective-permute-start.10 = (f32[32,512]{1,0:T(8,128)S(1)}, f32[32,512]{1,0:T(8,128)S(1)}, u32[]{:S(2)}, u32[]{:S(2)}) collective-permute-start(f32[32,512]{1,0:T(8,128)S(1)} %add.45), channel_id=1, source_target_pairs={{0,16},{4,20},{8,24},{12,28},{16,0},{20,4},{24,8},{28,12},{1,17},{... | collective-permute-start | bytes 196616 | tf_op jit(solution)/shard_map/ppermute | solution.py:339
  50.3 4.3 %collective-permute-start.15 = (f32[32,512]{1,0:T(8,128)S(1)}, f32[32,512]{1,0:T(8,128)S(1)}, u32[]{:S(2)}, u32[]{:S(2)}) collective-permute-start(f32[32,512]{1,0:T(8,128)S(1)} %add.50), channel_id=1, source_target_pairs={{0,8},{4,12},{8,0},{12,4},{16,24},{20,28},{24,16},{28,20},{1,9},{5... | collective-permute-start | bytes 196616 | tf_op jit(solution)/shard_map/ppermute | solution.py:339
  51.8 2.9 %collective-permute-start.16 = (f32[32,512]{1,0:T(8,128)S(1)}, f32[32,512]{1,0:T(8,128)S(1)}, u32[]{:S(2)}, u32[]{:S(2)}) collective-permute-start(f32[32,512]{1,0:T(8,128)S(1)} %add.46), channel_id=1, source_target_pairs={{0,1},{1,0},{2,3},{3,2},{4,5},{5,4},{6,7},{7,6},{8,9},{9,8},{10,11... | collective-permute-start | bytes 196616 | tf_op jit(solution)/shard_map/ppermute | solution.py:339
  54.6 1.3 %collective-permute-start.17 = (f32[32,512]{1,0:T(8,128)S(1)}, f32[32,512]{1,0:T(8,128)S(1)}, u32[]{:S(2)}, u32[]{:S(2)}) collective-permute-start(f32[32,512]{1,0:T(8,128)S(1)} %add.51), channel_id=1, source_target_pairs={{0,1},{1,0},{2,3},{3,2},{4,5},{5,4},{6,7},{7,6},{8,9},{9,8},{10,11... | collective-permute-start | bytes 196616 | tf_op jit(solution)/shard_map/ppermute | solution.py:339

commit v10 on v9

--- a/solution.py
+++ b/solution.py
@@ -52,7 +52,7 @@
 def attend_kernel(
     steps, requests, heads, len_hbm, tokens_hbm, gain_hbm, table_hbm, rel_hbm, w_hbm, k_hbm, v_hbm,
     out_ref, len_ref, tokens_ref, gain_ref, table_ref, rel_ref, w_buf, k_buf, v_buf,
-    bias_buf, score_buf, weight_buf, start_buf, step_buf, small_sem, w_sem, k_sem, v_sem,
+    bias_buf, score_buf, weight_buf, lane_buf, start_buf, step_buf, small_sem, w_sem, k_sem, v_sem,
 ):
     tokens = steps * requests
     group = steps * heads
@@ -166,23 +166,23 @@
     lane = iota((1, LANES), 1)
     stats = jnp.where(lane == row_head, top, jnp.where(lane == heads + row_head, total, 0.0))
     group_own = own_head[:group]
-    first = iota((8, 1), 0) < steps
 
     def folded(part):
         half = part[:8] + part[8:]
         return half + pltpu.roll(half, steps, 0)
 
-    stat_pairs = []
-    for pair in range(requests // 2):
-        sums, stat_parts = [], []
-        for r in (2 * pair, 2 * pair + 1):
-            at = slice(r * group, (r + 1) * group)
-            sums.append(folded(jnp.where(group_own, dot(weight_buf[at, :], v_buf[r]) + score_buf[at, :], 0.0)))
-            stat_parts.append(folded(stats[at]))
-        out_ref[8 * pair : 8 * pair + 8, :] = jnp.where(first, sums[0], sums[1])
-        stat_pairs.append(jnp.where(first, stat_parts[0], stat_parts[1]))
+    blocks_of_lanes = features // LANES
+    for r in range(requests):
+        at, rows_of = slice(r * group, (r + 1) * group), pl.ds(r, steps, requests)
+        own = jnp.where(group_own, dot(weight_buf[at, :], v_buf[r]) + score_buf[at, :], 0.0)
+        own = folded(own)[:steps]
+        for c in range(blocks_of_lanes):
+            lane_buf[c, rows_of, :] = own[:, c * LANES : (c + 1) * LANES]
+        lane_buf[blocks_of_lanes, rows_of, :] = folded(stats[at])[:steps]
+    for c in range(blocks_of_lanes):
+        out_ref[:tokens, c * LANES : (c + 1) * LANES] = lane_buf[c]
     out_ref[tokens:, :] = jnp.zeros((2 * heads, features), F32)
-    out_ref[tokens:, :LANES] = turned(jnp.concatenate(stat_pairs, axis=0))[: 2 * heads]
+    out_ref[tokens:, :LANES] = turned(lane_buf[blocks_of_lanes])[: 2 * heads]
 
 
 def turned(value):
@@ -234,14 +234,9 @@
     give_ref[...] = jnp.where(low, value[half:], value[:half])
 
 
-def project_kernel(steps, requests, one_ref, two_ref, w_ref, _, keep_ref, give_ref):
-    tokens = steps * requests
+def project_kernel(tokens, one_ref, two_ref, w_ref, _, keep_ref, give_ref):
     sums, _, totals = merge_parts(tokens, (one_ref, two_ref))
     attended = (sums / totals).astype(BF16)
-    row = iota((tokens, 1), 0)
-    source = modulo(row, requests) * steps + over(row, requests)
-    order = jnp.where(source == iota((1, tokens), 1), 1.0, 0.0).astype(BF16)
-    attended = dot(order, attended).astype(BF16)
     store_halves(dot(attended, w_ref[...]), 1, keep_ref, give_ref)
 
 
@@ -406,6 +401,7 @@
             pltpu.VMEM((rows, cache_rows), F32),
             pltpu.VMEM((rows, cache_rows), F32),
             pltpu.VMEM((rows, cache_rows), BF16),
+            pltpu.VMEM((features // LANES + 1, tokens, LANES), F32),
             pltpu.VMEM((buckets, LANES), jnp.int32),
             pltpu.VMEM((buckets, steps * heads, LANES), F32),
             dma((5,)),
@@ -429,7 +425,7 @@
             )
     half_shape = ((half, width), F32)
     keep, give = call(
-        functools.partial(project_kernel, steps, requests), [half_shape, half_shape], [VMEM] * 4, 4
+        functools.partial(project_kernel, tokens), [half_shape, half_shape], [VMEM] * 4, 4
     )(packed, other, w_out, token)
 
     half_sum = keep + swap(give, tp_bits[0])

time: 56.9 us -> 56.7 us (level)
  no operation moved by 1% of the time
where the time goes in v10:
time: 56.7 us; the launch traced here: 56.5 us
  starting transfers between devices  25.9 us (46%)
  waiting for transfers between devices  16.3 us (29%)
  Pallas kernels  13.1 us (23%)
  other arithmetic  0.84 us (1%)
    ppermute x18, starting transfers between devices, swap(): lax.ppermute(value, axis, [(i, i ^ flip) for i in range(lax.axis_size(axi...  25.9 us
    ppermute x18, waiting for transfers between devices, swap(): lax.ppermute(value, axis, [(i, i ^ flip) for i in range(lax.axis_size(axi...  16.3 us
    pallas_call x3, Pallas kernels, fetch(): call(functools.partial(fetch_kernel, index), [(shape, BF16), ((8, LANES),...  5.36 us
    pallas_call x1, Pallas kernels, on_device(): call(functools.partial(attend_kernel, steps, requests, heads), [(packed_s...  4.23 us
    pallas_call x1, Pallas kernels, on_device(): call(expert_kernel, expert_shapes, [VMEM] * 10, 8)  2.07 us
  transfers between devices with their start and end apart: 18, of which 15 were waited for; matrix products, arithmetic and copies ran while one was open for 0% of the time, Pallas kernels for 10%

profile of v10, /device:TPU:0, one launch (start us, length us, event | category | flops | bytes accessed | tf_op | source)
XLA Modules:
  0.0 56.5 jit_solution(5131240528131101840)
XLA Ops:
  0.0 4.2 %shard_map.136.one_ref = f32[72,256]{1,0:T(8,128)S(1)} custom-call(s32[16]{0:T(128)} %len_hbm.1, bf16[64,1024]{1,0:T(8,128)(2,1)} %bitcast.6, f32[1024]{0:T(1024)} %gain_hbm.1, s32[2052]{0:T(1024)} %table_hbm.1, f32[4,32]{1,0:T(4,128)} %bitcast.13, bf16[3,1024,256]{2,1,0:T(8,128)(2,1)} %w_hbm.1, bf16[16,256,256]{2,1,0:T(8,128)(2,1)} %k_hbm.1, ...), custom_call_target="tpu_custom_call" | custom-call | tf_op jit(solution)/shard_map/pallas_call | solution.py:387
  4.2 3.0 %collective-permute-start = (f32[72,256]{1,0:T(8,128)S(1)}, f32[72,256]{1,0:T(8,128)S(1)}, u32[]{:S(2)}, u32[]{:S(2)}) collective-permute-start(f32[72,256]{1,0:T(8,128)S(1)} %shard_map.136.one_ref), channel_id=1, source_target_pairs={{0,4},{4,0},{8,12},{12,8},{16,20},{20,16},{24,28},{28,24},{1,5},{5... | collective-permute-start | bytes 221192 | tf_op jit(solution)/shard_map/ppermute | solution.py:334
  7.2 2.3 %collective-permute-done.two_ref = f32[72,256]{1,0:T(8,128)S(1)} collective-permute-done((f32[72,256]{1,0:T(8,128)S(1)}, f32[72,256]{1,0:T(8,128)S(1)}, u32[]{:S(2)}, u32[]{:S(2)}) %collective-permute-start) | collective-permute-done | bytes 73760 | tf_op jit(solution)/shard_map/ppermute | solution.py:334
  9.8 2.2 %collective-permute-start.1 = (f32[72,256]{1,0:T(8,128)S(1)}, f32[72,256]{1,0:T(8,128)S(1)}, u32[]{:S(2)}, u32[]{:S(2)}) collective-permute-start(f32[72,256]{1,0:T(8,128)S(1)} %shard_map.137.after_ref.one_ref), channel_id=1, source_target_pairs={{0,8},{4,12},{8,0},{12,4},{16,24},{20,28},{24,16},{28,20},{1,9},{5... | collective-permute-start | bytes 221192 | tf_op jit(solution)/shard_map/ppermute | solution.py:334
  12.0 1.8 %shard_map.138 = (bf16[1408,1024]{1,0:T(8,128)(2,1)S(1)}, f32[8,128]{1,0:T(8,128)S(1)}) custom-call(f32[72,256]{1,0:T(8,128)S(1)} %shard_map.137.after_ref.one_ref, bf16[2,1408,1024]{2,1,0:T(8,128)(2,1)} %weights_hbm.4), custom_call_target="tpu_custom_call" | custom-call | tf_op jit(solution)/shard_map/pallas_call | solution.py:266
  13.8 0.5 collective-permute-done.1.two_ref
  14.6 3.1 %collective-permute-start.2 = (f32[72,256]{1,0:T(8,128)S(1)}, f32[72,256]{1,0:T(8,128)S(1)}, u32[]{:S(2)}, u32[]{:S(2)}) collective-permute-start(f32[72,256]{1,0:T(8,128)S(1)} %shard_map.139.after_ref.one_ref), channel_id=1, source_target_pairs={{0,16},{4,20},{8,24},{12,28},{16,0},{20,4},{24,8},{28,12},{1,17},{... | collective-permute-start | bytes 221192 | tf_op jit(solution)/shard_map/ppermute | solution.py:334
  17.7 1.8 %shard_map.140 = (bf16[1408,1024]{1,0:T(8,128)(2,1)S(1)}, f32[8,128]{1,0:T(8,128)S(1)}) custom-call(f32[72,256]{1,0:T(8,128)S(1)} %shard_map.139.after_ref.one_ref, bf16[2,1408,1024]{2,1,0:T(8,128)(2,1)} %weights_hbm.4), custom_call_target="tpu_custom_call" | custom-call | tf_op jit(solution)/shard_map/pallas_call | solution.py:266
  19.5 0.5 collective-permute-done.2.two_ref
  20.0 0.5 shard_map.141
  20.6 1.3 %collective-permute-done.3 = f32[32,1024]{1,0:T(8,128)S(1)} collective-permute-done((f32[32,1024]{1,0:T(8,128)S(1)}, f32[32,1024]{1,0:T(8,128)S(1)}, u32[]{:S(2)}, u32[]{:S(2)}) %collective-permute-start.3) | collective-permute-done | bytes 131104 | tf_op jit(solution)/shard_map/ppermute | solution.py:334
  21.9 1.9 %collective-permute-start.4 = (f32[32,1024]{1,0:T(8,128)S(1)}, f32[32,1024]{1,0:T(8,128)S(1)}, u32[]{:S(2)}, u32[]{:S(2)}) collective-permute-start(f32[32,1024]{1,0:T(8,128)S(1)} %add.40.after_ref.one_ref), channel_id=1, source_target_pairs={{0,2},{1,3},{2,0},{3,1},{4,6},{5,7},{6,4},{7,5},{8,10},{9,11},{10,... | collective-permute-start | bytes 393224 | tf_op jit(solution)/shard_map/ppermute | solution.py:334
  23.9 1.8 %shard_map.142 = (bf16[1408,1024]{1,0:T(8,128)(2,1)S(1)}, f32[8,128]{1,0:T(8,128)S(1)}) custom-call(f32[32,1024]{1,0:T(8,128)S(1)} %add.40.after_ref.one_ref, bf16[1408,1024]{1,0:T(8,128)(2,1)} %weights_hbm.5), custom_call_target="tpu_custom_call" | custom-call | tf_op jit(solution)/shard_map/pallas_call | solution.py:266
  25.6 2.0 %collective-permute-done.4.two_ref = f32[32,1024]{1,0:T(8,128)S(1)} collective-permute-done((f32[32,1024]{1,0:T(8,128)S(1)}, f32[32,1024]{1,0:T(8,128)S(1)}, u32[]{:S(2)}, u32[]{:S(2)}) %collective-permute-start.4) | collective-permute-done | bytes 131104 | tf_op jit(solution)/shard_map/ppermute | solution.py:334
  27.9 1.2 %collective-permute-done.5.back_ref = f32[32,1024]{1,0:T(8,128)S(1)} collective-permute-done((f32[32,1024]{1,0:T(8,128)S(1)}, f32[32,1024]{1,0:T(8,128)S(1)}, u32[]{:S(2)}, u32[]{:S(2)}) %collective-permute-start.5) | collective-permute-done | bytes 131104 | tf_op jit(solution)/shard_map/ppermute | solution.py:334
  29.1 2.1 %shard_map.145 = (f32[64,1024]{1,0:T(8,128)S(1)}, bf16[64,1408]{1,0:T(8,128)(2,1)S(1)}, f32[32,512]{1,0:T(8,128)S(1)}, f32[32,512]{1,0:T(8,128)S(1)}) custom-call(f32[32,1024]{1,0:T(8,128)S(1)} %get-tuple-element.27.mid_own_ref, bf16[32,1024]{1,0:T(8,128)(2,1)S(1)} %get-tuple-element.28.moe_own_ref, f32[64,128]{1,0:T(8,128)S(1)} %get-tuple-element.29.picks_ref, ...), custom_call_target="tpu_custom_call" | custom-call | tf_op jit(solution)/shard_map/pallas_call | solution.py:447
  31.8 0.4 collective-permute-start.11
  32.5 1.8 %collective-permute-start.7 = (f32[32,512]{1,0:T(8,128)S(1)}, f32[32,512]{1,0:T(8,128)S(1)}, u32[]{:S(2)}, u32[]{:S(2)}) collective-permute-start(f32[32,512]{1,0:T(8,128)S(1)} %add.42), channel_id=1, source_target_pairs={{0,2},{1,3},{2,0},{3,1},{4,6},{5,7},{6,4},{7,5},{8,10},{9,11},{10,... | collective-permute-start | bytes 196616 | tf_op jit(solution)/shard_map/ppermute | solution.py:334
  34.3 1.6 %collective-permute-start.12 = (f32[32,512]{1,0:T(8,128)S(1)}, f32[32,512]{1,0:T(8,128)S(1)}, u32[]{:S(2)}, u32[]{:S(2)}) collective-permute-start(f32[32,512]{1,0:T(8,128)S(1)} %add.47), channel_id=1, source_target_pairs={{0,4},{4,0},{8,12},{12,8},{16,20},{20,16},{24,28},{28,24},{1,5},{5... | collective-permute-start | bytes 196616 | tf_op jit(solution)/shard_map/ppermute | solution.py:334
  35.9 1.0 %collective-permute-done.7 = f32[32,512]{1,0:T(8,128)S(1)} collective-permute-done((f32[32,512]{1,0:T(8,128)S(1)}, f32[32,512]{1,0:T(8,128)S(1)}, u32[]{:S(2)}, u32[]{:S(2)}) %collective-permute-start.7) | collective-permute-done | bytes 65568 | tf_op jit(solution)/shard_map/ppermute | solution.py:334
  36.9 1.8 %collective-permute-start.8 = (f32[32,512]{1,0:T(8,128)S(1)}, f32[32,512]{1,0:T(8,128)S(1)}, u32[]{:S(2)}, u32[]{:S(2)}) collective-permute-start(f32[32,512]{1,0:T(8,128)S(1)} %add.43), channel_id=1, source_target_pairs={{0,4},{4,0},{8,12},{12,8},{16,20},{20,16},{24,28},{28,24},{1,5},{5... | collective-permute-start | bytes 196616 | tf_op jit(solution)/shard_map/ppermute | solution.py:334
  38.9 1.4 %collective-permute-start.13 = (f32[32,512]{1,0:T(8,128)S(1)}, f32[32,512]{1,0:T(8,128)S(1)}, u32[]{:S(2)}, u32[]{:S(2)}) collective-permute-start(f32[32,512]{1,0:T(8,128)S(1)} %add.48), channel_id=1, source_target_pairs={{0,2},{1,3},{2,0},{3,1},{4,6},{5,7},{6,4},{7,5},{8,10},{9,11},{10,... | collective-permute-start | bytes 196616 | tf_op jit(solution)/shard_map/ppermute | solution.py:334
  40.2 1.0 %collective-permute-done.8 = f32[32,512]{1,0:T(8,128)S(1)} collective-permute-done((f32[32,512]{1,0:T(8,128)S(1)}, f32[32,512]{1,0:T(8,128)S(1)}, u32[]{:S(2)}, u32[]{:S(2)}) %collective-permute-start.8) | collective-permute-done | bytes 65568 | tf_op jit(solution)/shard_map/ppermute | solution.py:334
  41.2 1.9 %collective-permute-start.9 = (f32[32,512]{1,0:T(8,128)S(1)}, f32[32,512]{1,0:T(8,128)S(1)}, u32[]{:S(2)}, u32[]{:S(2)}) collective-permute-start(f32[32,512]{1,0:T(8,128)S(1)} %add.44), channel_id=1, source_target_pairs={{0,8},{4,12},{8,0},{12,4},{16,24},{20,28},{24,16},{28,20},{1,9},{5... | collective-permute-start | bytes 196616 | tf_op jit(solution)/shard_map/ppermute | solution.py:334
  43.2 3.2 %collective-permute-start.14 = (f32[32,512]{1,0:T(8,128)S(1)}, f32[32,512]{1,0:T(8,128)S(1)}, u32[]{:S(2)}, u32[]{:S(2)}) collective-permute-start(f32[32,512]{1,0:T(8,128)S(1)} %add.49), channel_id=1, source_target_pairs={{0,16},{4,20},{8,24},{12,28},{16,0},{20,4},{24,8},{28,12},{1,17},{... | collective-permute-start | bytes 196616 | tf_op jit(solution)/shard_map/ppermute | solution.py:334
  46.4 2.2 %collective-permute-start.10 = (f32[32,512]{1,0:T(8,128)S(1)}, f32[32,512]{1,0:T(8,128)S(1)}, u32[]{:S(2)}, u32[]{:S(2)}) collective-permute-start(f32[32,512]{1,0:T(8,128)S(1)} %add.45), channel_id=1, source_target_pairs={{0,16},{4,20},{8,24},{12,28},{16,0},{20,4},{24,8},{28,12},{1,17},{... | collective-permute-start | bytes 196616 | tf_op jit(solution)/shard_map/ppermute | solution.py:334
  48.7 1.4 %collective-permute-done.14 = f32[32,512]{1,0:T(8,128)S(1)} collective-permute-done((f32[32,512]{1,0:T(8,128)S(1)}, f32[32,512]{1,0:T(8,128)S(1)}, u32[]{:S(2)}, u32[]{:S(2)}) %collective-permute-start.14) | collective-permute-done | bytes 65568 | tf_op jit(solution)/shard_map/ppermute | solution.py:334
  50.1 1.1 %collective-permute-start.15 = (f32[32,512]{1,0:T(8,128)S(1)}, f32[32,512]{1,0:T(8,128)S(1)}, u32[]{:S(2)}, u32[]{:S(2)}) collective-permute-start(f32[32,512]{1,0:T(8,128)S(1)} %add.50), channel_id=1, source_target_pairs={{0,8},{4,12},{8,0},{12,4},{16,24},{20,28},{24,16},{28,20},{1,9},{5... | collective-permute-start | bytes 196616 | tf_op jit(solution)/shard_map/ppermute | solution.py:334
  51.2 0.5 collective-permute-done.10
  51.8 2.7 %collective-permute-done.15 = f32[32,512]{1,0:T(8,128)S(1)} collective-permute-done((f32[32,512]{1,0:T(8,128)S(1)}, f32[32,512]{1,0:T(8,128)S(1)}, u32[]{:S(2)}, u32[]{:S(2)}) %collective-permute-start.15) | collective-permute-done | bytes 65568 | tf_op jit(solution)/shard_map/ppermute | solution.py:334
  54.6 1.2 %collective-permute-done.17 = f32[32,512]{1,0:T(8,128)S(1)} collective-permute-done((f32[32,512]{1,0:T(8,128)S(1)}, f32[32,512]{1,0:T(8,128)S(1)}, u32[]{:S(2)}, u32[]{:S(2)}) %collective-permute-start.17) | collective-permute-done | bytes 65568 | tf_op jit(solution)/shard_map/ppermute | solution.py:334
  55.8 0.7 %fusion = bf16[64,1024]{1,0:T(8,128)(2,1)} fusion(f32[64,1024]{1,0:T(8,128)S(1)} %get-tuple-element.33, f32[32,1024]{1,0:T(8,128)S(1)} %get-tuple-element.40, f32[32,1024]{1,0:T(8,128)S(1)} %get-tuple-element.39), kind=kLoop, calls=%fused_computation.1 | loop fusion | flops 196608 | bytes 655360 | tf_op jit(solution)/shard_map/convert_element_type | solution.py:459
  (41 shorter events, 2.4 us)
Async XLA Ops:
  4.2 5.3 %collective-permute-start = (f32[72,256]{1,0:T(8,128)S(1)}, f32[72,256]{1,0:T(8,128)S(1)}, u32[]{:S(2)}, u32[]{:S(2)}) collective-permute-start(f32[72,256]{1,0:T(8,128)S(1)} %shard_map.136.one_ref), channel_id=1, source_target_pairs={{0,4},{4,0},{8,12},{12,8},{16,20},{20,16},{24,28},{28,24},{1,5},{5... | collective-permute-start | bytes 221192 | tf_op jit(solution)/shard_map/ppermute | solution.py:334
  9.8 4.5 %collective-permute-start.1 = (f32[72,256]{1,0:T(8,128)S(1)}, f32[72,256]{1,0:T(8,128)S(1)}, u32[]{:S(2)}, u32[]{:S(2)}) collective-permute-start(f32[72,256]{1,0:T(8,128)S(1)} %shard_map.137.after_ref.one_ref), channel_id=1, source_target_pairs={{0,8},{4,12},{8,0},{12,4},{16,24},{20,28},{24,16},{28,20},{1,9},{5... | collective-permute-start | bytes 221192 | tf_op jit(solution)/shard_map/ppermute | solution.py:334
  14.6 5.4 %copy-start.1 = (bf16[256,1024]{1,0:T(8,128)(2,1)S(1)}, bf16[256,1024]{1,0:T(8,128)(2,1)}, u32[]{:S(2)}) copy-start(bf16[256,1024]{1,0:T(8,128)(2,1)} %w_ref.1) | copy-start | bytes 1572868
  14.6 5.4 %collective-permute-start.2 = (f32[72,256]{1,0:T(8,128)S(1)}, f32[72,256]{1,0:T(8,128)S(1)}, u32[]{:S(2)}, u32[]{:S(2)}) collective-permute-start(f32[72,256]{1,0:T(8,128)S(1)} %shard_map.139.after_ref.one_ref), channel_id=1, source_target_pairs={{0,16},{4,20},{8,24},{12,28},{16,0},{20,4},{24,8},{28,12},{1,17},{... | collective-permute-start | bytes 221192 | tf_op jit(solution)/shard_map/ppermute | solution.py:334
  19.5 8.3 %copy-start = (bf16[4,16,1024]{2,1,0:T(8,128)(2,1)S(1)}, bf16[4,16,1024]{2,1,0:T(8,128)(2,1)}, u32[]{:S(2)}) copy-start(bf16[4,16,1024]{2,1,0:T(8,128)(2,1)} %param.14) | copy-start | bytes 393220
  19.5 8.3 %copy-start.3 = (f32[1024]{0:T(1024)S(1)}, f32[1024]{0:T(1024)}, u32[]{:S(2)}) copy-start(f32[1024]{0:T(1024)} %param.21) | copy-start | bytes 12292
  19.5 8.3 %copy-start.4 = (s32[4,16,2]{1,2,0:T(2,128)S(1)}, s32[4,16,2]{1,2,0:T(2,128)}, u32[]{:S(2)}) copy-start(s32[4,16,2]{1,2,0:T(2,128)} %param.25) | copy-start | bytes 1540
  19.5 9.6 %copy-start.2 = (bf16[1024,16]{0,1:T(8,128)(2,1)S(1)}, bf16[1024,16]{0,1:T(8,128)(2,1)}, u32[]{:S(2)}) copy-start(bf16[1024,16]{0,1:T(8,128)(2,1)} %param.24) | copy-start | bytes 98308
  20.5 1.4 %collective-permute-start.3 = (f32[32,1024]{1,0:T(8,128)S(1)}, f32[32,1024]{1,0:T(8,128)S(1)}, u32[]{:S(2)}, u32[]{:S(2)}) collective-permute-start(f32[32,1024]{1,0:T(8,128)S(1)} %get-tuple-element.25), channel_id=1, source_target_pairs={{0,1},{1,0},{2,3},{3,2},{4,5},{5,4},{6,7},{7,6},{8,9},{9,8},{10,11... | collective-permute-start | bytes 393224 | tf_op jit(solution)/shard_map/ppermute | solution.py:334
  21.9 5.7 %collective-permute-start.4 = (f32[32,1024]{1,0:T(8,128)S(1)}, f32[32,1024]{1,0:T(8,128)S(1)}, u32[]{:S(2)}, u32[]{:S(2)}) collective-permute-start(f32[32,1024]{1,0:T(8,128)S(1)} %add.40.after_ref.one_ref), channel_id=1, source_target_pairs={{0,2},{1,3},{2,0},{3,1},{4,6},{5,7},{6,4},{7,5},{8,10},{9,11},{10,... | collective-permute-start | bytes 393224 | tf_op jit(solution)/shard_map/ppermute | solution.py:334
  27.7 1.4 %collective-permute-start.5 = (f32[32,1024]{1,0:T(8,128)S(1)}, f32[32,1024]{1,0:T(8,128)S(1)}, u32[]{:S(2)}, u32[]{:S(2)}) collective-permute-start(f32[32,1024]{1,0:T(8,128)S(1)} %shard_map.143.half_ref), channel_id=1, source_target_pairs={{0,1},{1,0},{2,3},{3,2},{4,5},{5,4},{6,7},{7,6},{8,9},{9,8},{10,11... | collective-permute-start | bytes 393224 | tf_op jit(solution)/shard_map/ppermute | solution.py:334
  31.2 1.3 %collective-permute-start.6 = (f32[32,512]{1,0:T(8,128)S(1)}, f32[32,512]{1,0:T(8,128)S(1)}, u32[]{:S(2)}, u32[]{:S(2)}) collective-permute-start(f32[32,512]{1,0:T(8,128)S(1)} %get-tuple-element.35), channel_id=1, source_target_pairs={{0,1},{1,0},{2,3},{3,2},{4,5},{5,4},{6,7},{7,6},{8,9},{9,8},{10,11... | collective-permute-start | bytes 196616 | tf_op jit(solution)/shard_map/ppermute | solution.py:334
  31.8 2.5 %collective-permute-start.11 = (f32[32,512]{1,0:T(8,128)S(1)}, f32[32,512]{1,0:T(8,128)S(1)}, u32[]{:S(2)}, u32[]{:S(2)}) collective-permute-start(f32[32,512]{1,0:T(8,128)S(1)} %get-tuple-element.38), channel_id=1, source_target_pairs={{0,1},{1,0},{2,3},{3,2},{4,5},{5,4},{6,7},{7,6},{8,9},{9,8},{10,11... | collective-permute-start | bytes 196616 | tf_op jit(solution)/shard_map/ppermute | solution.py:334
  32.5 4.3 %collective-permute-start.7 = (f32[32,512]{1,0:T(8,128)S(1)}, f32[32,512]{1,0:T(8,128)S(1)}, u32[]{:S(2)}, u32[]{:S(2)}) collective-permute-start(f32[32,512]{1,0:T(8,128)S(1)} %add.42), channel_id=1, source_target_pairs={{0,2},{1,3},{2,0},{3,1},{4,6},{5,7},{6,4},{7,5},{8,10},{9,11},{10,... | collective-permute-start | bytes 196616 | tf_op jit(solution)/shard_map/ppermute | solution.py:334
  34.3 4.5 %collective-permute-start.12 = (f32[32,512]{1,0:T(8,128)S(1)}, f32[32,512]{1,0:T(8,128)S(1)}, u32[]{:S(2)}, u32[]{:S(2)}) collective-permute-start(f32[32,512]{1,0:T(8,128)S(1)} %add.47), channel_id=1, source_target_pairs={{0,4},{4,0},{8,12},{12,8},{16,20},{20,16},{24,28},{28,24},{1,5},{5... | collective-permute-start | bytes 196616 | tf_op jit(solution)/shard_map/ppermute | solution.py:334
  36.9 4.3 %collective-permute-start.8 = (f32[32,512]{1,0:T(8,128)S(1)}, f32[32,512]{1,0:T(8,128)S(1)}, u32[]{:S(2)}, u32[]{:S(2)}) collective-permute-start(f32[32,512]{1,0:T(8,128)S(1)} %add.43), channel_id=1, source_target_pairs={{0,4},{4,0},{8,12},{12,8},{16,20},{20,16},{24,28},{28,24},{1,5},{5... | collective-permute-start | bytes 196616 | tf_op jit(solution)/shard_map/ppermute | solution.py:334
  38.9 4.3 %collective-permute-start.13 = (f32[32,512]{1,0:T(8,128)S(1)}, f32[32,512]{1,0:T(8,128)S(1)}, u32[]{:S(2)}, u32[]{:S(2)}) collective-permute-start(f32[32,512]{1,0:T(8,128)S(1)} %add.48), channel_id=1, source_target_pairs={{0,2},{1,3},{2,0},{3,1},{4,6},{5,7},{6,4},{7,5},{8,10},{9,11},{10,... | collective-permute-start | bytes 196616 | tf_op jit(solution)/shard_map/ppermute | solution.py:334
  41.2 5.2 %collective-permute-start.9 = (f32[32,512]{1,0:T(8,128)S(1)}, f32[32,512]{1,0:T(8,128)S(1)}, u32[]{:S(2)}, u32[]{:S(2)}) collective-permute-start(f32[32,512]{1,0:T(8,128)S(1)} %add.44), channel_id=1, source_target_pairs={{0,8},{4,12},{8,0},{12,4},{16,24},{20,28},{24,16},{28,20},{1,9},{5... | collective-permute-start | bytes 196616 | tf_op jit(solution)/shard_map/ppermute | solution.py:334
  43.2 6.9 %collective-permute-start.14 = (f32[32,512]{1,0:T(8,128)S(1)}, f32[32,512]{1,0:T(8,128)S(1)}, u32[]{:S(2)}, u32[]{:S(2)}) collective-permute-start(f32[32,512]{1,0:T(8,128)S(1)} %add.49), channel_id=1, source_target_pairs={{0,16},{4,20},{8,24},{12,28},{16,0},{20,4},{24,8},{28,12},{1,17},{... | collective-permute-start | bytes 196616 | tf_op jit(solution)/shard_map/ppermute | solution.py:334
  46.4 5.2 %collective-permute-start.10 = (f32[32,512]{1,0:T(8,128)S(1)}, f32[32,512]{1,0:T(8,128)S(1)}, u32[]{:S(2)}, u32[]{:S(2)}) collective-permute-start(f32[32,512]{1,0:T(8,128)S(1)} %add.45), channel_id=1, source_target_pairs={{0,16},{4,20},{8,24},{12,28},{16,0},{20,4},{24,8},{28,12},{1,17},{... | collective-permute-start | bytes 196616 | tf_op jit(solution)/shard_map/ppermute | solution.py:334
  50.1 4.3 %collective-permute-start.15 = (f32[32,512]{1,0:T(8,128)S(1)}, f32[32,512]{1,0:T(8,128)S(1)}, u32[]{:S(2)}, u32[]{:S(2)}) collective-permute-start(f32[32,512]{1,0:T(8,128)S(1)} %add.50), channel_id=1, source_target_pairs={{0,8},{4,12},{8,0},{12,4},{16,24},{20,28},{24,16},{28,20},{1,9},{5... | collective-permute-start | bytes 196616 | tf_op jit(solution)/shard_map/ppermute | solution.py:334
  51.7 2.9 %collective-permute-start.16 = (f32[32,512]{1,0:T(8,128)S(1)}, f32[32,512]{1,0:T(8,128)S(1)}, u32[]{:S(2)}, u32[]{:S(2)}) collective-permute-start(f32[32,512]{1,0:T(8,128)S(1)} %add.46), channel_id=1, source_target_pairs={{0,1},{1,0},{2,3},{3,2},{4,5},{5,4},{6,7},{7,6},{8,9},{9,8},{10,11... | collective-permute-start | bytes 196616 | tf_op jit(solution)/shard_map/ppermute | solution.py:334
  54.5 1.3 %collective-permute-start.17 = (f32[32,512]{1,0:T(8,128)S(1)}, f32[32,512]{1,0:T(8,128)S(1)}, u32[]{:S(2)}, u32[]{:S(2)}) collective-permute-start(f32[32,512]{1,0:T(8,128)S(1)} %add.51), channel_id=1, source_target_pairs={{0,1},{1,0},{2,3},{3,2},{4,5},{5,4},{6,7},{7,6},{8,9},{9,8},{10,11... | collective-permute-start | bytes 196616 | tf_op jit(solution)/shard_map/ppermute | solution.py:334

commit v11 on v10

--- a/solution.py
+++ b/solution.py
@@ -159,7 +159,7 @@
     fresh_weights = jnp.where(fresh_live, jnp.exp(fresh_scores - top), 0.0)
     total = jnp.sum(weights, axis=1, keepdims=True) + jnp.sum(fresh_weights, axis=1, keepdims=True)
     weight_buf[...] = weights.astype(BF16)
-    score_buf[...] = dot(fresh_weights.astype(BF16), fresh_values)
+    fresh_rows = fresh_weights.astype(BF16)
     for copy in v_copies:
         copy.wait()
 
@@ -174,7 +174,7 @@
     blocks_of_lanes = features // LANES
     for r in range(requests):
         at, rows_of = slice(r * group, (r + 1) * group), pl.ds(r, steps, requests)
-        own = jnp.where(group_own, dot(weight_buf[at, :], v_buf[r]) + score_buf[at, :], 0.0)
+        own = jnp.where(group_own, dot(weight_buf[at, :], v_buf[r]) + dot(fresh_rows[at], fresh_values), 0.0)
         own = folded(own)[:steps]
         for c in range(blocks_of_lanes):
             lane_buf[c, rows_of, :] = own[:, c * LANES : (c + 1) * LANES]

time: 56.7 us -> 56.4 us (level)
  no operation moved by 1% of the time
where the time goes in v11:
time: 56.4 us; the launch traced here: 56.1 us
  starting transfers between devices  25.9 us (46%)
  waiting for transfers between devices  16.3 us (29%)
  Pallas kernels  12.7 us (23%)
  other arithmetic  0.84 us (1%)
    ppermute x18, starting transfers between devices, swap(): lax.ppermute(value, axis, [(i, i ^ flip) for i in range(lax.axis_size(axi...  25.9 us
    ppermute x18, waiting for transfers between devices, swap(): lax.ppermute(value, axis, [(i, i ^ flip) for i in range(lax.axis_size(axi...  16.3 us
    pallas_call x3, Pallas kernels, fetch(): call(functools.partial(fetch_kernel, index), [(shape, BF16), ((8, LANES),...  5.36 us
    pallas_call x1, Pallas kernels, on_device(): call(functools.partial(attend_kernel, steps, requests, heads), [(packed_s...  3.84 us
    pallas_call x1, Pallas kernels, on_device(): call(expert_kernel, expert_shapes, [VMEM] * 10, 8)  2.07 us
  transfers between devices with their start and end apart: 18, of which 15 were waited for; matrix products, arithmetic and copies ran while one was open for 0% of the time, Pallas kernels for 10%

profile of v11, /device:TPU:0, one launch (start us, length us, event | category | flops | bytes accessed | tf_op | source)
XLA Modules:
  0.0 56.1 jit_solution(9573058563310412444)
XLA Ops:
  0.0 3.8 %shard_map.136.one_ref = f32[72,256]{1,0:T(8,128)S(1)} custom-call(s32[16]{0:T(128)} %len_hbm.1, bf16[64,1024]{1,0:T(8,128)(2,1)} %bitcast.6, f32[1024]{0:T(1024)} %gain_hbm.1, s32[2052]{0:T(1024)} %table_hbm.1, f32[4,32]{1,0:T(4,128)} %bitcast.13, bf16[3,1024,256]{2,1,0:T(8,128)(2,1)} %w_hbm.1, bf16[16,256,256]{2,1,0:T(8,128)(2,1)} %k_hbm.1, ...), custom_call_target="tpu_custom_call" | custom-call | tf_op jit(solution)/shard_map/pallas_call | solution.py:387
  3.8 3.0 %collective-permute-start = (f32[72,256]{1,0:T(8,128)S(1)}, f32[72,256]{1,0:T(8,128)S(1)}, u32[]{:S(2)}, u32[]{:S(2)}) collective-permute-start(f32[72,256]{1,0:T(8,128)S(1)} %shard_map.136.one_ref), channel_id=1, source_target_pairs={{0,4},{4,0},{8,12},{12,8},{16,20},{20,16},{24,28},{28,24},{1,5},{5... | collective-permute-start | bytes 221192 | tf_op jit(solution)/shard_map/ppermute | solution.py:334
  6.8 2.3 %collective-permute-done.two_ref = f32[72,256]{1,0:T(8,128)S(1)} collective-permute-done((f32[72,256]{1,0:T(8,128)S(1)}, f32[72,256]{1,0:T(8,128)S(1)}, u32[]{:S(2)}, u32[]{:S(2)}) %collective-permute-start) | collective-permute-done | bytes 73760 | tf_op jit(solution)/shard_map/ppermute | solution.py:334
  9.4 2.2 %collective-permute-start.1 = (f32[72,256]{1,0:T(8,128)S(1)}, f32[72,256]{1,0:T(8,128)S(1)}, u32[]{:S(2)}, u32[]{:S(2)}) collective-permute-start(f32[72,256]{1,0:T(8,128)S(1)} %shard_map.137.after_ref.one_ref), channel_id=1, source_target_pairs={{0,8},{4,12},{8,0},{12,4},{16,24},{20,28},{24,16},{28,20},{1,9},{5... | collective-permute-start | bytes 221192 | tf_op jit(solution)/shard_map/ppermute | solution.py:334
  11.6 1.8 %shard_map.138 = (bf16[1408,1024]{1,0:T(8,128)(2,1)S(1)}, f32[8,128]{1,0:T(8,128)S(1)}) custom-call(f32[72,256]{1,0:T(8,128)S(1)} %shard_map.137.after_ref.one_ref, bf16[2,1408,1024]{2,1,0:T(8,128)(2,1)} %weights_hbm.4), custom_call_target="tpu_custom_call" | custom-call | tf_op jit(solution)/shard_map/pallas_call | solution.py:266
  13.4 0.5 collective-permute-done.1.two_ref
  14.2 3.1 %collective-permute-start.2 = (f32[72,256]{1,0:T(8,128)S(1)}, f32[72,256]{1,0:T(8,128)S(1)}, u32[]{:S(2)}, u32[]{:S(2)}) collective-permute-start(f32[72,256]{1,0:T(8,128)S(1)} %shard_map.139.after_ref.one_ref), channel_id=1, source_target_pairs={{0,16},{4,20},{8,24},{12,28},{16,0},{20,4},{24,8},{28,12},{1,17},{... | collective-permute-start | bytes 221192 | tf_op jit(solution)/shard_map/ppermute | solution.py:334
  17.3 1.8 %shard_map.140 = (bf16[1408,1024]{1,0:T(8,128)(2,1)S(1)}, f32[8,128]{1,0:T(8,128)S(1)}) custom-call(f32[72,256]{1,0:T(8,128)S(1)} %shard_map.139.after_ref.one_ref, bf16[2,1408,1024]{2,1,0:T(8,128)(2,1)} %weights_hbm.4), custom_call_target="tpu_custom_call" | custom-call | tf_op jit(solution)/shard_map/pallas_call | solution.py:266
  19.2 0.5 collective-permute-done.2.two_ref
  19.6 0.5 shard_map.141
  20.2 1.3 %collective-permute-done.3 = f32[32,1024]{1,0:T(8,128)S(1)} collective-permute-done((f32[32,1024]{1,0:T(8,128)S(1)}, f32[32,1024]{1,0:T(8,128)S(1)}, u32[]{:S(2)}, u32[]{:S(2)}) %collective-permute-start.3) | collective-permute-done | bytes 131104 | tf_op jit(solution)/shard_map/ppermute | solution.py:334
  21.5 1.9 %collective-permute-start.4 = (f32[32,1024]{1,0:T(8,128)S(1)}, f32[32,1024]{1,0:T(8,128)S(1)}, u32[]{:S(2)}, u32[]{:S(2)}) collective-permute-start(f32[32,1024]{1,0:T(8,128)S(1)} %add.40.after_ref.one_ref), channel_id=1, source_target_pairs={{0,2},{1,3},{2,0},{3,1},{4,6},{5,7},{6,4},{7,5},{8,10},{9,11},{10,... | collective-permute-start | bytes 393224 | tf_op jit(solution)/shard_map/ppermute | solution.py:334
  23.5 1.8 %shard_map.142 = (bf16[1408,1024]{1,0:T(8,128)(2,1)S(1)}, f32[8,128]{1,0:T(8,128)S(1)}) custom-call(f32[32,1024]{1,0:T(8,128)S(1)} %add.40.after_ref.one_ref, bf16[1408,1024]{1,0:T(8,128)(2,1)} %weights_hbm.5), custom_call_target="tpu_custom_call" | custom-call | tf_op jit(solution)/shard_map/pallas_call | solution.py:266
  25.3 2.0 %collective-permute-done.4.two_ref = f32[32,1024]{1,0:T(8,128)S(1)} collective-permute-done((f32[32,1024]{1,0:T(8,128)S(1)}, f32[32,1024]{1,0:T(8,128)S(1)}, u32[]{:S(2)}, u32[]{:S(2)}) %collective-permute-start.4) | collective-permute-done | bytes 131104 | tf_op jit(solution)/shard_map/ppermute | solution.py:334
  27.5 1.2 %collective-permute-done.5.back_ref = f32[32,1024]{1,0:T(8,128)S(1)} collective-permute-done((f32[32,1024]{1,0:T(8,128)S(1)}, f32[32,1024]{1,0:T(8,128)S(1)}, u32[]{:S(2)}, u32[]{:S(2)}) %collective-permute-start.5) | collective-permute-done | bytes 131104 | tf_op jit(solution)/shard_map/ppermute | solution.py:334
  28.7 2.1 %shard_map.145 = (f32[64,1024]{1,0:T(8,128)S(1)}, bf16[64,1408]{1,0:T(8,128)(2,1)S(1)}, f32[32,512]{1,0:T(8,128)S(1)}, f32[32,512]{1,0:T(8,128)S(1)}) custom-call(f32[32,1024]{1,0:T(8,128)S(1)} %get-tuple-element.27.mid_own_ref, bf16[32,1024]{1,0:T(8,128)(2,1)S(1)} %get-tuple-element.28.moe_own_ref, f32[64,128]{1,0:T(8,128)S(1)} %get-tuple-element.29.picks_ref, ...), custom_call_target="tpu_custom_call" | custom-call | tf_op jit(solution)/shard_map/pallas_call | solution.py:447
  31.4 0.4 collective-permute-start.11
  32.1 1.8 %collective-permute-start.7 = (f32[32,512]{1,0:T(8,128)S(1)}, f32[32,512]{1,0:T(8,128)S(1)}, u32[]{:S(2)}, u32[]{:S(2)}) collective-permute-start(f32[32,512]{1,0:T(8,128)S(1)} %add.42), channel_id=1, source_target_pairs={{0,2},{1,3},{2,0},{3,1},{4,6},{5,7},{6,4},{7,5},{8,10},{9,11},{10,... | collective-permute-start | bytes 196616 | tf_op jit(solution)/shard_map/ppermute | solution.py:334
  33.9 1.6 %collective-permute-start.12 = (f32[32,512]{1,0:T(8,128)S(1)}, f32[32,512]{1,0:T(8,128)S(1)}, u32[]{:S(2)}, u32[]{:S(2)}) collective-permute-start(f32[32,512]{1,0:T(8,128)S(1)} %add.47), channel_id=1, source_target_pairs={{0,4},{4,0},{8,12},{12,8},{16,20},{20,16},{24,28},{28,24},{1,5},{5... | collective-permute-start | bytes 196616 | tf_op jit(solution)/shard_map/ppermute | solution.py:334
  35.5 1.0 %collective-permute-done.7 = f32[32,512]{1,0:T(8,128)S(1)} collective-permute-done((f32[32,512]{1,0:T(8,128)S(1)}, f32[32,512]{1,0:T(8,128)S(1)}, u32[]{:S(2)}, u32[]{:S(2)}) %collective-permute-start.7) | collective-permute-done | bytes 65568 | tf_op jit(solution)/shard_map/ppermute | solution.py:334
  36.5 1.8 %collective-permute-start.8 = (f32[32,512]{1,0:T(8,128)S(1)}, f32[32,512]{1,0:T(8,128)S(1)}, u32[]{:S(2)}, u32[]{:S(2)}) collective-permute-start(f32[32,512]{1,0:T(8,128)S(1)} %add.43), channel_id=1, source_target_pairs={{0,4},{4,0},{8,12},{12,8},{16,20},{20,16},{24,28},{28,24},{1,5},{5... | collective-permute-start | bytes 196616 | tf_op jit(solution)/shard_map/ppermute | solution.py:334
  38.5 1.4 %collective-permute-start.13 = (f32[32,512]{1,0:T(8,128)S(1)}, f32[32,512]{1,0:T(8,128)S(1)}, u32[]{:S(2)}, u32[]{:S(2)}) collective-permute-start(f32[32,512]{1,0:T(8,128)S(1)} %add.48), channel_id=1, source_target_pairs={{0,2},{1,3},{2,0},{3,1},{4,6},{5,7},{6,4},{7,5},{8,10},{9,11},{10,... | collective-permute-start | bytes 196616 | tf_op jit(solution)/shard_map/ppermute | solution.py:334
  39.8 1.0 %collective-permute-done.8 = f32[32,512]{1,0:T(8,128)S(1)} collective-permute-done((f32[32,512]{1,0:T(8,128)S(1)}, f32[32,512]{1,0:T(8,128)S(1)}, u32[]{:S(2)}, u32[]{:S(2)}) %collective-permute-start.8) | collective-permute-done | bytes 65568 | tf_op jit(solution)/shard_map/ppermute | solution.py:334
  40.8 1.9 %collective-permute-start.9 = (f32[32,512]{1,0:T(8,128)S(1)}, f32[32,512]{1,0:T(8,128)S(1)}, u32[]{:S(2)}, u32[]{:S(2)}) collective-permute-start(f32[32,512]{1,0:T(8,128)S(1)} %add.44), channel_id=1, source_target_pairs={{0,8},{4,12},{8,0},{12,4},{16,24},{20,28},{24,16},{28,20},{1,9},{5... | collective-permute-start | bytes 196616 | tf_op jit(solution)/shard_map/ppermute | solution.py:334
  42.8 3.2 %collective-permute-start.14 = (f32[32,512]{1,0:T(8,128)S(1)}, f32[32,512]{1,0:T(8,128)S(1)}, u32[]{:S(2)}, u32[]{:S(2)}) collective-permute-start(f32[32,512]{1,0:T(8,128)S(1)} %add.49), channel_id=1, source_target_pairs={{0,16},{4,20},{8,24},{12,28},{16,0},{20,4},{24,8},{28,12},{1,17},{... | collective-permute-start | bytes 196616 | tf_op jit(solution)/shard_map/ppermute | solution.py:334
  46.0 2.2 %collective-permute-start.10 = (f32[32,512]{1,0:T(8,128)S(1)}, f32[32,512]{1,0:T(8,128)S(1)}, u32[]{:S(2)}, u32[]{:S(2)}) collective-permute-start(f32[32,512]{1,0:T(8,128)S(1)} %add.45), channel_id=1, source_target_pairs={{0,16},{4,20},{8,24},{12,28},{16,0},{20,4},{24,8},{28,12},{1,17},{... | collective-permute-start | bytes 196616 | tf_op jit(solution)/shard_map/ppermute | solution.py:334
  48.3 1.4 %collective-permute-done.14 = f32[32,512]{1,0:T(8,128)S(1)} collective-permute-done((f32[32,512]{1,0:T(8,128)S(1)}, f32[32,512]{1,0:T(8,128)S(1)}, u32[]{:S(2)}, u32[]{:S(2)}) %collective-permute-start.14) | collective-permute-done | bytes 65568 | tf_op jit(solution)/shard_map/ppermute | solution.py:334
  49.7 1.1 %collective-permute-start.15 = (f32[32,512]{1,0:T(8,128)S(1)}, f32[32,512]{1,0:T(8,128)S(1)}, u32[]{:S(2)}, u32[]{:S(2)}) collective-permute-start(f32[32,512]{1,0:T(8,128)S(1)} %add.50), channel_id=1, source_target_pairs={{0,8},{4,12},{8,0},{12,4},{16,24},{20,28},{24,16},{28,20},{1,9},{5... | collective-permute-start | bytes 196616 | tf_op jit(solution)/shard_map/ppermute | solution.py:334
  50.8 0.5 collective-permute-done.10
  51.4 2.7 %collective-permute-done.15 = f32[32,512]{1,0:T(8,128)S(1)} collective-permute-done((f32[32,512]{1,0:T(8,128)S(1)}, f32[32,512]{1,0:T(8,128)S(1)}, u32[]{:S(2)}, u32[]{:S(2)}) %collective-permute-start.15) | collective-permute-done | bytes 65568 | tf_op jit(solution)/shard_map/ppermute | solution.py:334
  54.2 1.2 %collective-permute-done.17 = f32[32,512]{1,0:T(8,128)S(1)} collective-permute-done((f32[32,512]{1,0:T(8,128)S(1)}, f32[32,512]{1,0:T(8,128)S(1)}, u32[]{:S(2)}, u32[]{:S(2)}) %collective-permute-start.17) | collective-permute-done | bytes 65568 | tf_op jit(solution)/shard_map/ppermute | solution.py:334
  55.4 0.7 %fusion = bf16[64,1024]{1,0:T(8,128)(2,1)} fusion(f32[64,1024]{1,0:T(8,128)S(1)} %get-tuple-element.33, f32[32,1024]{1,0:T(8,128)S(1)} %get-tuple-element.40, f32[32,1024]{1,0:T(8,128)S(1)} %get-tuple-element.39), kind=kLoop, calls=%fused_computation.1 | loop fusion | flops 196608 | bytes 655360 | tf_op jit(solution)/shard_map/convert_element_type | solution.py:459
  (41 shorter events, 2.4 us)
Async XLA Ops:
  3.8 5.3 %collective-permute-start = (f32[72,256]{1,0:T(8,128)S(1)}, f32[72,256]{1,0:T(8,128)S(1)}, u32[]{:S(2)}, u32[]{:S(2)}) collective-permute-start(f32[72,256]{1,0:T(8,128)S(1)} %shard_map.136.one_ref), channel_id=1, source_target_pairs={{0,4},{4,0},{8,12},{12,8},{16,20},{20,16},{24,28},{28,24},{1,5},{5... | collective-permute-start | bytes 221192 | tf_op jit(solution)/shard_map/ppermute | solution.py:334
  9.4 4.5 %collective-permute-start.1 = (f32[72,256]{1,0:T(8,128)S(1)}, f32[72,256]{1,0:T(8,128)S(1)}, u32[]{:S(2)}, u32[]{:S(2)}) collective-permute-start(f32[72,256]{1,0:T(8,128)S(1)} %shard_map.137.after_ref.one_ref), channel_id=1, source_target_pairs={{0,8},{4,12},{8,0},{12,4},{16,24},{20,28},{24,16},{28,20},{1,9},{5... | collective-permute-start | bytes 221192 | tf_op jit(solution)/shard_map/ppermute | solution.py:334
  14.2 5.4 %copy-start.1 = (bf16[256,1024]{1,0:T(8,128)(2,1)S(1)}, bf16[256,1024]{1,0:T(8,128)(2,1)}, u32[]{:S(2)}) copy-start(bf16[256,1024]{1,0:T(8,128)(2,1)} %w_ref.1) | copy-start | bytes 1572868
  14.2 5.4 %collective-permute-start.2 = (f32[72,256]{1,0:T(8,128)S(1)}, f32[72,256]{1,0:T(8,128)S(1)}, u32[]{:S(2)}, u32[]{:S(2)}) collective-permute-start(f32[72,256]{1,0:T(8,128)S(1)} %shard_map.139.after_ref.one_ref), channel_id=1, source_target_pairs={{0,16},{4,20},{8,24},{12,28},{16,0},{20,4},{24,8},{28,12},{1,17},{... | collective-permute-start | bytes 221192 | tf_op jit(solution)/shard_map/ppermute | solution.py:334
  19.1 8.3 %copy-start = (bf16[4,16,1024]{2,1,0:T(8,128)(2,1)S(1)}, bf16[4,16,1024]{2,1,0:T(8,128)(2,1)}, u32[]{:S(2)}) copy-start(bf16[4,16,1024]{2,1,0:T(8,128)(2,1)} %param.14) | copy-start | bytes 393220
  19.1 8.3 %copy-start.3 = (f32[1024]{0:T(1024)S(1)}, f32[1024]{0:T(1024)}, u32[]{:S(2)}) copy-start(f32[1024]{0:T(1024)} %param.21) | copy-start | bytes 12292
  19.1 8.3 %copy-start.4 = (s32[4,16,2]{1,2,0:T(2,128)S(1)}, s32[4,16,2]{1,2,0:T(2,128)}, u32[]{:S(2)}) copy-start(s32[4,16,2]{1,2,0:T(2,128)} %param.25) | copy-start | bytes 1540
  19.1 9.6 %copy-start.2 = (bf16[1024,16]{0,1:T(8,128)(2,1)S(1)}, bf16[1024,16]{0,1:T(8,128)(2,1)}, u32[]{:S(2)}) copy-start(bf16[1024,16]{0,1:T(8,128)(2,1)} %param.24) | copy-start | bytes 98308
  20.1 1.4 %collective-permute-start.3 = (f32[32,1024]{1,0:T(8,128)S(1)}, f32[32,1024]{1,0:T(8,128)S(1)}, u32[]{:S(2)}, u32[]{:S(2)}) collective-permute-start(f32[32,1024]{1,0:T(8,128)S(1)} %get-tuple-element.25), channel_id=1, source_target_pairs={{0,1},{1,0},{2,3},{3,2},{4,5},{5,4},{6,7},{7,6},{8,9},{9,8},{10,11... | collective-permute-start | bytes 393224 | tf_op jit(solution)/shard_map/ppermute | solution.py:334
  21.5 5.7 %collective-permute-start.4 = (f32[32,1024]{1,0:T(8,128)S(1)}, f32[32,1024]{1,0:T(8,128)S(1)}, u32[]{:S(2)}, u32[]{:S(2)}) collective-permute-start(f32[32,1024]{1,0:T(8,128)S(1)} %add.40.after_ref.one_ref), channel_id=1, source_target_pairs={{0,2},{1,3},{2,0},{3,1},{4,6},{5,7},{6,4},{7,5},{8,10},{9,11},{10,... | collective-permute-start | bytes 393224 | tf_op jit(solution)/shard_map/ppermute | solution.py:334
  27.3 1.4 %collective-permute-start.5 = (f32[32,1024]{1,0:T(8,128)S(1)}, f32[32,1024]{1,0:T(8,128)S(1)}, u32[]{:S(2)}, u32[]{:S(2)}) collective-permute-start(f32[32,1024]{1,0:T(8,128)S(1)} %shard_map.143.half_ref), channel_id=1, source_target_pairs={{0,1},{1,0},{2,3},{3,2},{4,5},{5,4},{6,7},{7,6},{8,9},{9,8},{10,11... | collective-permute-start | bytes 393224 | tf_op jit(solution)/shard_map/ppermute | solution.py:334
  30.8 1.3 %collective-permute-start.6 = (f32[32,512]{1,0:T(8,128)S(1)}, f32[32,512]{1,0:T(8,128)S(1)}, u32[]{:S(2)}, u32[]{:S(2)}) collective-permute-start(f32[32,512]{1,0:T(8,128)S(1)} %get-tuple-element.35), channel_id=1, source_target_pairs={{0,1},{1,0},{2,3},{3,2},{4,5},{5,4},{6,7},{7,6},{8,9},{9,8},{10,11... | collective-permute-start | bytes 196616 | tf_op jit(solution)/shard_map/ppermute | solution.py:334
  31.4 2.5 %collective-permute-start.11 = (f32[32,512]{1,0:T(8,128)S(1)}, f32[32,512]{1,0:T(8,128)S(1)}, u32[]{:S(2)}, u32[]{:S(2)}) collective-permute-start(f32[32,512]{1,0:T(8,128)S(1)} %get-tuple-element.38), channel_id=1, source_target_pairs={{0,1},{1,0},{2,3},{3,2},{4,5},{5,4},{6,7},{7,6},{8,9},{9,8},{10,11... | collective-permute-start | bytes 196616 | tf_op jit(solution)/shard_map/ppermute | solution.py:334
  32.1 4.3 %collective-permute-start.7 = (f32[32,512]{1,0:T(8,128)S(1)}, f32[32,512]{1,0:T(8,128)S(1)}, u32[]{:S(2)}, u32[]{:S(2)}) collective-permute-start(f32[32,512]{1,0:T(8,128)S(1)} %add.42), channel_id=1, source_target_pairs={{0,2},{1,3},{2,0},{3,1},{4,6},{5,7},{6,4},{7,5},{8,10},{9,11},{10,... | collective-permute-start | bytes 196616 | tf_op jit(solution)/shard_map/ppermute | solution.py:334
  33.9 4.5 %collective-permute-start.12 = (f32[32,512]{1,0:T(8,128)S(1)}, f32[32,512]{1,0:T(8,128)S(1)}, u32[]{:S(2)}, u32[]{:S(2)}) collective-permute-start(f32[32,512]{1,0:T(8,128)S(1)} %add.47), channel_id=1, source_target_pairs={{0,4},{4,0},{8,12},{12,8},{16,20},{20,16},{24,28},{28,24},{1,5},{5... | collective-permute-start | bytes 196616 | tf_op jit(solution)/shard_map/ppermute | solution.py:334
  36.5 4.3 %collective-permute-start.8 = (f32[32,512]{1,0:T(8,128)S(1)}, f32[32,512]{1,0:T(8,128)S(1)}, u32[]{:S(2)}, u32[]{:S(2)}) collective-permute-start(f32[32,512]{1,0:T(8,128)S(1)} %add.43), channel_id=1, source_target_pairs={{0,4},{4,0},{8,12},{12,8},{16,20},{20,16},{24,28},{28,24},{1,5},{5... | collective-permute-start | bytes 196616 | tf_op jit(solution)/shard_map/ppermute | solution.py:334
  38.5 4.3 %collective-permute-start.13 = (f32[32,512]{1,0:T(8,128)S(1)}, f32[32,512]{1,0:T(8,128)S(1)}, u32[]{:S(2)}, u32[]{:S(2)}) collective-permute-start(f32[32,512]{1,0:T(8,128)S(1)} %add.48), channel_id=1, source_target_pairs={{0,2},{1,3},{2,0},{3,1},{4,6},{5,7},{6,4},{7,5},{8,10},{9,11},{10,... | collective-permute-start | bytes 196616 | tf_op jit(solution)/shard_map/ppermute | solution.py:334
  40.8 5.2 %collective-permute-start.9 = (f32[32,512]{1,0:T(8,128)S(1)}, f32[32,512]{1,0:T(8,128)S(1)}, u32[]{:S(2)}, u32[]{:S(2)}) collective-permute-start(f32[32,512]{1,0:T(8,128)S(1)} %add.44), channel_id=1, source_target_pairs={{0,8},{4,12},{8,0},{12,4},{16,24},{20,28},{24,16},{28,20},{1,9},{5... | collective-permute-start | bytes 196616 | tf_op jit(solution)/shard_map/ppermute | solution.py:334
  42.8 6.9 %collective-permute-start.14 = (f32[32,512]{1,0:T(8,128)S(1)}, f32[32,512]{1,0:T(8,128)S(1)}, u32[]{:S(2)}, u32[]{:S(2)}) collective-permute-start(f32[32,512]{1,0:T(8,128)S(1)} %add.49), channel_id=1, source_target_pairs={{0,16},{4,20},{8,24},{12,28},{16,0},{20,4},{24,8},{28,12},{1,17},{... | collective-permute-start | bytes 196616 | tf_op jit(solution)/shard_map/ppermute | solution.py:334
  46.0 5.2 %collective-permute-start.10 = (f32[32,512]{1,0:T(8,128)S(1)}, f32[32,512]{1,0:T(8,128)S(1)}, u32[]{:S(2)}, u32[]{:S(2)}) collective-permute-start(f32[32,512]{1,0:T(8,128)S(1)} %add.45), channel_id=1, source_target_pairs={{0,16},{4,20},{8,24},{12,28},{16,0},{20,4},{24,8},{28,12},{1,17},{... | collective-permute-start | bytes 196616 | tf_op jit(solution)/shard_map/ppermute | solution.py:334
  49.7 4.3 %collective-permute-start.15 = (f32[32,512]{1,0:T(8,128)S(1)}, f32[32,512]{1,0:T(8,128)S(1)}, u32[]{:S(2)}, u32[]{:S(2)}) collective-permute-start(f32[32,512]{1,0:T(8,128)S(1)} %add.50), channel_id=1, source_target_pairs={{0,8},{4,12},{8,0},{12,4},{16,24},{20,28},{24,16},{28,20},{1,9},{5... | collective-permute-start | bytes 196616 | tf_op jit(solution)/shard_map/ppermute | solution.py:334
  51.3 2.9 %collective-permute-start.16 = (f32[32,512]{1,0:T(8,128)S(1)}, f32[32,512]{1,0:T(8,128)S(1)}, u32[]{:S(2)}, u32[]{:S(2)}) collective-permute-start(f32[32,512]{1,0:T(8,128)S(1)} %add.46), channel_id=1, source_target_pairs={{0,1},{1,0},{2,3},{3,2},{4,5},{5,4},{6,7},{7,6},{8,9},{9,8},{10,11... | collective-permute-start | bytes 196616 | tf_op jit(solution)/shard_map/ppermute | solution.py:334
  54.1 1.3 %collective-permute-start.17 = (f32[32,512]{1,0:T(8,128)S(1)}, f32[32,512]{1,0:T(8,128)S(1)}, u32[]{:S(2)}, u32[]{:S(2)}) collective-permute-start(f32[32,512]{1,0:T(8,128)S(1)} %add.51), channel_id=1, source_target_pairs={{0,1},{1,0},{2,3},{3,2},{4,5},{5,4},{6,7},{7,6},{8,9},{9,8},{10,11... | collective-permute-start | bytes 196616 | tf_op jit(solution)/shard_map/ppermute | solution.py:334
